TPU v7x, 768 devices: a whole 4x8x12 slice. The times are simulated.
768 devices in a mesh: node: 96 (over z, x, core), local: 8 (over y).
Axes of the slice: x: 4, y: 8, z: 12, core: 2. Of those that a mesh axis runs over, the one named last changes fastest.
Arguments:
- layer_input: bfloat16 [12288, 3584], P('node', 'local'), may hold values from -6 to 6
- output_grad: bfloat16 [12288, 3584], P('node', 'local'), may hold values from -6 to 6
- gate_weight: bfloat16 [96, 3584, 1024], P('node', None, 'local'), may hold values from -0.09375 to 0.09375
- up_weight: bfloat16 [96, 3584, 1024], P('node', None, 'local'), may hold values from -0.09375 to 0.09375
- down_weight: bfloat16 [96, 1024, 3584], P('node', 'local'), may hold values from -0.1875 to 0.1875
- route_offset: int32 [12288, 2], P('node'), may hold values from 0 to 3, all different within a row; in each aligned block of 128 rows (0 to 127, 128 to 255, ...) at most 80 rows name the same one
- gate_fixed: int32 [12288, 2], P('node'), may hold values from 4096 to 65535
Outputs:
- input_grad: bfloat16 [12288, 3584], P('node', 'local')
- gate_grad: float32 [12288, 2], P('node')
Inputs may be any that keep to these rules, and one draw needn't show every extreme that they name: `route_offset`: each token names 2 different offsets. Among the 128 tokens of one node no offset is named more than 80 times, and in some node one offset is named exactly 80 times.
All inputs are finite; a program needn't handle non-finite values.
Results may differ from a plain program's by a relative error of at most 0.0049.
Values may be sent and summed in bfloat16 or wider, within the bound.
No kernel may reach another device: no remote copies, remote signals or barrier semaphores. Data moves between devices by JAX's collectives and lax.ppermute only.
A program may use at most 64 MiB of HBM per device.

v0:
```python
import jax
import jax.numpy as jnp
from jax import lax
from jax.sharding import PartitionSpec as P

GROUP = 4
CAPACITY = 80


def from_behind(value, axis, steps):
    count = lax.axis_size(axis)
    pairs = [(source, (source + steps) % count) for source in range(count)]
    return lax.ppermute(value, axis, pairs)


def packer(chosen, capacity):
    ranks = jnp.cumsum(chosen.astype(jnp.int32)) - 1
    slots = jnp.arange(capacity, dtype=jnp.int32)
    return ((ranks[None, :] == slots[:, None]) & chosen[None, :]).astype(jnp.bfloat16)


def hidden_grads(rows_in, rows_grad, gate_cols, up_cols, down_rows):
    gate_pre = jnp.dot(rows_in, gate_cols, preferred_element_type=jnp.float32)
    up_pre = jnp.dot(rows_in, up_cols, preferred_element_type=jnp.float32)
    hidden_grad = lax.dot_general(
        rows_grad, down_rows, (((1,), (1,)), ((), ())), preferred_element_type=jnp.float32
    )
    sigmoid = jax.nn.sigmoid(gate_pre)
    swish = gate_pre * sigmoid
    gate_part = jnp.sum(swish * up_pre * hidden_grad, axis=1)
    up_grad = (hidden_grad * swish).astype(jnp.bfloat16)
    pre_grad = (hidden_grad * up_pre * sigmoid * (1.0 + gate_pre * (1.0 - sigmoid))).astype(
        jnp.bfloat16
    )
    return (gate_part, up_grad, pre_grad)


def carry_out(first, second):
    got_first = [first[0]]
    got_second = [second[0]]
    for offset in range(1, GROUP):
        moved_first, moved_second = from_behind((first[offset], second[offset]), "node", offset)
        got_first.append(moved_first)
        got_second.append(moved_second)
    return (jnp.stack(got_first), jnp.stack(got_second))


def carry_home(first, second):
    got_first = [first[0]]
    got_second = [second[0]]
    for offset in range(1, GROUP):
        moved_first, moved_second = from_behind((first[offset], second[offset]), "node", -offset)
        got_first.append(moved_first)
        got_second.append(moved_second)
    return (jnp.stack(got_first), jnp.stack(got_second))


def body(layer_input, output_grad, gate_weight, up_weight, down_weight, route_offset, gate_fixed):
    local_count = lax.axis_size("local")
    gate_cols = gate_weight[0]
    up_cols = up_weight[0]
    down_rows = down_weight[0]
    gates = gate_fixed.astype(jnp.float32) / 65536.0
    slot_list = []
    weights = []
    hit_list = []
    packed_in = []
    packed_grad = []
    for offset in range(GROUP):
        hits = route_offset == offset
        chosen = jnp.any(hits, axis=1)
        table = packer(chosen, CAPACITY)
        ranks = jnp.cumsum(chosen.astype(jnp.int32)) - 1
        slot_list.append(jnp.clip(ranks, 0, CAPACITY - 1))
        hit_list.append(hits)
        weights.append(jnp.sum(jnp.where(hits, gates, jnp.zeros_like(gates)), axis=1))
        packed_in.append(
            jnp.dot(table, layer_input, preferred_element_type=jnp.float32).astype(jnp.bfloat16)
        )
        packed_grad.append(
            jnp.dot(table, output_grad, preferred_element_type=jnp.float32).astype(jnp.bfloat16)
        )
    send_in = jnp.stack(packed_in)
    send_grad = jnp.stack(packed_grad)
    send_in, send_grad = (
        lax.all_gather(send_in, "local", axis=2, tiled=True),
        lax.all_gather(send_grad, "local", axis=2, tiled=True),
    )
    got_in, got_grad = carry_out(send_in, send_grad)
    width = got_in.shape[2]
    routed = GROUP * CAPACITY
    flat_in = got_in.reshape(routed, width)
    flat_grad = got_grad.reshape(routed, width)
    gate_part, up_grad, pre_grad = hidden_grads(flat_in, flat_grad, gate_cols, up_cols, down_rows)
    joined_grad = jnp.concatenate((pre_grad, up_grad), axis=1)
    joined_cols = jnp.concatenate((gate_cols, up_cols), axis=1)
    back = lax.dot_general(
        joined_grad, joined_cols, (((1,), (1,)), ((), ())), preferred_element_type=jnp.float32
    )
    gate_wide = jnp.broadcast_to(gate_part[:, None], (routed, local_count))
    summed, gate_sum = (
        lax.psum_scatter(
            back.reshape(GROUP, CAPACITY, width), "local", scatter_dimension=2, tiled=True
        ),
        lax.psum_scatter(
            gate_wide.reshape(GROUP, CAPACITY, local_count),
            "local",
            scatter_dimension=2,
            tiled=True,
        ),
    )
    home_back, home_gate = carry_home(summed, gate_sum)
    input_acc = jnp.zeros(layer_input.shape, jnp.float32)
    gate_acc = jnp.zeros(gate_fixed.shape, jnp.float32)
    for offset in range(GROUP):
        rows_back = jnp.take(home_back[offset], slot_list[offset], axis=0)
        gate_back = jnp.take(home_gate[offset], slot_list[offset], axis=0)
        input_acc = input_acc + weights[offset][:, None] * rows_back
        gate_acc = gate_acc + jnp.where(hit_list[offset], gate_back, jnp.zeros_like(gate_acc))
    return (input_acc.astype(jnp.bfloat16), gate_acc)


def solution(mesh):
    in_specs = (
        P("node", "local"),
        P("node", "local"),
        P("node", None, "local"),
        P("node", None, "local"),
        P("node", "local", None),
        P("node", None),
        P("node", None),
    )
    out_specs = (P("node", "local"), P("node", None))
    return jax.shard_map(body, mesh=mesh, in_specs=in_specs, out_specs=out_specs, check_vma=False)
```

profile of v0, /device:TPU:1, one launch (start us, length us, event | category | flops | bytes accessed | tf_op | source)
XLA Modules:
  0.0 314.5 jit_solution(1751071385348828509)
XLA Ops:
  7.2 0.8 fusion.55
  8.8 1.1 fusion.11
  9.9 1.1 fusion.10
  11.4 1.1 fusion.9
  12.9 1.1 fusion.8
  14.1 1.0 copy.41
  16.0 1.0 copy.36
  17.1 60.4 %all-gather.5.cloned.1.call-done = bf16[4,80,3584]{1,0,2:T(4,128)(2,1)} async-done(((bf16[4,80,448]{1,0,2:T(4,128)(2,1)}), bf16[4,80,3584]{1,0,2:T(4,128)(2,1)}) %all-gather.5.cloned.1.call-update) | async-done | bytes 2293776 | tf_op jit(solution)/shard_map/all_gather | solution.py:86
  77.5 12.8 %fusion.59 = (bf16[1,80,3584]{1,0,2:T(2,128)(2,1)S(1)}, bf16[1,80,3584]{1,0,2:T(2,128)(2,1)}, bf16[1,80,3584]{1,0,2:T(2,128)(2,1)}, bf16[1,80,3584]{1,0,2:T(2,128)(2,1)}) fusion(bf16[4,80,3584]{1,0,2:T(4,128)(2,1)} %all-gather.5.cloned.1.call-done), kind=kLoop, calls=%fused_computation.122 | loop fusion | bytes 4587520 | tf_op jit(solution)/shard_map/slice | solution.py:39
  90.3 4.7 %copy.56 = bf16[1,80,3584]{2,1,0:T(8,128)(2,1)} copy(bf16[1,80,3584]{1,0,2:T(2,128)(2,1)} %get-tuple-element.31) | data formatting | bytes 1146880
  95.1 5.3 %collective-permute-start.5 = (bf16[80,3584]{1,0:T(8,128)(2,1)}, bf16[80,3584]{1,0:T(8,128)(2,1)}, u32[]{:S(2)}, u32[]{:S(2)}) collective-permute-start(bf16[80,3584]{1,0:T(8,128)(2,1)} %bitcast.24), channel_id=1, source_target_pairs={{0,24},{8,32},{16,40},{24,48},{32,56},{40,64},{48,72},{56,80},{64,... | collective-permute-start | bytes 1720328 | tf_op jit(solution)/shard_map/ppermute | solution.py:13
  100.4 4.7 %copy.55 = bf16[1,80,3584]{2,1,0:T(8,128)(2,1)} copy(bf16[1,80,3584]{1,0,2:T(2,128)(2,1)} %get-tuple-element.29) | data formatting | bytes 1146880
  105.1 2.2 collective-permute-start.4
  107.3 4.8 %copy.54 = bf16[1,80,3584]{2,1,0:T(8,128)(2,1)} copy(bf16[1,80,3584]{1,0,2:T(2,128)(2,1)} %get-tuple-element.30) | data formatting | bytes 1146880
  112.1 2.0 collective-permute-start.3
  114.1 19.8 %all-gather.3.cloned.1.call-done = bf16[4,80,3584]{1,0,2:T(4,128)(2,1)} async-done(((bf16[4,80,448]{1,0,2:T(4,128)(2,1)}), bf16[4,80,3584]{1,0,2:T(4,128)(2,1)}) %all-gather.3.cloned.1.call-update) | async-done | bytes 2293776 | tf_op jit(solution)/shard_map/all_gather | solution.py:87
  133.9 13.2 %fusion.60 = (bf16[1,80,3584]{1,0,2:T(2,128)(2,1)}, bf16[1,80,3584]{1,0,2:T(2,128)(2,1)}, bf16[1,80,3584]{1,0,2:T(2,128)(2,1)}, bf16[1,80,3584]{1,0,2:T(2,128)(2,1)}) fusion(bf16[4,80,3584]{1,0,2:T(4,128)(2,1)} %all-gather.3.cloned.1.call-done), kind=kLoop, calls=%fused_computation.123 | loop fusion | bytes 4587520 | tf_op jit(solution)/shard_map/slice | solution.py:40
  147.0 3.1 copy.53
  150.2 4.7 %copy.52 = bf16[1,80,3584]{2,1,0:T(8,128)(2,1)} copy(bf16[1,80,3584]{1,0,2:T(2,128)(2,1)} %get-tuple-element.35) | data formatting | bytes 1146880
  154.9 5.3 %collective-permute-start.2 = (bf16[80,3584]{1,0:T(8,128)(2,1)}, bf16[80,3584]{1,0:T(8,128)(2,1)}, u32[]{:S(2)}, u32[]{:S(2)}) collective-permute-start(bf16[80,3584]{1,0:T(8,128)(2,1)} %bitcast.12), channel_id=1, source_target_pairs={{0,24},{8,32},{16,40},{24,48},{32,56},{40,64},{48,72},{56,80},{64,... | collective-permute-start | bytes 1720328 | tf_op jit(solution)/shard_map/ppermute | solution.py:13
  160.2 4.9 %copy.51 = bf16[1,80,3584]{2,1,0:T(8,128)(2,1)} copy(bf16[1,80,3584]{1,0,2:T(2,128)(2,1)} %get-tuple-element.33) | data formatting | bytes 1146880
  165.1 2.2 collective-permute-start.1
  167.3 4.7 %copy.50 = bf16[1,80,3584]{2,1,0:T(8,128)(2,1)} copy(bf16[1,80,3584]{1,0,2:T(2,128)(2,1)} %get-tuple-element.34) | data formatting | bytes 1146880
  172.0 2.1 copy.49
  174.1 2.0 collective-permute-start
  176.2 1.9 pad_maximum_fusion.1
  180.1 8.7 %collective-permute-done.1 = bf16[80,3584]{1,0:T(8,128)(2,1)} collective-permute-done((bf16[80,3584]{1,0:T(8,128)(2,1)}, bf16[80,3584]{1,0:T(8,128)(2,1)}, u32[]{:S(2)}, u32[]{:S(2)}) %collective-permute-start.1) | collective-permute-done | bytes 573472 | tf_op jit(solution)/shard_map/ppermute | solution.py:13
  188.8 1.3 collective-permute-done
  190.1 1.5 pad_maximum_fusion
  191.6 0.9 multiply_reduce_fusion
  192.5 3.0 fusion
  195.4 8.0 %copy.47 = f32[4,80,3584]{1,0,2:T(4,128)} copy(f32[4,80,3584]{2,1,0:T(8,128)} %bitcast.92) | data formatting | bytes 9175040
  203.5 8.3 %reshape.258 = f32[3584,320]{1,0:T(8,128)} reshape(f32[3584,4,80]{2,1,0:T(4,128)} %bitcast.89) | data formatting | bytes 9175040
  211.8 1.3 dynamic-slice
  213.3 21.9 %all-reduce = f32[4,80,8]{1,0,2:T(4,128)S(1)} all-reduce(f32[4,80,8]{1,0,2:T(4,128)S(1)} %broadcast_in_dim.72), channel_id=3, replica_groups=mesh['node'=96,'local'=8] {'local'}, use_global_device_ids=true, to_apply=%region_14.16.clone | all-reduce | flops 2560 | bytes 20480
  235.9 17.0 %collective-permute-start.11 = (f32[80,1]{0,1:T(1,128)S(1)}, f32[80,1]{0,1:T(1,128)S(1)}, u32[]{:S(2)}, u32[]{:S(2)}) collective-permute-start(f32[80,1]{0,1:T(1,128)S(1)} %get-tuple-element.44), channel_id=1, source_target_pairs={{0,744},{8,752},{16,760},{24,0},{32,8},{40,16},{48,24},{56,32},{64... | collective-permute-start | bytes 968 | tf_op jit(solution)/shard_map/ppermute | solution.py:13
  252.9 2.5 collective-permute-start.10
  255.4 1.9 collective-permute-start.9
  257.3 1.2 gather_fusion.4
  258.6 1.2 gather_fusion.7
  259.8 1.2 gather_fusion.6
  261.0 1.2 gather_fusion.5
  262.3 22.8 %reduce-scatter.4.cloned.1.call-done = f32[448,320]{1,0:T(8,128)} async-done(((f32[3584,320]{1,0:T(8,128)}), f32[448,320]{1,0:T(8,128)}) %reduce-scatter.4.cloned.1.call-update) | async-done | bytes 573456
  285.1 1.6 reshape.259
  287.6 9.0 %collective-permute-start.8 = (f32[80,448]{1,0:T(8,128)S(1)}, f32[80,448]{1,0:T(8,128)S(1)}, u32[]{:S(2)}, u32[]{:S(2)}) collective-permute-start(f32[80,448]{1,0:T(8,128)S(1)} %bitcast.101), channel_id=1, source_target_pairs={{0,744},{8,752},{16,760},{24,0},{32,8},{40,16},{48,24},{56,32},{64... | collective-permute-start | bytes 430088 | tf_op jit(solution)/shard_map/ppermute | solution.py:13
  296.7 2.5 collective-permute-start.7
  299.3 2.5 collective-permute-start.6
  305.1 1.2 collective-permute-done.6
  (79 shorter events, 11.3 us)
Async XLA Ops:
  7.2 184.4 %copy-start = (bf16[1,128,3584]{2,1,0:T(8,128)(2,1)S(1)}, bf16[1,128,3584]{2,1,0:T(8,128)(2,1)}, u32[]{:S(2)}) copy-start(bf16[1,128,3584]{2,1,0:T(8,128)(2,1)} %param.15) | copy-start | bytes 2752516
  7.2 8.0 %copy-start.4 = (bf16[128,448]{0,1:T(8,128)(2,1)S(1)}, bf16[128,448]{0,1:T(8,128)(2,1)}, u32[]{:S(2)}) copy-start(bf16[128,448]{0,1:T(8,128)(2,1)} %param.12) | copy-start | bytes 344068
  7.2 70.3 %all-gather.5.cloned.1.call-start = ((), (), s32[]{:S(2)}) async-start(), calls=%async_computation.2 | async-start | bytes 4128768 | tf_op jit(solution)/shard_map/all_gather | solution.py:86
  15.1 118.8 %all-gather.3.cloned.1.call-start = ((), (), s32[]{:S(2)}) async-start(), calls=%async_computation.1 | async-start | bytes 4128768 | tf_op jit(solution)/shard_map/all_gather | solution.py:87
  17.0 268.1 %reduce-scatter.4.cloned.1.call-start = ((), (), s32[]{:S(2)}) async-start(), calls=%async_computation.3 | async-start | bytes 6193152
  95.1 79.1 %collective-permute-start.5 = (bf16[80,3584]{1,0:T(8,128)(2,1)}, bf16[80,3584]{1,0:T(8,128)(2,1)}, u32[]{:S(2)}, u32[]{:S(2)}) collective-permute-start(bf16[80,3584]{1,0:T(8,128)(2,1)} %bitcast.24), channel_id=1, source_target_pairs={{0,24},{8,32},{16,40},{24,48},{32,56},{40,64},{48,72},{56,80},{64,... | collective-permute-start | bytes 1720328 | tf_op jit(solution)/shard_map/ppermute | solution.py:13
  105.1 71.0 %collective-permute-start.4 = (bf16[80,3584]{1,0:T(8,128)(2,1)}, bf16[80,3584]{1,0:T(8,128)(2,1)}, u32[]{:S(2)}, u32[]{:S(2)}) collective-permute-start(bf16[80,3584]{1,0:T(8,128)(2,1)} %bitcast.22), channel_id=1, source_target_pairs={{0,16},{8,24},{16,32},{24,40},{32,48},{40,56},{48,64},{56,72},{64,... | collective-permute-start | bytes 1720328 | tf_op jit(solution)/shard_map/ppermute | solution.py:13
  112.1 64.1 %collective-permute-start.3 = (bf16[80,3584]{1,0:T(8,128)(2,1)}, bf16[80,3584]{1,0:T(8,128)(2,1)}, u32[]{:S(2)}, u32[]{:S(2)}) collective-permute-start(bf16[80,3584]{1,0:T(8,128)(2,1)} %bitcast.20), channel_id=1, source_target_pairs={{0,8},{8,16},{16,24},{24,32},{32,40},{40,48},{48,56},{56,64},{64,7... | collective-permute-start | bytes 1720328 | tf_op jit(solution)/shard_map/ppermute | solution.py:13
  154.9 25.2 %collective-permute-start.2 = (bf16[80,3584]{1,0:T(8,128)(2,1)}, bf16[80,3584]{1,0:T(8,128)(2,1)}, u32[]{:S(2)}, u32[]{:S(2)}) collective-permute-start(bf16[80,3584]{1,0:T(8,128)(2,1)} %bitcast.12), channel_id=1, source_target_pairs={{0,24},{8,32},{16,40},{24,48},{32,56},{40,64},{48,72},{56,80},{64,... | collective-permute-start | bytes 1720328 | tf_op jit(solution)/shard_map/ppermute | solution.py:13
  160.2 11.8 %copy-start.1 = (bf16[1,80,3584]{1,0,2:T(2,128)(2,1)S(1)}, bf16[1,80,3584]{1,0,2:T(2,128)(2,1)}, u32[]{:S(2)}) copy-start(bf16[1,80,3584]{1,0,2:T(2,128)(2,1)} %get-tuple-element.32) | copy-start | bytes 1720324
  165.1 23.7 %collective-permute-start.1 = (bf16[80,3584]{1,0:T(8,128)(2,1)}, bf16[80,3584]{1,0:T(8,128)(2,1)}, u32[]{:S(2)}, u32[]{:S(2)}) collective-permute-start(bf16[80,3584]{1,0:T(8,128)(2,1)} %bitcast.10), channel_id=1, source_target_pairs={{0,16},{8,24},{16,32},{24,40},{32,48},{40,56},{48,64},{56,72},{64,... | collective-permute-start | bytes 1720328 | tf_op jit(solution)/shard_map/ppermute | solution.py:13
  174.1 16.0 %collective-permute-start = (bf16[80,3584]{1,0:T(8,128)(2,1)}, bf16[80,3584]{1,0:T(8,128)(2,1)S(1)}, u32[]{:S(2)}, u32[]{:S(2)}) collective-permute-start(bf16[80,3584]{1,0:T(8,128)(2,1)} %bitcast.98), channel_id=1, source_target_pairs={{0,8},{8,16},{16,24},{24,32},{32,40},{40,48},{48,56},{56,64},{64,7... | collective-permute-start | bytes 1720328 | tf_op jit(solution)/shard_map/ppermute | solution.py:13
  176.2 2.0 copy-start.2
  178.1 1.2 copy-start.3
  235.9 22.7 %collective-permute-start.11 = (f32[80,1]{0,1:T(1,128)S(1)}, f32[80,1]{0,1:T(1,128)S(1)}, u32[]{:S(2)}, u32[]{:S(2)}) collective-permute-start(f32[80,1]{0,1:T(1,128)S(1)} %get-tuple-element.44), channel_id=1, source_target_pairs={{0,744},{8,752},{16,760},{24,0},{32,8},{40,16},{48,24},{56,32},{64... | collective-permute-start | bytes 968 | tf_op jit(solution)/shard_map/ppermute | solution.py:13
  252.9 6.9 %collective-permute-start.10 = (f32[80,1]{0,1:T(1,128)S(1)}, f32[80,1]{0,1:T(1,128)S(1)}, u32[]{:S(2)}, u32[]{:S(2)}) collective-permute-start(f32[80,1]{0,1:T(1,128)S(1)} %get-tuple-element.45), channel_id=1, source_target_pairs={{0,752},{8,760},{16,0},{24,8},{32,16},{40,24},{48,32},{56,40},{64,... | collective-permute-start | bytes 968 | tf_op jit(solution)/shard_map/ppermute | solution.py:13
  255.4 5.7 %collective-permute-start.9 = (f32[80,1]{0,1:T(1,128)S(1)}, f32[80,1]{0,1:T(1,128)S(1)}, u32[]{:S(2)}, u32[]{:S(2)}) collective-permute-start(f32[80,1]{0,1:T(1,128)S(1)} %get-tuple-element.46), channel_id=1, source_target_pairs={{0,760},{8,0},{16,8},{24,16},{32,24},{40,32},{48,40},{56,48},{64,5... | collective-permute-start | bytes 968 | tf_op jit(solution)/shard_map/ppermute | solution.py:13
  262.3 39.5 %copy-start.5 = (s32[128,2]{0,1:T(2,128)S(1)}, s32[128,2]{0,1:T(2,128)}, u32[]{:S(2)}) copy-start(s32[128,2]{0,1:T(2,128)} %param.16) | copy-start | bytes 3076
  262.3 39.5 %copy-start.6 = (s32[128,2]{0,1:T(2,128)S(1)}, s32[128,2]{0,1:T(2,128)}, u32[]{:S(2)}) copy-start(s32[128,2]{0,1:T(2,128)} %param.17) | copy-start | bytes 3076
  287.6 15.8 %collective-permute-start.8 = (f32[80,448]{1,0:T(8,128)S(1)}, f32[80,448]{1,0:T(8,128)S(1)}, u32[]{:S(2)}, u32[]{:S(2)}) collective-permute-start(f32[80,448]{1,0:T(8,128)S(1)} %bitcast.101), channel_id=1, source_target_pairs={{0,744},{8,752},{16,760},{24,0},{32,8},{40,16},{48,24},{56,32},{64... | collective-permute-start | bytes 430088 | tf_op jit(solution)/shard_map/ppermute | solution.py:13
  296.7 7.6 %collective-permute-start.7 = (f32[80,448]{1,0:T(8,128)S(1)}, f32[80,448]{1,0:T(8,128)S(1)}, u32[]{:S(2)}, u32[]{:S(2)}) collective-permute-start(f32[80,448]{1,0:T(8,128)S(1)} %bitcast.100), channel_id=1, source_target_pairs={{0,752},{8,760},{16,0},{24,8},{32,16},{40,24},{48,32},{56,40},{64,... | collective-permute-start | bytes 430088 | tf_op jit(solution)/shard_map/ppermute | solution.py:13
  299.3 7.0 %collective-permute-start.6 = (f32[80,448]{1,0:T(8,128)S(1)}, f32[80,448]{1,0:T(8,128)S(1)}, u32[]{:S(2)}, u32[]{:S(2)}) collective-permute-start(f32[80,448]{1,0:T(8,128)S(1)} %bitcast.99), channel_id=1, source_target_pairs={{0,760},{8,0},{16,8},{24,16},{32,24},{40,32},{48,40},{56,48},{64,5... | collective-permute-start | bytes 430088 | tf_op jit(solution)/shard_map/ppermute | solution.py:13
Sparse Core Ops, SparseCore 0:
  15.2 62.2 all-gather.4
  79.9 53.9 all-gather.2
  211.9 73.1 reduce-scatter.3
where the time goes:
time: 316 us; the launch traced here: 315 us
  waiting for transfers between devices  114 us (36%)
  local copies, waits for them, and re-layouts  92.5 us (29%)
  starting transfers between devices  54.6 us (17%)
  blocking collectives  21.9 us (7%)
  between operations  14.3 us (5%)
  matrix products  10.4 us (3%)
  other arithmetic  6.33 us (2%)
    all_gather x1, waiting for transfers between devices, body(): lax.all_gather(send_in, 'local', axis=2, tiled=True)  60.4 us
    unnamed x32, local copies, waits for them, and re-layouts  55.3 us
    ppermute x12, starting transfers between devices, from_behind(): return lax.ppermute(value, axis, pairs)  54.4 us
    unnamed x4, waiting for transfers between devices  22.9 us
    unnamed x1, blocking collectives  21.9 us
    all_gather x1, waiting for transfers between devices, body(): lax.all_gather(send_grad, 'local', axis=2, tiled=True)  19.8 us
    slice x1, local copies, waits for them, and re-layouts, carry_out(): got_second = [second[0]]  13.2 us
    slice x1, local copies, waits for them, and re-layouts, carry_out(): got_first = [first[0]]  12.8 us
  transfers between devices with their start and end apart: 15, of which 7 were waited for; matrix products, arithmetic and copies ran while one was open for 24% of the time, Pallas kernels for 0%

commit v1 on v0

v1 whole, which is shorter than its diff:
```python
import jax
import jax.numpy as jnp
from jax import lax
from jax.experimental import pallas as pl
from jax.experimental.pallas import tpu as pltpu
from jax.sharding import PartitionSpec as P

GROUP = 4
CAP = 80
TOK = 128
LANE = 128
FEAT = 448
HID = 128
LOCAL = 8
ROUTED = GROUP * CAP
OUT_ROWS = 7 * CAP + 16
PART_ROWS = 3 * ROUTED + 2 * CAP + 16
HOME_ROWS = 4 * CAP + 16
LEVELS = 15
INTERPRET = False

f32 = jnp.float32
bf16 = jnp.bfloat16
NT = (((1,), (1,)), ((), ()))
TN = (((0,), (0,)), ((), ()))


def from_behind(value, axis, steps):
    count = lax.axis_size(axis)
    pairs = [(source, (source + steps) % count) for source in range(count)]
    return lax.ppermute(value, axis, pairs)


def tables(route):
    offsets = lax.broadcasted_iota(jnp.int32, (8, TOK), 0)
    first = jnp.broadcast_to(route[0:1], (8, TOK)) == offsets
    second = jnp.broadcast_to(route[1:2], (8, TOK)) == offsets
    chosen = jnp.where(first | second, 1.0, 0.0)
    before = lax.broadcasted_iota(jnp.int32, (TOK, TOK), 0) < lax.broadcasted_iota(jnp.int32, (TOK, TOK), 1)
    ranks = jnp.dot(chosen.astype(bf16), jnp.where(before, 1.0, 0.0).astype(bf16), preferred_element_type=f32)
    ranks = jnp.where(chosen > 0.5, ranks, -1.0)
    slots = lax.broadcasted_iota(jnp.int32, (CAP, TOK), 0).astype(f32)
    return [
        jnp.where(slots == jnp.broadcast_to(ranks[o : o + 1], (CAP, TOK)), 1.0, 0.0).astype(bf16)
        for o in range(GROUP)
    ]


def level_of(top):
    level = jnp.zeros_like(top)
    for step in range(1, LEVELS):
        level = level + jnp.where(top < 2.0 ** (3 - 8 * step), 1.0, 0.0)
    return level


def power_of(level, sign):
    power = jnp.full_like(level, 2.0 ** (sign * 12))
    for step in range(1, LEVELS):
        power = jnp.where(level > step - 0.5, 2.0 ** (sign * (12 + 8 * step)), power)
    return power


def scaled(values):
    wide = values.astype(f32)
    top = jnp.max(jnp.max(jnp.abs(wide), axis=0, keepdims=True), axis=1, keepdims=True)
    level = level_of(jnp.broadcast_to(top, (1, TOK)))
    return (wide * power_of(level, 1)).astype(bf16), level


def pack_kernel(route_ref, in_ref, grad_ref, *out_refs):
    table = jnp.concatenate(tables(route_ref[...]), axis=0)
    rows_in, level_in = scaled(in_ref[...])
    rows_grad, level_grad = scaled(grad_ref[...])
    tail = jnp.concatenate([rows_in[384:448], rows_grad[384:448]], axis=0)
    parts = [rows_in[0:128], rows_in[128:256], rows_in[256:384]]
    parts += [rows_grad[0:128], rows_grad[128:256], rows_grad[256:384], tail]
    for place, part in enumerate(parts):
        packed = lax.dot_general(table, part, NT, preferred_element_type=f32).astype(bf16)
        for o in range(GROUP):
            out_refs[o][place * CAP : (place + 1) * CAP, :] = packed[o * CAP : (o + 1) * CAP]
    line = lax.broadcasted_iota(jnp.int32, (16, LANE), 0)
    levels = jnp.where(line == 0, level_in, jnp.where(line == 1, level_grad, 0.0)).astype(bf16)
    for o in range(GROUP):
        out_refs[o][7 * CAP : OUT_ROWS, :] = levels


def expert_kernel(got_ref, gate_ref, up_ref, down_ref, out_ref):
    zero_cols = jnp.zeros((64, 2 * HID), bf16)
    zero_half = jnp.zeros((64, HID), bf16)
    pre = jnp.zeros((ROUTED, 2 * HID), f32)
    grad = jnp.zeros((ROUTED, HID), f32)

    def rows_of(d, o, place):
        start = d * GROUP * OUT_ROWS + o * OUT_ROWS + place * CAP
        return got_ref[start : start + CAP, :]

    def column(d, place):
        return jnp.concatenate([rows_of(d, o, place) for o in range(GROUP)], axis=0)

    for d in range(LOCAL):
        low = d * FEAT
        tail = column(d, 6)
        in_a = jnp.concatenate([column(d, 0), column(d, 1)], axis=1)
        in_b = jnp.concatenate([column(d, 2), tail], axis=1)
        grad_a = jnp.concatenate([column(d, 3), column(d, 4)], axis=1)
        grad_b = jnp.concatenate([column(d, 5), tail], axis=1)
        both = jnp.concatenate([gate_ref[low : low + FEAT, :], up_ref[low : low + FEAT, :]], axis=1)
        down = down_ref[low : low + FEAT, :]
        both_b = jnp.concatenate([both[256:448], zero_cols], axis=0)
        down_b = jnp.concatenate([down[256:384], zero_half, down[384:448]], axis=0)
        part = jnp.dot(in_a, both[0:256], preferred_element_type=f32)
        part = part + jnp.dot(in_b, both_b, preferred_element_type=f32)
        part_grad = jnp.dot(grad_a, down[0:256], preferred_element_type=f32)
        part_grad = part_grad + jnp.dot(grad_b, down_b, preferred_element_type=f32)
        back_in = []
        back_grad = []
        for o in range(GROUP):
            start = d * GROUP * OUT_ROWS + o * OUT_ROWS + 7 * CAP
            levels = got_ref[start : start + 16, :].astype(f32)
            inverse_in = power_of(levels[0:1], -1)
            inverse_grad = power_of(levels[1:2], -1)
            back_in.append(part[o * CAP : (o + 1) * CAP] * jnp.concatenate([inverse_in, inverse_in], axis=1))
            back_grad.append(part_grad[o * CAP : (o + 1) * CAP] * inverse_grad)
        pre = pre + jnp.concatenate(back_in, axis=0)
        grad = grad + jnp.concatenate(back_grad, axis=0)
    gate_pre = pre[:, 0:HID]
    up_pre = pre[:, HID : 2 * HID]
    sigmoid = jax.nn.sigmoid(gate_pre)
    swish = gate_pre * sigmoid
    product = swish * up_pre * grad
    up_grad = (grad * swish).astype(bf16)
    pre_grad = (grad * up_pre * sigmoid * (1.0 + gate_pre * (1.0 - sigmoid))).astype(bf16)
    hidden = jnp.concatenate([pre_grad, up_grad], axis=1)
    paired = jnp.concatenate([hidden[0 : 2 * CAP], hidden[2 * CAP : 4 * CAP]], axis=1)
    line = lax.broadcasted_iota(jnp.int32, (16, LANE), 0)
    gate_rows = jnp.zeros((16, LANE), f32)
    for o in range(GROUP):
        piece = jnp.concatenate([product[o * CAP : (o + 1) * CAP], jnp.zeros((LANE - CAP, HID), f32)], axis=0)
        total = lax.dot_general(
            jnp.ones((8, HID), f32), piece, NT, preferred_element_type=f32, precision=lax.Precision.HIGHEST
        )[0:1]
        high = total.astype(bf16).astype(f32)
        gate_rows = jnp.where(line == 2 * o, high, gate_rows)
        gate_rows = jnp.where(line == 2 * o + 1, total - high, gate_rows)
    gate_rows = gate_rows.astype(bf16)
    for d in range(LOCAL):
        low = d * FEAT
        base = d * PART_ROWS
        both = jnp.concatenate([gate_ref[low : low + FEAT, :], up_ref[low : low + FEAT, :]], axis=1)
        wide = lax.dot_general(hidden, both[0:384], NT, preferred_element_type=f32).astype(bf16)
        for j in range(3):
            out_ref[base + j * ROUTED : base + (j + 1) * ROUTED, :] = wide[:, j * LANE : (j + 1) * LANE]
        corner = jnp.concatenate([both[384:448], zero_cols], axis=1)
        other = jnp.concatenate([zero_cols, both[384:448]], axis=1)
        ends = jnp.concatenate([corner, other], axis=0)
        tail = lax.dot_general(paired, ends, NT, preferred_element_type=f32).astype(bf16)
        out_ref[base + 3 * ROUTED : base + 3 * ROUTED + 2 * CAP, :] = tail
        out_ref[base + 3 * ROUTED + 2 * CAP : base + PART_ROWS, :] = gate_rows


def sum_kernel(part_ref, *out_refs):
    def total(start, rows):
        value = part_ref[start : start + rows, :].astype(f32)
        for d in range(1, LOCAL):
            value = value + part_ref[d * PART_ROWS + start : d * PART_ROWS + start + rows, :].astype(f32)
        return value

    for j in range(3):
        for o in range(GROUP):
            out_refs[o][j * CAP : (j + 1) * CAP, :] = total(j * ROUTED + o * CAP, CAP).astype(bf16)
    for half in range(2):
        tail = total(3 * ROUTED + half * CAP, CAP).astype(bf16)
        out_refs[half][3 * CAP : 4 * CAP, :] = tail
        out_refs[half + 2][3 * CAP : 4 * CAP, :] = tail
    gates = total(3 * ROUTED + 2 * CAP, 16)
    line = lax.broadcasted_iota(jnp.int32, (16, LANE), 0)
    for o in range(GROUP):
        gate = gates[2 * o : 2 * o + 1] + gates[2 * o + 1 : 2 * o + 2]
        high = gate.astype(bf16).astype(f32)
        rows = jnp.where(line == 0, high, jnp.where(line == 1, gate - high, 0.0))
        out_refs[o][4 * CAP : HOME_ROWS, :] = rows.astype(bf16)


def unpack_kernel(route_ref, fixed_ref, *refs):
    got_refs = refs[0:GROUP]
    out_ref, gate_ref = refs[GROUP], refs[GROUP + 1]
    route = route_ref[...]
    weights = fixed_ref[...].astype(f32) / 65536.0
    table = tables(route)
    head = jnp.zeros((384, TOK), f32)
    tail = jnp.zeros((64, TOK), f32)
    gate = jnp.zeros((2, TOK), f32)
    for o in range(GROUP):
        got = got_refs[o]
        hits = route == o
        weight = jnp.sum(jnp.where(hits, weights, 0.0), axis=0, keepdims=True)
        rows = jnp.concatenate([got[j * CAP : (j + 1) * CAP, :] for j in range(4)], axis=1)
        back = lax.dot_general(rows, table[o], TN, preferred_element_type=f32)
        head = head + weight * back[0:384]
        tail = tail + weight * (back[384:448] if o < 2 else back[448:512])
        gates = jnp.dot(got[4 * CAP : HOME_ROWS, 0:CAP], table[o], preferred_element_type=f32)
        gate = gate + jnp.where(hits, gates[0:1] + gates[1:2], 0.0)
    out_ref[0:384, :] = head.astype(bf16)
    out_ref[384:448, :] = tail.astype(bf16)
    gate_ref[...] = gate


def call(kernel, outs, *args):
    return pl.pallas_call(kernel, out_shape=outs, interpret=INTERPRET)(*args)


def body(layer_input, output_grad, gate_weight, up_weight, down_weight, route_offset, gate_fixed):
    route = route_offset.T
    packed = call(
        pack_kernel,
        [jax.ShapeDtypeStruct((OUT_ROWS, LANE), bf16)] * GROUP,
        route,
        layer_input.T,
        output_grad.T,
    )
    got = [packed[0]] + [from_behind(packed[o], "node", o) for o in range(1, GROUP)]
    shard = jnp.concatenate(got, axis=0).astype(jnp.float16)
    full = lax.all_gather(shard, "local", axis=0, tiled=True).astype(bf16)
    partial = call(
        expert_kernel,
        jax.ShapeDtypeStruct((LOCAL * PART_ROWS, LANE), bf16),
        full,
        gate_weight[0],
        up_weight[0],
        down_weight[0].T,
    )
    shares = lax.all_to_all(partial, "local", 0, 0, tiled=True)
    summed = call(sum_kernel, [jax.ShapeDtypeStruct((HOME_ROWS, LANE), bf16)] * GROUP, shares)
    home = [summed[0]] + [from_behind(summed[o], "node", -o) for o in range(1, GROUP)]
    input_grad, gate_grad = call(
        unpack_kernel,
        [jax.ShapeDtypeStruct((FEAT, TOK), bf16), jax.ShapeDtypeStruct((2, TOK), f32)],
        route,
        gate_fixed.T,
        *home,
    )
    return input_grad.T, gate_grad.T


def solution(mesh):
    in_specs = (
        P("node", "local"),
        P("node", "local"),
        P("node", None, "local"),
        P("node", None, "local"),
        P("node", "local", None),
        P("node", None),
        P("node", None),
    )
    out_specs = (P("node", "local"), P("node", None))
    return jax.shard_map(body, mesh=mesh, in_specs=in_specs, out_specs=out_specs, check_vma=False)
```

time: 316 us -> 172 us (0.54)
  waiting for transfers between devices: 114 us -> 19.7 us
  local copies, waits for them, and re-layouts: 92.5 us -> 2.86 us
  blocking collectives: 21.9 us -> 110 us
  starting transfers between devices: 54.6 us -> 20.6 us
  Pallas kernels: 0 us -> 14.5 us
  between operations: 14.3 us -> 0.71 us
  matrix products: 10.4 us -> 0 us
  other arithmetic: 6.33 us -> 2.77 us
    all_gather x2 -> x0, waiting for transfers between devices: 80.2 us -> none  [the longest x1 60.4 us: body(): lax.all_gather(send_in, 'local', axis=2, tiled=True)]
    all_to_all x0 -> x1, blocking collectives: none -> 60.2 us  [body(): shares = lax.all_to_all(partial, 'local', 0, 0, tiled=True)]
    unnamed x32 -> x9, local copies, waits for them, and re-layouts: 55.3 us -> 2.86 us
    all_gather x0 -> x1, blocking collectives: none -> 50.1 us  [body(): full = lax.all_gather(shard, 'local', axis=0, tiled=True).astype(bf16)]
    ppermute x12 -> x6, starting transfers between devices: 54.4 us -> 20.6 us  [from_behind(): return lax.ppermute(value, axis, pairs)]
    slice x3 -> x0, local copies, waits for them, and re-layouts: 26.6 us -> none  [the longest x1 13.2 us: carry_out(): got_second = [second[0]]]
    unnamed x4 -> x0, waiting for transfers between devices: 22.9 us -> none
    unnamed x1 -> x0, blocking collectives: 21.9 us -> none
  transfers between devices with their start and end apart: 15 -> 6, of which waited for: 7 -> 5; matrix products, arithmetic and copies ran while one was open for 24% -> 1% of each run, Pallas kernels for 0% -> 0%
where the time goes in v1:
time: 172 us; the launch traced here: 171 us
  blocking collectives  110 us (64%)
  starting transfers between devices  20.6 us (12%)
  waiting for transfers between devices  19.7 us (11%)
  Pallas kernels  14.5 us (8%)
  local copies, waits for them, and re-layouts  2.86 us (2%)
  other arithmetic  2.77 us (2%)
    all_to_all x1, blocking collectives, body(): shares = lax.all_to_all(partial, 'local', 0, 0, tiled=True)  60.2 us
    all_gather x1, blocking collectives, body(): full = lax.all_gather(shard, 'local', axis=0, tiled=True).astype(bf16)  50.1 us
    ppermute x6, starting transfers between devices, from_behind(): return lax.ppermute(value, axis, pairs)  20.6 us
    ppermute x6, waiting for transfers between devices, from_behind(): return lax.ppermute(value, axis, pairs)  19.7 us
    pallas_call x4, Pallas kernels, call(): return pl.pallas_call(kernel, out_shape=outs, interpret=INTERPRET)(*args)  14.5 us
  transfers between devices with their start and end apart: 6, of which 5 were waited for; matrix products, arithmetic and copies ran while one was open for 1% of the time, Pallas kernels for 0%

profile of v1, /device:TPU:1, one launch (start us, length us, event | category | flops | bytes accessed | tf_op | source)
XLA Modules:
  0.0 171.4 jit_solution(1394750207542098292)
XLA Ops:
  0.6 2.2 %shard_map.86 = (bf16[576,128]{1,0:T(8,128)(2,1)}, bf16[576,128]{1,0:T(8,128)(2,1)}, bf16[576,128]{1,0:T(8,128)(2,1)}, bf16[576,128]{1,0:T(8,128)(2,1)}) custom-call(s32[2,128]{1,0:T(2,128)} %bitcast.20, bf16[448,128]{1,0:T(8,128)(2,1)} %bitcast.18, bf16[448,128]{1,0:T(8,128)(2,1)} %bitcast.19), custom_call_target="tpu_custom_call" | custom-call | tf_op jit(solution)/shard_map/pallas_call | solution.py:209
  2.9 0.0 copy-start
  2.9 4.6 %collective-permute-start = (bf16[576,128]{1,0:T(8,128)(2,1)}, bf16[576,128]{1,0:T(8,128)(2,1)S(1)}, u32[]{:S(2)}, u32[]{:S(2)}) collective-permute-start(bf16[576,128]{1,0:T(8,128)(2,1)} %get-tuple-element.13), channel_id=1, source_target_pairs={{0,8},{8,16},{16,24},{24,32},{32,40},{40,48},{48,56},{56,64},{64,7... | collective-permute-start | bytes 442376 | tf_op jit(solution)/shard_map/ppermute | solution.py:31
  7.5 3.1 %collective-permute-start.1 = (bf16[576,128]{1,0:T(8,128)(2,1)}, bf16[576,128]{1,0:T(8,128)(2,1)S(1)}, u32[]{:S(2)}, u32[]{:S(2)}) collective-permute-start(bf16[576,128]{1,0:T(8,128)(2,1)} %get-tuple-element.14), channel_id=1, source_target_pairs={{0,16},{8,24},{16,32},{24,40},{32,48},{40,56},{48,64},{56,72},{64,... | collective-permute-start | bytes 442376 | tf_op jit(solution)/shard_map/ppermute | solution.py:31
  10.6 3.4 %collective-permute-start.2 = (bf16[576,128]{1,0:T(8,128)(2,1)}, bf16[576,128]{1,0:T(8,128)(2,1)S(1)}, u32[]{:S(2)}, u32[]{:S(2)}) collective-permute-start(bf16[576,128]{1,0:T(8,128)(2,1)} %get-tuple-element.15), channel_id=1, source_target_pairs={{0,24},{8,32},{16,40},{24,48},{32,56},{40,64},{48,72},{56,80},{64,... | collective-permute-start | bytes 442376 | tf_op jit(solution)/shard_map/ppermute | solution.py:31
  14.1 2.2 %copy.9 = bf16[1,128,3584]{1,2,0:T(8,128)(2,1)} copy(bf16[1,128,3584]{2,1,0:T(8,128)(2,1)} %param.11) | data formatting | bytes 1835008 | tf_op args[4]
  16.3 0.2 collective-permute-done
  16.4 9.5 %collective-permute-done.1 = bf16[576,128]{1,0:T(8,128)(2,1)S(1)} collective-permute-done((bf16[576,128]{1,0:T(8,128)(2,1)}, bf16[576,128]{1,0:T(8,128)(2,1)S(1)}, u32[]{:S(2)}, u32[]{:S(2)}) %collective-permute-start.1) | collective-permute-done | bytes 147488 | tf_op jit(solution)/shard_map/ppermute | solution.py:31
  26.0 4.4 %collective-permute-done.2 = bf16[576,128]{1,0:T(8,128)(2,1)S(1)} collective-permute-done((bf16[576,128]{1,0:T(8,128)(2,1)}, bf16[576,128]{1,0:T(8,128)(2,1)S(1)}, u32[]{:S(2)}, u32[]{:S(2)}) %collective-permute-start.2) | collective-permute-done | bytes 147488 | tf_op jit(solution)/shard_map/ppermute | solution.py:31
  30.4 0.0 copy-done
  30.4 0.1 maximum_convert_fusion
  30.5 50.1 %all-gather.1 = f16[18432,128]{1,0:T(8,128)(2,1)S(1)} all-gather(f16[2304,128]{1,0:T(8,128)(2,1)S(1)} %maximum_convert_fusion), channel_id=1, replica_groups=mesh['node'=96,'local'=8] {'local'}, dimensions={0}, use_global_device_ids=true | all-gather | bytes 5308416 | tf_op jit(solution)/shard_map/all_gather | solution.py:223
  80.6 2.7 %convert_element_type.7.got_ref = bf16[18432,128]{1,0:T(8,128)(2,1)} convert(f16[18432,128]{1,0:T(8,128)(2,1)S(1)} %all-gather.1) | non-fusion elementwise | flops 2359296 | bytes 9437184 | tf_op jit(solution)/shard_map/convert_element_type | solution.py:223
  83.3 7.5 %shard_map.87 = bf16[9088,128]{1,0:T(8,128)(2,1)} custom-call(bf16[18432,128]{1,0:T(8,128)(2,1)} %convert_element_type.7.got_ref, bf16[3584,128]{1,0:T(8,128)(2,1)} %bitcast.16, bf16[3584,128]{1,0:T(8,128)(2,1)} %bitcast.17, bf16[3584,128]{1,0:T(8,128)(2,1)} %bitcast.15), custom_call_target="tpu_custom_call" | custom-call | tf_op jit(solution)/shard_map/pallas_call | solution.py:209
  90.8 60.2 %all_to_all.11 = bf16[8,1136,128]{2,1,0:T(8,128)(2,1)} all-to-all(bf16[8,1136,128]{2,1,0:T(8,128)(2,1)} %bitcast.14), channel_id=1, replica_groups=mesh['node'=96,'local'=8] {'local'}, dimensions={0} | all-to-all | bytes 4653056 | tf_op jit(solution)/shard_map/all_to_all | solution.py:232
  151.0 2.6 %shard_map.88 = (bf16[336,128]{1,0:T(8,128)(2,1)}, bf16[336,128]{1,0:T(8,128)(2,1)}, bf16[336,128]{1,0:T(8,128)(2,1)}, bf16[336,128]{1,0:T(8,128)(2,1)}) custom-call(bf16[9088,128]{1,0:T(8,128)(2,1)} %bitcast.13), custom_call_target="tpu_custom_call" | custom-call | tf_op jit(solution)/shard_map/pallas_call | solution.py:209
  153.7 4.1 %collective-permute-start.3 = (bf16[336,128]{1,0:T(8,128)(2,1)}, bf16[336,128]{1,0:T(8,128)(2,1)S(1)}, u32[]{:S(2)}, u32[]{:S(2)}) collective-permute-start(bf16[336,128]{1,0:T(8,128)(2,1)} %get-tuple-element.17), channel_id=1, source_target_pairs={{0,760},{8,0},{16,8},{24,16},{32,24},{40,32},{48,40},{56,48},{64,5... | collective-permute-start | bytes 258056 | tf_op jit(solution)/shard_map/ppermute | solution.py:31
  157.8 3.4 %collective-permute-start.4 = (bf16[336,128]{1,0:T(8,128)(2,1)}, bf16[336,128]{1,0:T(8,128)(2,1)S(1)}, u32[]{:S(2)}, u32[]{:S(2)}) collective-permute-start(bf16[336,128]{1,0:T(8,128)(2,1)} %get-tuple-element.18), channel_id=1, source_target_pairs={{0,752},{8,760},{16,0},{24,8},{32,16},{40,24},{48,32},{56,40},{64,... | collective-permute-start | bytes 258056 | tf_op jit(solution)/shard_map/ppermute | solution.py:31
  161.1 1.9 %collective-permute-start.5 = (bf16[336,128]{1,0:T(8,128)(2,1)}, bf16[336,128]{1,0:T(8,128)(2,1)S(1)}, u32[]{:S(2)}, u32[]{:S(2)}) collective-permute-start(bf16[336,128]{1,0:T(8,128)(2,1)} %get-tuple-element.19), channel_id=1, source_target_pairs={{0,744},{8,752},{16,760},{24,0},{32,8},{40,16},{48,24},{56,32},{64... | collective-permute-start | bytes 258056 | tf_op jit(solution)/shard_map/ppermute | solution.py:31
  163.1 0.0 collective-permute-done.3.refs_1_
  163.1 0.0 copy-start.1
  163.1 0.8 collective-permute-done.4.refs_2_
  163.9 0.0 copy-start.2
  163.9 4.7 %collective-permute-done.5.refs_3_ = bf16[336,128]{1,0:T(8,128)(2,1)S(1)} collective-permute-done((bf16[336,128]{1,0:T(8,128)(2,1)}, bf16[336,128]{1,0:T(8,128)(2,1)S(1)}, u32[]{:S(2)}, u32[]{:S(2)}) %collective-permute-start.5) | collective-permute-done | bytes 86048 | tf_op jit(solution)/shard_map/ppermute | solution.py:31
  168.7 0.0 copy-start.3
  168.7 0.0 copy-done.1
  168.7 0.0 copy-done.2
  168.7 0.6 copy-done.3
  169.3 2.1 %shard_map.89 = (bf16[448,128]{1,0:T(8,128)(2,1)}, f32[2,128]{1,0:T(2,128)}) custom-call(s32[2,128]{1,0:T(2,128)} %bitcast.21, s32[2,128]{1,0:T(2,128)} %bitcast.22, bf16[336,128]{1,0:T(8,128)(2,1)} %get-tuple-element.16.refs_0_, bf16[336,128]{1,0:T(8,128)(2,1)} %copy-done.1, bf16[336,128]{1,0:T(8,128)(2,1)} %copy-done.2, bf16[336,128]{1,0:T(8,128)(2,1)} %copy-done.3), custom_call_target="tpu_custom_call" | custom-call | tf_op jit(solution)/shard_map/pallas_call | solution.py:209
Async XLA Ops:
  2.9 27.5 %copy-start = (bf16[576,128]{1,0:T(8,128)(2,1)S(1)}, bf16[576,128]{1,0:T(8,128)(2,1)}, u32[]{:S(2)}) copy-start(bf16[576,128]{1,0:T(8,128)(2,1)} %get-tuple-element.12) | copy-start | bytes 442372
  2.9 13.6 %collective-permute-start = (bf16[576,128]{1,0:T(8,128)(2,1)}, bf16[576,128]{1,0:T(8,128)(2,1)S(1)}, u32[]{:S(2)}, u32[]{:S(2)}) collective-permute-start(bf16[576,128]{1,0:T(8,128)(2,1)} %get-tuple-element.13), channel_id=1, source_target_pairs={{0,8},{8,16},{16,24},{24,32},{32,40},{40,48},{48,56},{56,64},{64,7... | collective-permute-start | bytes 442376 | tf_op jit(solution)/shard_map/ppermute | solution.py:31
  7.5 18.5 %collective-permute-start.1 = (bf16[576,128]{1,0:T(8,128)(2,1)}, bf16[576,128]{1,0:T(8,128)(2,1)S(1)}, u32[]{:S(2)}, u32[]{:S(2)}) collective-permute-start(bf16[576,128]{1,0:T(8,128)(2,1)} %get-tuple-element.14), channel_id=1, source_target_pairs={{0,16},{8,24},{16,32},{24,40},{32,48},{40,56},{48,64},{56,72},{64,... | collective-permute-start | bytes 442376 | tf_op jit(solution)/shard_map/ppermute | solution.py:31
  10.6 19.8 %collective-permute-start.2 = (bf16[576,128]{1,0:T(8,128)(2,1)}, bf16[576,128]{1,0:T(8,128)(2,1)S(1)}, u32[]{:S(2)}, u32[]{:S(2)}) collective-permute-start(bf16[576,128]{1,0:T(8,128)(2,1)} %get-tuple-element.15), channel_id=1, source_target_pairs={{0,24},{8,32},{16,40},{24,48},{32,56},{40,64},{48,72},{56,80},{64,... | collective-permute-start | bytes 442376 | tf_op jit(solution)/shard_map/ppermute | solution.py:31
  153.7 9.4 %collective-permute-start.3 = (bf16[336,128]{1,0:T(8,128)(2,1)}, bf16[336,128]{1,0:T(8,128)(2,1)S(1)}, u32[]{:S(2)}, u32[]{:S(2)}) collective-permute-start(bf16[336,128]{1,0:T(8,128)(2,1)} %get-tuple-element.17), channel_id=1, source_target_pairs={{0,760},{8,0},{16,8},{24,16},{32,24},{40,32},{48,40},{56,48},{64,5... | collective-permute-start | bytes 258056 | tf_op jit(solution)/shard_map/ppermute | solution.py:31
  157.8 6.2 %collective-permute-start.4 = (bf16[336,128]{1,0:T(8,128)(2,1)}, bf16[336,128]{1,0:T(8,128)(2,1)S(1)}, u32[]{:S(2)}, u32[]{:S(2)}) collective-permute-start(bf16[336,128]{1,0:T(8,128)(2,1)} %get-tuple-element.18), channel_id=1, source_target_pairs={{0,752},{8,760},{16,0},{24,8},{32,16},{40,24},{48,32},{56,40},{64,... | collective-permute-start | bytes 258056 | tf_op jit(solution)/shard_map/ppermute | solution.py:31
  161.1 7.5 %collective-permute-start.5 = (bf16[336,128]{1,0:T(8,128)(2,1)}, bf16[336,128]{1,0:T(8,128)(2,1)S(1)}, u32[]{:S(2)}, u32[]{:S(2)}) collective-permute-start(bf16[336,128]{1,0:T(8,128)(2,1)} %get-tuple-element.19), channel_id=1, source_target_pairs={{0,744},{8,752},{16,760},{24,0},{32,8},{40,16},{48,24},{56,32},{64... | collective-permute-start | bytes 258056 | tf_op jit(solution)/shard_map/ppermute | solution.py:31
  163.1 5.6 %copy-start.1 = (bf16[336,128]{1,0:T(8,128)(2,1)}, bf16[336,128]{1,0:T(8,128)(2,1)S(1)}, u32[]{:S(2)}) copy-start(bf16[336,128]{1,0:T(8,128)(2,1)S(1)} %collective-permute-done.3.refs_1_) | copy-start | bytes 258052
  163.9 4.7 %copy-start.2 = (bf16[336,128]{1,0:T(8,128)(2,1)}, bf16[336,128]{1,0:T(8,128)(2,1)S(1)}, u32[]{:S(2)}) copy-start(bf16[336,128]{1,0:T(8,128)(2,1)S(1)} %collective-permute-done.4.refs_2_) | copy-start | bytes 258052
  168.7 0.6 copy-start.3

commit v2 on v1

--- a/solution.py
+++ b/solution.py
@@ -206,7 +206,7 @@
 
 
 def call(kernel, outs, *args):
-    return pl.pallas_call(kernel, out_shape=outs, interpret=INTERPRET)(*args)
+    return pl.pallas_call(kernel, out_shape=outs, interpret=INTERPRET, compiler_params=pltpu.CompilerParams(vmem_limit_bytes=24 * 1024 * 1024))(*args)
 
 
 def body(layer_input, output_grad, gate_weight, up_weight, down_weight, route_offset, gate_fixed):

time: 172 us -> 162 us (0.942)
  Pallas kernels: 14.5 us -> 4.81 us
  other arithmetic: 2.77 us -> 0.67 us
  local copies, waits for them, and re-layouts: 2.86 us -> 4.93 us
    pallas_call x4, Pallas kernels: 14.5 us -> 4.81 us  [call(): pl.pallas_call(kernel, out_shape=outs, interpret=INTERPRET, compiler_para...]
    convert_element_type x1, other arithmetic: 2.66 us -> 0.55 us  [body(): full = lax.all_gather(shard, 'local', axis=0, tiled=True).astype(bf16)]
    unnamed x9 -> x15, local copies, waits for them, and re-layouts: 2.86 us -> 4.93 us
where the time goes in v2:
time: 162 us
  blocking collectives  110 us (68%)
  starting transfers between devices  20.5 us (13%)
  waiting for transfers between devices  19.9 us (12%)
  local copies, waits for them, and re-layouts  4.93 us (3%)
  Pallas kernels  4.81 us (3%)
    all_to_all x1, blocking collectives, body(): shares = lax.all_to_all(partial, 'local', 0, 0, tiled=True)  59.9 us
    all_gather x1, blocking collectives, body(): full = lax.all_gather(shard, 'local', axis=0, tiled=True).astype(bf16)  50.1 us
    ppermute x6, starting transfers between devices, from_behind(): return lax.ppermute(value, axis, pairs)  20.5 us
    ppermute x6, waiting for transfers between devices, from_behind(): return lax.ppermute(value, axis, pairs)  19.9 us
    unnamed x15, local copies, waits for them, and re-layouts  4.93 us
    pallas_call x4, Pallas kernels, call(): pl.pallas_call(kernel, out_shape=outs, interpret=INTERPRET, compiler_para...  4.81 us
  transfers between devices with their start and end apart: 6, of which 5 were waited for; matrix products, arithmetic and copies ran while one was open for 1% of the time, Pallas kernels for 0%

profile of v2, /device:TPU:1, one launch (start us, length us, event | category | flops | bytes accessed | tf_op | source)
XLA Modules:
  0.0 161.6 jit_solution(14824983311711718601)
XLA Ops:
  0.6 0.0 copy-start.2
  0.6 0.9 copy-done.2
  1.5 0.0 copy-start.3
  1.5 0.9 copy-done.3
  2.4 0.0 copy-start.4
  2.4 0.7 copy-done.4
  3.1 0.4 shard_map.86
  3.6 4.5 %collective-permute-start = (bf16[576,128]{1,0:T(8,128)(2,1)S(1)}, bf16[576,128]{1,0:T(8,128)(2,1)S(1)}, u32[]{:S(2)}, u32[]{:S(2)}) collective-permute-start(bf16[576,128]{1,0:T(8,128)(2,1)S(1)} %get-tuple-element.13), channel_id=1, source_target_pairs={{0,8},{8,16},{16,24},{24,32},{32,40},{40,48},{48,56},{56,64},{64,7... | collective-permute-start | bytes 442376 | tf_op jit(solution)/shard_map/ppermute | solution.py:31
  8.1 3.1 %collective-permute-start.1 = (bf16[576,128]{1,0:T(8,128)(2,1)S(1)}, bf16[576,128]{1,0:T(8,128)(2,1)S(1)}, u32[]{:S(2)}, u32[]{:S(2)}) collective-permute-start(bf16[576,128]{1,0:T(8,128)(2,1)S(1)} %get-tuple-element.14), channel_id=1, source_target_pairs={{0,16},{8,24},{16,32},{24,40},{32,48},{40,56},{48,64},{56,72},{64,... | collective-permute-start | bytes 442376 | tf_op jit(solution)/shard_map/ppermute | solution.py:31
  11.2 3.4 %collective-permute-start.2 = (bf16[576,128]{1,0:T(8,128)(2,1)S(1)}, bf16[576,128]{1,0:T(8,128)(2,1)S(1)}, u32[]{:S(2)}, u32[]{:S(2)}) collective-permute-start(bf16[576,128]{1,0:T(8,128)(2,1)S(1)} %get-tuple-element.15), channel_id=1, source_target_pairs={{0,24},{8,32},{16,40},{24,48},{32,56},{40,64},{48,72},{56,80},{64,... | collective-permute-start | bytes 442376 | tf_op jit(solution)/shard_map/ppermute | solution.py:31
  14.6 1.6 copy.9
  16.2 0.6 collective-permute-done
  16.8 9.5 %collective-permute-done.1 = bf16[576,128]{1,0:T(8,128)(2,1)S(1)} collective-permute-done((bf16[576,128]{1,0:T(8,128)(2,1)S(1)}, bf16[576,128]{1,0:T(8,128)(2,1)S(1)}, u32[]{:S(2)}, u32[]{:S(2)}) %collective-permute-start.1) | collective-permute-done | bytes 147488 | tf_op jit(solution)/shard_map/ppermute | solution.py:31
  26.3 4.4 %collective-permute-done.2 = bf16[576,128]{1,0:T(8,128)(2,1)S(1)} collective-permute-done((bf16[576,128]{1,0:T(8,128)(2,1)S(1)}, bf16[576,128]{1,0:T(8,128)(2,1)S(1)}, u32[]{:S(2)}, u32[]{:S(2)}) %collective-permute-start.2) | collective-permute-done | bytes 147488 | tf_op jit(solution)/shard_map/ppermute | solution.py:31
  30.8 0.1 maximum_convert_fusion
  30.9 50.1 %all-gather.1 = f16[18432,128]{1,0:T(8,128)(2,1)S(1)} all-gather(f16[2304,128]{1,0:T(8,128)(2,1)S(1)} %maximum_convert_fusion), channel_id=1, replica_groups=mesh['node'=96,'local'=8] {'local'}, dimensions={0}, use_global_device_ids=true | all-gather | bytes 5308416 | tf_op jit(solution)/shard_map/all_gather | solution.py:223
  81.0 0.0 copy-start
  81.0 0.0 copy-start.1
  81.0 0.5 convert_element_type.7.got_ref
  81.6 0.6 copy-done
  82.2 0.3 copy-done.1
  82.5 3.0 %shard_map.87 = bf16[9088,128]{1,0:T(8,128)(2,1)S(1)} custom-call(bf16[18432,128]{1,0:T(8,128)(2,1)S(1)} %convert_element_type.7.got_ref, bf16[3584,128]{1,0:T(8,128)(2,1)S(1)} %bitcast.16, bf16[3584,128]{1,0:T(8,128)(2,1)S(1)} %bitcast.17, bf16[3584,128]{1,0:T(8,128)(2,1)S(1)} %bitcast.15), custom_call_target="tpu_custom_call" | custom-call | tf_op jit(solution)/shard_map/pallas_call | solution.py:209
  85.4 59.9 %all_to_all.11 = bf16[8,1136,128]{2,1,0:T(8,128)(2,1)S(1)} all-to-all(bf16[8,1136,128]{2,1,0:T(8,128)(2,1)S(1)} %bitcast.14), channel_id=1, replica_groups=mesh['node'=96,'local'=8] {'local'}, dimensions={0} | all-to-all | bytes 4653056 | tf_op jit(solution)/shard_map/all_to_all | solution.py:232
  145.3 0.0 copy-start.5
  145.3 0.0 copy-start.6
  145.3 0.3 shard_map.88
  145.6 4.1 %collective-permute-start.3 = (bf16[336,128]{1,0:T(8,128)(2,1)S(1)}, bf16[336,128]{1,0:T(8,128)(2,1)S(1)}, u32[]{:S(2)}, u32[]{:S(2)}) collective-permute-start(bf16[336,128]{1,0:T(8,128)(2,1)S(1)} %get-tuple-element.17), channel_id=1, source_target_pairs={{0,760},{8,0},{16,8},{24,16},{32,24},{40,32},{48,40},{56,48},{64,5... | collective-permute-start | bytes 258056 | tf_op jit(solution)/shard_map/ppermute | solution.py:31
  149.8 3.4 %collective-permute-start.4 = (bf16[336,128]{1,0:T(8,128)(2,1)S(1)}, bf16[336,128]{1,0:T(8,128)(2,1)S(1)}, u32[]{:S(2)}, u32[]{:S(2)}) collective-permute-start(bf16[336,128]{1,0:T(8,128)(2,1)S(1)} %get-tuple-element.18), channel_id=1, source_target_pairs={{0,752},{8,760},{16,0},{24,8},{32,16},{40,24},{48,32},{56,40},{64,... | collective-permute-start | bytes 258056 | tf_op jit(solution)/shard_map/ppermute | solution.py:31
  153.2 1.9 %collective-permute-start.5 = (bf16[336,128]{1,0:T(8,128)(2,1)S(1)}, bf16[336,128]{1,0:T(8,128)(2,1)S(1)}, u32[]{:S(2)}, u32[]{:S(2)}) collective-permute-start(bf16[336,128]{1,0:T(8,128)(2,1)S(1)} %get-tuple-element.19), channel_id=1, source_target_pairs={{0,744},{8,752},{16,760},{24,0},{32,8},{40,16},{48,24},{56,32},{64... | collective-permute-start | bytes 258056 | tf_op jit(solution)/shard_map/ppermute | solution.py:31
  155.1 0.0 collective-permute-done.3.refs_1_
  155.1 0.6 collective-permute-done.4.refs_2_
  155.7 4.7 %collective-permute-done.5.refs_3_ = bf16[336,128]{1,0:T(8,128)(2,1)S(1)} collective-permute-done((bf16[336,128]{1,0:T(8,128)(2,1)S(1)}, bf16[336,128]{1,0:T(8,128)(2,1)S(1)}, u32[]{:S(2)}, u32[]{:S(2)}) %collective-permute-start.5) | collective-permute-done | bytes 86048 | tf_op jit(solution)/shard_map/ppermute | solution.py:31
  160.5 0.0 copy-done.5
  160.5 0.0 copy-done.6
  160.5 1.1 shard_map.89
Async XLA Ops:
  0.6 0.9 copy-start.2
  1.5 0.9 copy-start.3
  2.4 0.7 copy-start.4
  3.6 13.2 %collective-permute-start = (bf16[576,128]{1,0:T(8,128)(2,1)S(1)}, bf16[576,128]{1,0:T(8,128)(2,1)S(1)}, u32[]{:S(2)}, u32[]{:S(2)}) collective-permute-start(bf16[576,128]{1,0:T(8,128)(2,1)S(1)} %get-tuple-element.13), channel_id=1, source_target_pairs={{0,8},{8,16},{16,24},{24,32},{32,40},{40,48},{48,56},{56,64},{64,7... | collective-permute-start | bytes 442376 | tf_op jit(solution)/shard_map/ppermute | solution.py:31
  8.1 18.3 %collective-permute-start.1 = (bf16[576,128]{1,0:T(8,128)(2,1)S(1)}, bf16[576,128]{1,0:T(8,128)(2,1)S(1)}, u32[]{:S(2)}, u32[]{:S(2)}) collective-permute-start(bf16[576,128]{1,0:T(8,128)(2,1)S(1)} %get-tuple-element.14), channel_id=1, source_target_pairs={{0,16},{8,24},{16,32},{24,40},{32,48},{40,56},{48,64},{56,72},{64,... | collective-permute-start | bytes 442376 | tf_op jit(solution)/shard_map/ppermute | solution.py:31
  11.2 19.6 %collective-permute-start.2 = (bf16[576,128]{1,0:T(8,128)(2,1)S(1)}, bf16[576,128]{1,0:T(8,128)(2,1)S(1)}, u32[]{:S(2)}, u32[]{:S(2)}) collective-permute-start(bf16[576,128]{1,0:T(8,128)(2,1)S(1)} %get-tuple-element.15), channel_id=1, source_target_pairs={{0,24},{8,32},{16,40},{24,48},{32,56},{40,64},{48,72},{56,80},{64,... | collective-permute-start | bytes 442376 | tf_op jit(solution)/shard_map/ppermute | solution.py:31
  81.0 1.2 copy-start
  81.0 1.5 copy-start.1
  145.3 15.1 %copy-start.5 = (s32[128,2]{0,1:T(2,128)S(1)}, s32[128,2]{0,1:T(2,128)}, u32[]{:S(2)}) copy-start(s32[128,2]{0,1:T(2,128)} %param.12) | copy-start | bytes 3076
  145.3 15.1 %copy-start.6 = (s32[128,2]{0,1:T(2,128)S(1)}, s32[128,2]{0,1:T(2,128)}, u32[]{:S(2)}) copy-start(s32[128,2]{0,1:T(2,128)} %param.13) | copy-start | bytes 3076
  145.6 9.5 %collective-permute-start.3 = (bf16[336,128]{1,0:T(8,128)(2,1)S(1)}, bf16[336,128]{1,0:T(8,128)(2,1)S(1)}, u32[]{:S(2)}, u32[]{:S(2)}) collective-permute-start(bf16[336,128]{1,0:T(8,128)(2,1)S(1)} %get-tuple-element.17), channel_id=1, source_target_pairs={{0,760},{8,0},{16,8},{24,16},{32,24},{40,32},{48,40},{56,48},{64,5... | collective-permute-start | bytes 258056 | tf_op jit(solution)/shard_map/ppermute | solution.py:31
  149.8 6.0 %collective-permute-start.4 = (bf16[336,128]{1,0:T(8,128)(2,1)S(1)}, bf16[336,128]{1,0:T(8,128)(2,1)S(1)}, u32[]{:S(2)}, u32[]{:S(2)}) collective-permute-start(bf16[336,128]{1,0:T(8,128)(2,1)S(1)} %get-tuple-element.18), channel_id=1, source_target_pairs={{0,752},{8,760},{16,0},{24,8},{32,16},{40,24},{48,32},{56,40},{64,... | collective-permute-start | bytes 258056 | tf_op jit(solution)/shard_map/ppermute | solution.py:31
  153.2 7.3 %collective-permute-start.5 = (bf16[336,128]{1,0:T(8,128)(2,1)S(1)}, bf16[336,128]{1,0:T(8,128)(2,1)S(1)}, u32[]{:S(2)}, u32[]{:S(2)}) collective-permute-start(bf16[336,128]{1,0:T(8,128)(2,1)S(1)} %get-tuple-element.19), channel_id=1, source_target_pairs={{0,744},{8,752},{16,760},{24,0},{32,8},{40,16},{48,24},{56,32},{64... | collective-permute-start | bytes 258056 | tf_op jit(solution)/shard_map/ppermute | solution.py:31

commit v3 on v2

--- a/solution.py
+++ b/solution.py
@@ -14,9 +14,12 @@
 LOCAL = 8
 ROUTED = GROUP * CAP
 OUT_ROWS = 7 * CAP + 16
-PART_ROWS = 3 * ROUTED + 2 * CAP + 16
+HIDE_ROWS = 2 * ROUTED + 16
 HOME_ROWS = 4 * CAP + 16
 LEVELS = 15
+TOKEN_CEILING = 3
+HIDDEN_CEILING = 24
+GATE_CEILING = 44
 INTERPRET = False
 
 f32 = jnp.float32
@@ -46,31 +49,36 @@
     ]
 
 
-def level_of(top):
+def level_of(top, ceiling):
     level = jnp.zeros_like(top)
     for step in range(1, LEVELS):
-        level = level + jnp.where(top < 2.0 ** (3 - 8 * step), 1.0, 0.0)
+        level = level + jnp.where(top < 2.0 ** (ceiling - 8 * step), 1.0, 0.0)
     return level
 
 
-def power_of(level, sign):
-    power = jnp.full_like(level, 2.0 ** (sign * 12))
+def power_of(level, ceiling, sign):
+    base = 15 - ceiling
+    power = jnp.full_like(level, 2.0 ** (sign * base))
     for step in range(1, LEVELS):
-        power = jnp.where(level > step - 0.5, 2.0 ** (sign * (12 + 8 * step)), power)
+        power = jnp.where(level > step - 0.5, 2.0 ** (sign * (base + 8 * step)), power)
     return power
 
 
-def scaled(values):
+def level_for(wide, ceiling):
+    top = jnp.max(jnp.max(jnp.abs(wide), axis=0, keepdims=True), axis=1, keepdims=True)
+    return level_of(jnp.broadcast_to(top, (1, LANE)), ceiling)
+
+
+def scaled(values, ceiling):
     wide = values.astype(f32)
-    top = jnp.max(jnp.max(jnp.abs(wide), axis=0, keepdims=True), axis=1, keepdims=True)
-    level = level_of(jnp.broadcast_to(top, (1, TOK)))
-    return (wide * power_of(level, 1)).astype(bf16), level
+    level = level_for(wide, ceiling)
+    return (wide * power_of(level, ceiling, 1)).astype(bf16), level
 
 
 def pack_kernel(route_ref, in_ref, grad_ref, *out_refs):
     table = jnp.concatenate(tables(route_ref[...]), axis=0)
-    rows_in, level_in = scaled(in_ref[...])
-    rows_grad, level_grad = scaled(grad_ref[...])
+    rows_in, level_in = scaled(in_ref[...], TOKEN_CEILING)
+    rows_grad, level_grad = scaled(grad_ref[...], TOKEN_CEILING)
     tail = jnp.concatenate([rows_in[384:448], rows_grad[384:448]], axis=0)
     parts = [rows_in[0:128], rows_in[128:256], rows_in[256:384]]
     parts += [rows_grad[0:128], rows_grad[128:256], rows_grad[256:384], tail]
@@ -84,7 +92,7 @@
         out_refs[o][7 * CAP : OUT_ROWS, :] = levels
 
 
-def expert_kernel(got_ref, gate_ref, up_ref, down_ref, out_ref):
+def hidden_kernel(got_ref, gate_ref, up_ref, down_ref, out_ref):
     zero_cols = jnp.zeros((64, 2 * HID), bf16)
     zero_half = jnp.zeros((64, HID), bf16)
     pre = jnp.zeros((ROUTED, 2 * HID), f32)
@@ -117,8 +125,8 @@
         for o in range(GROUP):
             start = d * GROUP * OUT_ROWS + o * OUT_ROWS + 7 * CAP
             levels = got_ref[start : start + 16, :].astype(f32)
-            inverse_in = power_of(levels[0:1], -1)
-            inverse_grad = power_of(levels[1:2], -1)
+            inverse_in = power_of(levels[0:1], TOKEN_CEILING, -1)
+            inverse_grad = power_of(levels[1:2], TOKEN_CEILING, -1)
             back_in.append(part[o * CAP : (o + 1) * CAP] * jnp.concatenate([inverse_in, inverse_in], axis=1))
             back_grad.append(part_grad[o * CAP : (o + 1) * CAP] * inverse_grad)
         pre = pre + jnp.concatenate(back_in, axis=0)
@@ -128,53 +136,60 @@
     sigmoid = jax.nn.sigmoid(gate_pre)
     swish = gate_pre * sigmoid
     product = swish * up_pre * grad
-    up_grad = (grad * swish).astype(bf16)
-    pre_grad = (grad * up_pre * sigmoid * (1.0 + gate_pre * (1.0 - sigmoid))).astype(bf16)
-    hidden = jnp.concatenate([pre_grad, up_grad], axis=1)
-    paired = jnp.concatenate([hidden[0 : 2 * CAP], hidden[2 * CAP : 4 * CAP]], axis=1)
-    line = lax.broadcasted_iota(jnp.int32, (16, LANE), 0)
-    gate_rows = jnp.zeros((16, LANE), f32)
+    up_grad, level_up = scaled((grad * swish).astype(bf16), HIDDEN_CEILING)
+    pre_grad, level_pre = scaled(
+        (grad * up_pre * sigmoid * (1.0 + gate_pre * (1.0 - sigmoid))).astype(bf16), HIDDEN_CEILING
+    )
+    totals = []
     for o in range(GROUP):
         piece = jnp.concatenate([product[o * CAP : (o + 1) * CAP], jnp.zeros((LANE - CAP, HID), f32)], axis=0)
         total = lax.dot_general(
             jnp.ones((8, HID), f32), piece, NT, preferred_element_type=f32, precision=lax.Precision.HIGHEST
-        )[0:1]
+        )
+        totals.append(total[0:1])
+    level_gate = level_for(jnp.concatenate(totals, axis=0), GATE_CEILING)
+    power_gate = power_of(level_gate, GATE_CEILING, 1)
+    line = lax.broadcasted_iota(jnp.int32, (16, LANE), 0)
+    rows = jnp.where(line == 8, level_pre, jnp.where(line == 9, level_up, jnp.where(line == 10, level_gate, 0.0)))
+    for o in range(GROUP):
+        total = totals[o] * power_gate
         high = total.astype(bf16).astype(f32)
-        gate_rows = jnp.where(line == 2 * o, high, gate_rows)
-        gate_rows = jnp.where(line == 2 * o + 1, total - high, gate_rows)
-    gate_rows = gate_rows.astype(bf16)
+        rows = jnp.where(line == 2 * o, high, jnp.where(line == 2 * o + 1, total - high, rows))
+    out_ref[0:ROUTED, :] = pre_grad
+    out_ref[ROUTED : 2 * ROUTED, :] = up_grad
+    out_ref[2 * ROUTED : HIDE_ROWS, :] = rows.astype(bf16)
+
+
+def back_kernel(got_ref, gate_ref, up_ref, *out_refs):
+    zero_cols = jnp.zeros((64, 2 * HID), bf16)
+    head = jnp.zeros((ROUTED, 384), f32)
+    tail = jnp.zeros((2 * CAP, LANE), f32)
+    gates = jnp.zeros((16, LANE), f32)
     for d in range(LOCAL):
+        base = d * HIDE_ROWS
+        rows = got_ref[base + 2 * ROUTED : base + HIDE_ROWS, :].astype(f32)
+        inverse_pre = power_of(rows[8:9], HIDDEN_CEILING, -1)
+        inverse_up = power_of(rows[9:10], HIDDEN_CEILING, -1)
+        gates = gates + rows * power_of(rows[10:11], GATE_CEILING, -1)
+        pre_grad = (got_ref[base : base + ROUTED, :].astype(f32) * inverse_pre).astype(bf16)
+        up_grad = (got_ref[base + ROUTED : base + 2 * ROUTED, :].astype(f32) * inverse_up).astype(bf16)
+        hidden = jnp.concatenate([pre_grad, up_grad], axis=1)
+        paired = jnp.concatenate([hidden[0 : 2 * CAP], hidden[2 * CAP : 4 * CAP]], axis=1)
         low = d * FEAT
-        base = d * PART_ROWS
         both = jnp.concatenate([gate_ref[low : low + FEAT, :], up_ref[low : low + FEAT, :]], axis=1)
-        wide = lax.dot_general(hidden, both[0:384], NT, preferred_element_type=f32).astype(bf16)
-        for j in range(3):
-            out_ref[base + j * ROUTED : base + (j + 1) * ROUTED, :] = wide[:, j * LANE : (j + 1) * LANE]
+        head = head + lax.dot_general(hidden, both[0:384], NT, preferred_element_type=f32)
         corner = jnp.concatenate([both[384:448], zero_cols], axis=1)
         other = jnp.concatenate([zero_cols, both[384:448]], axis=1)
         ends = jnp.concatenate([corner, other], axis=0)
-        tail = lax.dot_general(paired, ends, NT, preferred_element_type=f32).astype(bf16)
-        out_ref[base + 3 * ROUTED : base + 3 * ROUTED + 2 * CAP, :] = tail
-        out_ref[base + 3 * ROUTED + 2 * CAP : base + PART_ROWS, :] = gate_rows
-
-
-def sum_kernel(part_ref, *out_refs):
-    def total(start, rows):
-        value = part_ref[start : start + rows, :].astype(f32)
-        for d in range(1, LOCAL):
-            value = value + part_ref[d * PART_ROWS + start : d * PART_ROWS + start + rows, :].astype(f32)
-        return value
-
-    for j in range(3):
-        for o in range(GROUP):
-            out_refs[o][j * CAP : (j + 1) * CAP, :] = total(j * ROUTED + o * CAP, CAP).astype(bf16)
-    for half in range(2):
-        tail = total(3 * ROUTED + half * CAP, CAP).astype(bf16)
-        out_refs[half][3 * CAP : 4 * CAP, :] = tail
-        out_refs[half + 2][3 * CAP : 4 * CAP, :] = tail
-    gates = total(3 * ROUTED + 2 * CAP, 16)
+        tail = tail + lax.dot_general(paired, ends, NT, preferred_element_type=f32)
+    head = head.astype(bf16)
+    tail = tail.astype(bf16)
     line = lax.broadcasted_iota(jnp.int32, (16, LANE), 0)
     for o in range(GROUP):
+        for j in range(3):
+            out_refs[o][j * CAP : (j + 1) * CAP, :] = head[o * CAP : (o + 1) * CAP, j * LANE : (j + 1) * LANE]
+        half = o % 2
+        out_refs[o][3 * CAP : 4 * CAP, :] = tail[half * CAP : (half + 1) * CAP]
         gate = gates[2 * o : 2 * o + 1] + gates[2 * o + 1 : 2 * o + 2]
         high = gate.astype(bf16).astype(f32)
         rows = jnp.where(line == 0, high, jnp.where(line == 1, gate - high, 0.0))
@@ -211,6 +226,8 @@
 
 def body(layer_input, output_grad, gate_weight, up_weight, down_weight, route_offset, gate_fixed):
     route = route_offset.T
+    gate_rows = lax.all_to_all(gate_weight[0], "local", 0, 0, tiled=True)
+    up_rows = lax.all_to_all(up_weight[0], "local", 0, 0, tiled=True)
     packed = call(
         pack_kernel,
         [jax.ShapeDtypeStruct((OUT_ROWS, LANE), bf16)] * GROUP,
@@ -221,16 +238,18 @@
     got = [packed[0]] + [from_behind(packed[o], "node", o) for o in range(1, GROUP)]
     shard = jnp.concatenate(got, axis=0).astype(jnp.float16)
     full = lax.all_gather(shard, "local", axis=0, tiled=True).astype(bf16)
-    partial = call(
-        expert_kernel,
-        jax.ShapeDtypeStruct((LOCAL * PART_ROWS, LANE), bf16),
+    hidden = call(
+        hidden_kernel,
+        jax.ShapeDtypeStruct((HIDE_ROWS, LANE), bf16),
         full,
         gate_weight[0],
         up_weight[0],
         down_weight[0].T,
     )
-    shares = lax.all_to_all(partial, "local", 0, 0, tiled=True)
-    summed = call(sum_kernel, [jax.ShapeDtypeStruct((HOME_ROWS, LANE), bf16)] * GROUP, shares)
+    spread = lax.all_gather(hidden.astype(jnp.float16), "local", axis=0, tiled=True).astype(bf16)
+    summed = call(
+        back_kernel, [jax.ShapeDtypeStruct((HOME_ROWS, LANE), bf16)] * GROUP, spread, gate_rows, up_rows
+    )
     home = [summed[0]] + [from_behind(summed[o], "node", -o) for o in range(1, GROUP)]
     input_grad, gate_grad = call(
         unpack_kernel,

time: 162 us -> 167 us (1.031)
  starting transfers between devices: 20.5 us -> 47.4 us
  blocking collectives: 110 us -> 89.7 us
  local copies, waits for them, and re-layouts: 4.93 us -> 2.2 us
    all_to_all x1 -> x0, blocking collectives: 59.9 us -> none  [body(): shares = lax.all_to_all(partial, 'local', 0, 0, tiled=True)]
    all_gather x0 -> x1, blocking collectives: none -> 22.7 us  [body(): lax.all_gather(hidden.astype(jnp.float16), 'local', axis=0, tiled=True)]
    all_gather x1, blocking collectives: 50.1 us -> 67 us  [body(): full = lax.all_gather(shard, 'local', axis=0, tiled=True).astype(bf16)]
    all_to_all x0 -> x2, starting transfers between devices: none -> 14.6 us  [the longest x1 7.78 us: body(): up_rows = lax.all_to_all(up_weight[0], 'local', 0, 0, tiled=True)]
    ppermute x6, starting transfers between devices: 20.5 us -> 32.8 us  [from_behind(): return lax.ppermute(value, axis, pairs)]
    unnamed x15 -> x11, local copies, waits for them, and re-layouts: 4.93 us -> 2.2 us
  transfers between devices with their start and end apart: 6 -> 8, of which waited for: 5 -> 3; matrix products, arithmetic and copies ran while one was open for 1% -> 2% of each run, Pallas kernels for 0% -> 2%
where the time goes in v3:
time: 167 us
  blocking collectives  89.7 us (54%)
  starting transfers between devices  47.4 us (28%)
  waiting for transfers between devices  19.2 us (11%)
  Pallas kernels  5.94 us (4%)
  local copies, waits for them, and re-layouts  2.2 us (1%)
  other arithmetic  1.68 us (1%)
    all_gather x1, blocking collectives, body(): full = lax.all_gather(shard, 'local', axis=0, tiled=True).astype(bf16)  67 us
    ppermute x6, starting transfers between devices, from_behind(): return lax.ppermute(value, axis, pairs)  32.8 us
    all_gather x1, blocking collectives, body(): lax.all_gather(hidden.astype(jnp.float16), 'local', axis=0, tiled=True)  22.7 us
    ppermute x6, waiting for transfers between devices, from_behind(): return lax.ppermute(value, axis, pairs)  19.2 us
    all_to_all x1, starting transfers between devices, body(): up_rows = lax.all_to_all(up_weight[0], 'local', 0, 0, tiled=True)  7.78 us
    all_to_all x1, starting transfers between devices, body(): gate_rows = lax.all_to_all(gate_weight[0], 'local', 0, 0, tiled=True)  6.83 us
    pallas_call x4, Pallas kernels, call(): pl.pallas_call(kernel, out_shape=outs, interpret=INTERPRET, compiler_para...  5.94 us
  transfers between devices with their start and end apart: 8, of which 3 were waited for; matrix products, arithmetic and copies ran while one was open for 2% of the time, Pallas kernels for 2%

profile of v3, /device:TPU:1, one launch (start us, length us, event | category | flops | bytes accessed | tf_op | source)
XLA Modules:
  0.0 166.9 jit_solution(8098352816190237566)
XLA Ops:
  0.6 0.0 copy-start.3
  0.6 0.0 copy-start.1
  0.6 0.0 copy-start.2
  0.7 7.8 %all-to-all-start.1 = ((bf16[8,448,128]{2,1,0:T(8,128)(2,1)}), bf16[8,448,128]{2,1,0:T(8,128)(2,1)S(1)}, u32[]{:S(2)}, u32[]{:S(2)}) async-start(bf16[8,448,128]{2,1,0:T(8,128)(2,1)} %bitcast.15), calls=%async_computation.1 | async-start | bytes 1835008 | tf_op jit(solution)/shard_map/all_to_all | solution.py:230
  8.4 0.0 copy-done.3
  8.4 0.0 copy-done.1
  8.5 0.0 copy-done.2
  8.5 0.5 shard_map.86
  8.9 4.0 %collective-permute-start = (bf16[576,128]{1,0:T(8,128)(2,1)S(1)}, bf16[576,128]{1,0:T(8,128)(2,1)S(1)}, u32[]{:S(2)}, u32[]{:S(2)}) collective-permute-start(bf16[576,128]{1,0:T(8,128)(2,1)S(1)} %get-tuple-element.13), channel_id=1, source_target_pairs={{0,8},{8,16},{16,24},{24,32},{32,40},{40,48},{48,56},{56,64},{64,7... | collective-permute-start | bytes 442376 | tf_op jit(solution)/shard_map/ppermute | solution.py:34
  12.9 3.1 %collective-permute-start.1 = (bf16[576,128]{1,0:T(8,128)(2,1)S(1)}, bf16[576,128]{1,0:T(8,128)(2,1)S(1)}, u32[]{:S(2)}, u32[]{:S(2)}) collective-permute-start(bf16[576,128]{1,0:T(8,128)(2,1)S(1)} %get-tuple-element.14), channel_id=1, source_target_pairs={{0,16},{8,24},{16,32},{24,40},{32,48},{40,56},{48,64},{56,72},{64,... | collective-permute-start | bytes 442376 | tf_op jit(solution)/shard_map/ppermute | solution.py:34
  16.0 3.4 %collective-permute-start.2 = (bf16[576,128]{1,0:T(8,128)(2,1)S(1)}, bf16[576,128]{1,0:T(8,128)(2,1)S(1)}, u32[]{:S(2)}, u32[]{:S(2)}) collective-permute-start(bf16[576,128]{1,0:T(8,128)(2,1)S(1)} %get-tuple-element.15), channel_id=1, source_target_pairs={{0,24},{8,32},{16,40},{24,48},{32,56},{40,64},{48,72},{56,80},{64,... | collective-permute-start | bytes 442376 | tf_op jit(solution)/shard_map/ppermute | solution.py:34
  19.5 1.6 copy.9
  21.0 0.0 collective-permute-done
  21.0 9.6 %collective-permute-done.1 = bf16[576,128]{1,0:T(8,128)(2,1)S(1)} collective-permute-done((bf16[576,128]{1,0:T(8,128)(2,1)S(1)}, bf16[576,128]{1,0:T(8,128)(2,1)S(1)}, u32[]{:S(2)}, u32[]{:S(2)}) %collective-permute-start.1) | collective-permute-done | bytes 147488 | tf_op jit(solution)/shard_map/ppermute | solution.py:34
  30.6 5.0 %collective-permute-done.2 = bf16[576,128]{1,0:T(8,128)(2,1)S(1)} collective-permute-done((bf16[576,128]{1,0:T(8,128)(2,1)S(1)}, bf16[576,128]{1,0:T(8,128)(2,1)S(1)}, u32[]{:S(2)}, u32[]{:S(2)}) %collective-permute-start.2) | collective-permute-done | bytes 147488 | tf_op jit(solution)/shard_map/ppermute | solution.py:34
  35.6 0.9 maximum_convert_fusion
  36.5 0.0 all-to-all-done.1
  36.5 6.8 %all-to-all-start = ((bf16[8,448,128]{2,1,0:T(8,128)(2,1)}), bf16[8,448,128]{2,1,0:T(8,128)(2,1)S(1)}, u32[]{:S(2)}, u32[]{:S(2)}) async-start(bf16[8,448,128]{2,1,0:T(8,128)(2,1)} %bitcast.8), calls=%async_computation | async-start | bytes 1835008 | tf_op jit(solution)/shard_map/all_to_all | solution.py:229
  43.4 67.0 %all-gather.2 = f16[18432,128]{1,0:T(8,128)(2,1)S(1)} all-gather(f16[2304,128]{1,0:T(8,128)(2,1)} %maximum_convert_fusion), channel_id=1, replica_groups=mesh['node'=96,'local'=8] {'local'}, dimensions={0}, use_global_device_ids=true | all-gather | bytes 5308416 | tf_op jit(solution)/shard_map/all_gather | solution.py:240
  110.4 0.0 copy-start
  110.4 0.6 convert_element_type.13.got_ref
  110.9 0.6 copy-done
  111.6 3.2 %shard_map.87 = bf16[656,128]{1,0:T(8,128)(2,1)S(1)} custom-call(bf16[18432,128]{1,0:T(8,128)(2,1)S(1)} %convert_element_type.13.got_ref, bf16[3584,128]{1,0:T(8,128)(2,1)} %bitcast.4.gate_ref, bf16[3584,128]{1,0:T(8,128)(2,1)S(1)} %bitcast.16, bf16[3584,128]{1,0:T(8,128)(2,1)S(1)} %bitcast.17), custom_call_target="tpu_custom_call" | custom-call | tf_op jit(solution)/shard_map/pallas_call | solution.py:224
  114.8 22.7 %all-gather.3 = f16[5248,128]{1,0:T(8,128)(2,1)S(1)} all-gather(f16[656,128]{1,0:T(8,128)(2,1)S(1)} %convert_element_type.14), channel_id=1, replica_groups=mesh['node'=96,'local'=8] {'local'}, dimensions={0}, use_global_device_ids=true | all-gather | bytes 1511424 | tf_op jit(solution)/shard_map/all_gather | solution.py:249
  137.5 0.1 convert_element_type.15.got_ref
  137.6 0.0 all-to-all-done
  137.7 0.0 copy-start.4
  137.7 1.2 shard_map.88
  138.8 8.2 %collective-permute-start.3 = (bf16[336,128]{1,0:T(8,128)(2,1)S(1)}, bf16[336,128]{1,0:T(8,128)(2,1)S(1)}, u32[]{:S(2)}, u32[]{:S(2)}) collective-permute-start(bf16[336,128]{1,0:T(8,128)(2,1)S(1)} %get-tuple-element.17), channel_id=1, source_target_pairs={{0,760},{8,0},{16,8},{24,16},{32,24},{40,32},{48,40},{56,48},{64,5... | collective-permute-start | bytes 258056 | tf_op jit(solution)/shard_map/ppermute | solution.py:34
  147.0 11.4 %collective-permute-start.4 = (bf16[336,128]{1,0:T(8,128)(2,1)S(1)}, bf16[336,128]{1,0:T(8,128)(2,1)S(1)}, u32[]{:S(2)}, u32[]{:S(2)}) collective-permute-start(bf16[336,128]{1,0:T(8,128)(2,1)S(1)} %get-tuple-element.18), channel_id=1, source_target_pairs={{0,752},{8,760},{16,0},{24,8},{32,16},{40,24},{48,32},{56,40},{64,... | collective-permute-start | bytes 258056 | tf_op jit(solution)/shard_map/ppermute | solution.py:34
  158.5 2.6 %collective-permute-start.5 = (bf16[336,128]{1,0:T(8,128)(2,1)S(1)}, bf16[336,128]{1,0:T(8,128)(2,1)S(1)}, u32[]{:S(2)}, u32[]{:S(2)}) collective-permute-start(bf16[336,128]{1,0:T(8,128)(2,1)S(1)} %get-tuple-element.19), channel_id=1, source_target_pairs={{0,744},{8,752},{16,760},{24,0},{32,8},{40,16},{48,24},{56,32},{64... | collective-permute-start | bytes 258056 | tf_op jit(solution)/shard_map/ppermute | solution.py:34
  161.1 0.0 collective-permute-done.3.refs_1_
  161.1 0.0 collective-permute-done.4.refs_2_
  161.1 4.6 %collective-permute-done.5.refs_3_ = bf16[336,128]{1,0:T(8,128)(2,1)S(1)} collective-permute-done((bf16[336,128]{1,0:T(8,128)(2,1)S(1)}, bf16[336,128]{1,0:T(8,128)(2,1)S(1)}, u32[]{:S(2)}, u32[]{:S(2)}) %collective-permute-start.5) | collective-permute-done | bytes 86048 | tf_op jit(solution)/shard_map/ppermute | solution.py:34
  165.8 0.0 copy-done.4
  165.8 1.1 shard_map.89
  (1 shorter events, 0.0 us)
Async XLA Ops:
  0.6 7.8 %copy-start.3 = (s32[128,2]{0,1:T(2,128)S(1)}, s32[128,2]{0,1:T(2,128)}, u32[]{:S(2)}) copy-start(s32[128,2]{0,1:T(2,128)} %param.12) | copy-start | bytes 3076
  0.6 7.8 %copy-start.1 = (bf16[128,448]{0,1:T(8,128)(2,1)S(1)}, bf16[128,448]{0,1:T(8,128)(2,1)}, u32[]{:S(2)}) copy-start(bf16[128,448]{0,1:T(8,128)(2,1)} %param.7) | copy-start | bytes 344068
  0.6 7.8 %copy-start.2 = (bf16[128,448]{0,1:T(8,128)(2,1)S(1)}, bf16[128,448]{0,1:T(8,128)(2,1)}, u32[]{:S(2)}) copy-start(bf16[128,448]{0,1:T(8,128)(2,1)} %param.8) | copy-start | bytes 344068
  0.7 35.9 %all-to-all-start.1 = ((bf16[8,448,128]{2,1,0:T(8,128)(2,1)}), bf16[8,448,128]{2,1,0:T(8,128)(2,1)S(1)}, u32[]{:S(2)}, u32[]{:S(2)}) async-start(bf16[8,448,128]{2,1,0:T(8,128)(2,1)} %bitcast.15), calls=%async_computation.1 | async-start | bytes 1835008 | tf_op jit(solution)/shard_map/all_to_all | solution.py:230
  8.9 12.1 %collective-permute-start = (bf16[576,128]{1,0:T(8,128)(2,1)S(1)}, bf16[576,128]{1,0:T(8,128)(2,1)S(1)}, u32[]{:S(2)}, u32[]{:S(2)}) collective-permute-start(bf16[576,128]{1,0:T(8,128)(2,1)S(1)} %get-tuple-element.13), channel_id=1, source_target_pairs={{0,8},{8,16},{16,24},{24,32},{32,40},{40,48},{48,56},{56,64},{64,7... | collective-permute-start | bytes 442376 | tf_op jit(solution)/shard_map/ppermute | solution.py:34
  12.9 17.7 %collective-permute-start.1 = (bf16[576,128]{1,0:T(8,128)(2,1)S(1)}, bf16[576,128]{1,0:T(8,128)(2,1)S(1)}, u32[]{:S(2)}, u32[]{:S(2)}) collective-permute-start(bf16[576,128]{1,0:T(8,128)(2,1)S(1)} %get-tuple-element.14), channel_id=1, source_target_pairs={{0,16},{8,24},{16,32},{24,40},{32,48},{40,56},{48,64},{56,72},{64,... | collective-permute-start | bytes 442376 | tf_op jit(solution)/shard_map/ppermute | solution.py:34
  16.0 19.6 %collective-permute-start.2 = (bf16[576,128]{1,0:T(8,128)(2,1)S(1)}, bf16[576,128]{1,0:T(8,128)(2,1)S(1)}, u32[]{:S(2)}, u32[]{:S(2)}) collective-permute-start(bf16[576,128]{1,0:T(8,128)(2,1)S(1)} %get-tuple-element.15), channel_id=1, source_target_pairs={{0,24},{8,32},{16,40},{24,48},{32,56},{40,64},{48,72},{56,80},{64,... | collective-permute-start | bytes 442376 | tf_op jit(solution)/shard_map/ppermute | solution.py:34
  36.5 101.1 %all-to-all-start = ((bf16[8,448,128]{2,1,0:T(8,128)(2,1)}), bf16[8,448,128]{2,1,0:T(8,128)(2,1)S(1)}, u32[]{:S(2)}, u32[]{:S(2)}) async-start(bf16[8,448,128]{2,1,0:T(8,128)(2,1)} %bitcast.8), calls=%async_computation | async-start | bytes 1835008 | tf_op jit(solution)/shard_map/all_to_all | solution.py:229
  110.4 1.2 copy-start
  137.7 28.1 %copy-start.4 = (s32[128,2]{0,1:T(2,128)S(1)}, s32[128,2]{0,1:T(2,128)}, u32[]{:S(2)}) copy-start(s32[128,2]{0,1:T(2,128)} %param.13) | copy-start | bytes 3076
  138.8 22.3 %collective-permute-start.3 = (bf16[336,128]{1,0:T(8,128)(2,1)S(1)}, bf16[336,128]{1,0:T(8,128)(2,1)S(1)}, u32[]{:S(2)}, u32[]{:S(2)}) collective-permute-start(bf16[336,128]{1,0:T(8,128)(2,1)S(1)} %get-tuple-element.17), channel_id=1, source_target_pairs={{0,760},{8,0},{16,8},{24,16},{32,24},{40,32},{48,40},{56,48},{64,5... | collective-permute-start | bytes 258056 | tf_op jit(solution)/shard_map/ppermute | solution.py:34
  147.0 14.1 %collective-permute-start.4 = (bf16[336,128]{1,0:T(8,128)(2,1)S(1)}, bf16[336,128]{1,0:T(8,128)(2,1)S(1)}, u32[]{:S(2)}, u32[]{:S(2)}) collective-permute-start(bf16[336,128]{1,0:T(8,128)(2,1)S(1)} %get-tuple-element.18), channel_id=1, source_target_pairs={{0,752},{8,760},{16,0},{24,8},{32,16},{40,24},{48,32},{56,40},{64,... | collective-permute-start | bytes 258056 | tf_op jit(solution)/shard_map/ppermute | solution.py:34
  158.5 7.3 %collective-permute-start.5 = (bf16[336,128]{1,0:T(8,128)(2,1)S(1)}, bf16[336,128]{1,0:T(8,128)(2,1)S(1)}, u32[]{:S(2)}, u32[]{:S(2)}) collective-permute-start(bf16[336,128]{1,0:T(8,128)(2,1)S(1)} %get-tuple-element.19), channel_id=1, source_target_pairs={{0,744},{8,752},{16,760},{24,0},{32,8},{40,16},{48,24},{56,32},{64... | collective-permute-start | bytes 258056 | tf_op jit(solution)/shard_map/ppermute | solution.py:34

commit v4 on v3

--- a/solution.py
+++ b/solution.py
@@ -16,6 +16,7 @@
 OUT_ROWS = 7 * CAP + 16
 HIDE_ROWS = 2 * ROUTED + 16
 HOME_ROWS = 4 * CAP + 16
+PAIR_ROWS = 2 * FEAT
 LEVELS = 15
 TOKEN_CEILING = 3
 HIDDEN_CEILING = 24
@@ -92,7 +93,14 @@
         out_refs[o][7 * CAP : OUT_ROWS, :] = levels
 
 
-def hidden_kernel(got_ref, gate_ref, up_ref, down_ref, out_ref):
+def both_of(pair_ref, d):
+    start = d * PAIR_ROWS
+    return jnp.concatenate(
+        [pair_ref[start : start + FEAT, :], pair_ref[start + FEAT : start + PAIR_ROWS, :]], axis=1
+    )
+
+
+def hidden_kernel(got_ref, pair_ref, down_ref, out_ref):
     zero_cols = jnp.zeros((64, 2 * HID), bf16)
     zero_half = jnp.zeros((64, HID), bf16)
     pre = jnp.zeros((ROUTED, 2 * HID), f32)
@@ -112,7 +120,7 @@
         in_b = jnp.concatenate([column(d, 2), tail], axis=1)
         grad_a = jnp.concatenate([column(d, 3), column(d, 4)], axis=1)
         grad_b = jnp.concatenate([column(d, 5), tail], axis=1)
-        both = jnp.concatenate([gate_ref[low : low + FEAT, :], up_ref[low : low + FEAT, :]], axis=1)
+        both = both_of(pair_ref, d)
         down = down_ref[low : low + FEAT, :]
         both_b = jnp.concatenate([both[256:448], zero_cols], axis=0)
         down_b = jnp.concatenate([down[256:384], zero_half, down[384:448]], axis=0)
@@ -160,7 +168,7 @@
     out_ref[2 * ROUTED : HIDE_ROWS, :] = rows.astype(bf16)
 
 
-def back_kernel(got_ref, gate_ref, up_ref, *out_refs):
+def back_kernel(got_ref, pair_ref, *out_refs):
     zero_cols = jnp.zeros((64, 2 * HID), bf16)
     head = jnp.zeros((ROUTED, 384), f32)
     tail = jnp.zeros((2 * CAP, LANE), f32)
@@ -175,8 +183,7 @@
         up_grad = (got_ref[base + ROUTED : base + 2 * ROUTED, :].astype(f32) * inverse_up).astype(bf16)
         hidden = jnp.concatenate([pre_grad, up_grad], axis=1)
         paired = jnp.concatenate([hidden[0 : 2 * CAP], hidden[2 * CAP : 4 * CAP]], axis=1)
-        low = d * FEAT
-        both = jnp.concatenate([gate_ref[low : low + FEAT, :], up_ref[low : low + FEAT, :]], axis=1)
+        both = both_of(pair_ref, d)
         head = head + lax.dot_general(hidden, both[0:384], NT, preferred_element_type=f32)
         corner = jnp.concatenate([both[384:448], zero_cols], axis=1)
         other = jnp.concatenate([zero_cols, both[384:448]], axis=1)
@@ -226,8 +233,10 @@
 
 def body(layer_input, output_grad, gate_weight, up_weight, down_weight, route_offset, gate_fixed):
     route = route_offset.T
-    gate_rows = lax.all_to_all(gate_weight[0], "local", 0, 0, tiled=True)
-    up_rows = lax.all_to_all(up_weight[0], "local", 0, 0, tiled=True)
+    pairs = jnp.concatenate(
+        [gate_weight[0].reshape(LOCAL, FEAT, HID), up_weight[0].reshape(LOCAL, FEAT, HID)], axis=1
+    ).reshape(LOCAL * PAIR_ROWS, HID)
+    pair_rows = lax.all_to_all(pairs, "local", 0, 0, tiled=True)
     packed = call(
         pack_kernel,
         [jax.ShapeDtypeStruct((OUT_ROWS, LANE), bf16)] * GROUP,
@@ -242,13 +251,12 @@
         hidden_kernel,
         jax.ShapeDtypeStruct((HIDE_ROWS, LANE), bf16),
         full,
-        gate_weight[0],
-        up_weight[0],
+        pairs,
         down_weight[0].T,
     )
     spread = lax.all_gather(hidden.astype(jnp.float16), "local", axis=0, tiled=True).astype(bf16)
     summed = call(
-        back_kernel, [jax.ShapeDtypeStruct((HOME_ROWS, LANE), bf16)] * GROUP, spread, gate_rows, up_rows
+        back_kernel, [jax.ShapeDtypeStruct((HOME_ROWS, LANE), bf16)] * GROUP, spread, pair_rows
     )
     home = [summed[0]] + [from_behind(summed[o], "node", -o) for o in range(1, GROUP)]
     input_grad, gate_grad = call(

time: 167 us -> 160 us (0.958)
  blocking collectives: 89.7 us -> 81.3 us
  other arithmetic: 1.68 us -> 4.7 us
  starting transfers between devices: 47.4 us -> 45.3 us
    all_gather x1, blocking collectives: 67 us -> 57.9 us  [body(): full = lax.all_gather(shard, 'local', axis=0, tiled=True).astype(bf16)]
    all_to_all x2 -> x1, starting transfers between devices: 14.6 us -> 7.77 us  [body(): pair_rows = lax.all_to_all(pairs, 'local', 0, 0, tiled=True)]
    ppermute x6, starting transfers between devices: 32.8 us -> 37.5 us  [from_behind(): return lax.ppermute(value, axis, pairs)]
    concatenate x0 -> x1, other arithmetic: none -> 2.87 us  [body(): jnp.concatenate([gate_weight[0].reshape(LOCAL, FEAT, HID), up_weight[0].r...]
  transfers between devices with their start and end apart: 8 -> 7, of which waited for: 3 -> 3; matrix products, arithmetic and copies ran while one was open for 2% -> 2% of each run, Pallas kernels for 2% -> 3%
where the time goes in v4:
time: 160 us; the launch traced here: 159 us
  blocking collectives  81.3 us (51%)
  starting transfers between devices  45.3 us (28%)
  waiting for transfers between devices  19.3 us (12%)
  Pallas kernels  6.32 us (4%)
  other arithmetic  4.7 us (3%)
    all_gather x1, blocking collectives, body(): full = lax.all_gather(shard, 'local', axis=0, tiled=True).astype(bf16)  57.9 us
    ppermute x6, starting transfers between devices, from_behind(): return lax.ppermute(value, axis, pairs)  37.5 us
    all_gather x1, blocking collectives, body(): lax.all_gather(hidden.astype(jnp.float16), 'local', axis=0, tiled=True)  23.4 us
    ppermute x6, waiting for transfers between devices, from_behind(): return lax.ppermute(value, axis, pairs)  19.3 us
    all_to_all x1, starting transfers between devices, body(): pair_rows = lax.all_to_all(pairs, 'local', 0, 0, tiled=True)  7.77 us
    pallas_call x4, Pallas kernels, call(): pl.pallas_call(kernel, out_shape=outs, interpret=INTERPRET, compiler_para...  6.32 us
  transfers between devices with their start and end apart: 7, of which 3 were waited for; matrix products, arithmetic and copies ran while one was open for 2% of the time, Pallas kernels for 3%

profile of v4, /device:TPU:1, one launch (start us, length us, event | category | flops | bytes accessed | tf_op | source)
XLA Modules:
  0.0 159.2 jit_solution(11034785564670302385)
XLA Ops:
  0.6 2.9 %pad_maximum_fusion = bf16[8,896,128]{2,1,0:T(8,128)(2,1)} fusion(bf16[8,448,128]{2,1,0:T(8,128)(2,1)} %bitcast.20, bf16[8,448,128]{2,1,0:T(8,128)(2,1)} %bitcast.21), kind=kLoop, calls=%fused_computation | loop fusion | flops 3670016 | bytes 3670016 | tf_op jit(solution)/shard_map/concatenate | solution.py:236
  3.5 0.0 copy-start
  3.5 0.0 copy-start.1
  3.5 0.0 copy-start.2
  3.5 7.8 %all-to-all-start = ((bf16[8,896,128]{2,1,0:T(8,128)(2,1)}), bf16[8,896,128]{2,1,0:T(8,128)(2,1)S(1)}, u32[]{:S(2)}, u32[]{:S(2)}) async-start(bf16[8,896,128]{2,1,0:T(8,128)(2,1)} %pad_maximum_fusion), calls=%async_computation | async-start | bytes 3670016 | tf_op jit(solution)/shard_map/all_to_all | solution.py:239
  11.3 0.0 copy-done
  11.3 0.0 copy-done.1
  11.3 0.0 copy-done.2
  11.3 0.5 shard_map.86
  11.8 4.0 %collective-permute-start = (bf16[576,128]{1,0:T(8,128)(2,1)S(1)}, bf16[576,128]{1,0:T(8,128)(2,1)S(1)}, u32[]{:S(2)}, u32[]{:S(2)}) collective-permute-start(bf16[576,128]{1,0:T(8,128)(2,1)S(1)} %get-tuple-element.13), channel_id=1, source_target_pairs={{0,8},{8,16},{16,24},{24,32},{32,40},{40,48},{48,56},{56,64},{64,7... | collective-permute-start | bytes 442376 | tf_op jit(solution)/shard_map/ppermute | solution.py:35
  15.7 3.1 %collective-permute-start.1 = (bf16[576,128]{1,0:T(8,128)(2,1)S(1)}, bf16[576,128]{1,0:T(8,128)(2,1)}, u32[]{:S(2)}, u32[]{:S(2)}) collective-permute-start(bf16[576,128]{1,0:T(8,128)(2,1)S(1)} %get-tuple-element.14), channel_id=1, source_target_pairs={{0,16},{8,24},{16,32},{24,40},{32,48},{40,56},{48,64},{56,72},{64,... | collective-permute-start | bytes 442376 | tf_op jit(solution)/shard_map/ppermute | solution.py:35
  18.9 3.4 %collective-permute-start.2 = (bf16[576,128]{1,0:T(8,128)(2,1)S(1)}, bf16[576,128]{1,0:T(8,128)(2,1)}, u32[]{:S(2)}, u32[]{:S(2)}) collective-permute-start(bf16[576,128]{1,0:T(8,128)(2,1)S(1)} %get-tuple-element.15), channel_id=1, source_target_pairs={{0,24},{8,32},{16,40},{24,48},{32,56},{40,64},{48,72},{56,80},{64,... | collective-permute-start | bytes 442376 | tf_op jit(solution)/shard_map/ppermute | solution.py:35
  22.3 1.6 copy.9
  23.9 0.0 collective-permute-done
  23.9 9.7 %collective-permute-done.1 = bf16[576,128]{1,0:T(8,128)(2,1)} collective-permute-done((bf16[576,128]{1,0:T(8,128)(2,1)S(1)}, bf16[576,128]{1,0:T(8,128)(2,1)}, u32[]{:S(2)}, u32[]{:S(2)}) %collective-permute-start.1) | collective-permute-done | bytes 147488 | tf_op jit(solution)/shard_map/ppermute | solution.py:35
  33.6 5.0 %collective-permute-done.2 = bf16[576,128]{1,0:T(8,128)(2,1)} collective-permute-done((bf16[576,128]{1,0:T(8,128)(2,1)S(1)}, bf16[576,128]{1,0:T(8,128)(2,1)}, u32[]{:S(2)}, u32[]{:S(2)}) %collective-permute-start.2) | collective-permute-done | bytes 147488 | tf_op jit(solution)/shard_map/ppermute | solution.py:35
  38.5 1.1 maximum_convert_fusion
  39.6 57.9 %all-gather.2 = f16[18432,128]{1,0:T(8,128)(2,1)S(1)} all-gather(f16[2304,128]{1,0:T(8,128)(2,1)S(1)} %maximum_convert_fusion), channel_id=1, replica_groups=mesh['node'=96,'local'=8] {'local'}, dimensions={0}, use_global_device_ids=true | all-gather | bytes 5308416 | tf_op jit(solution)/shard_map/all_gather | solution.py:249
  97.5 0.5 convert_element_type.13.got_ref
  98.1 3.6 %shard_map.87 = bf16[656,128]{1,0:T(8,128)(2,1)S(1)} custom-call(bf16[18432,128]{1,0:T(8,128)(2,1)S(1)} %convert_element_type.13.got_ref, bf16[7168,128]{1,0:T(8,128)(2,1)} %bitcast.6.pair_ref, bf16[3584,128]{1,0:T(8,128)(2,1)S(1)} %bitcast.14), custom_call_target="tpu_custom_call" | custom-call | tf_op jit(solution)/shard_map/pallas_call | solution.py:231
  101.7 23.4 %all-gather.3 = f16[5248,128]{1,0:T(8,128)(2,1)S(1)} all-gather(f16[656,128]{1,0:T(8,128)(2,1)S(1)} %convert_element_type.14), channel_id=1, replica_groups=mesh['node'=96,'local'=8] {'local'}, dimensions={0}, use_global_device_ids=true | all-gather | bytes 1511424 | tf_op jit(solution)/shard_map/all_gather | solution.py:257
  125.1 0.1 convert_element_type.15.got_ref
  125.3 0.0 copy-start.3
  125.3 0.0 all-to-all-done
  125.3 1.2 shard_map.88
  126.5 7.8 %collective-permute-start.3 = (bf16[336,128]{1,0:T(8,128)(2,1)S(1)}, bf16[336,128]{1,0:T(8,128)(2,1)S(1)}, u32[]{:S(2)}, u32[]{:S(2)}) collective-permute-start(bf16[336,128]{1,0:T(8,128)(2,1)S(1)} %get-tuple-element.17), channel_id=1, source_target_pairs={{0,760},{8,0},{16,8},{24,16},{32,24},{40,32},{48,40},{56,48},{64,5... | collective-permute-start | bytes 258056 | tf_op jit(solution)/shard_map/ppermute | solution.py:35
  134.3 16.5 %collective-permute-start.4 = (bf16[336,128]{1,0:T(8,128)(2,1)S(1)}, bf16[336,128]{1,0:T(8,128)(2,1)S(1)}, u32[]{:S(2)}, u32[]{:S(2)}) collective-permute-start(bf16[336,128]{1,0:T(8,128)(2,1)S(1)} %get-tuple-element.18), channel_id=1, source_target_pairs={{0,752},{8,760},{16,0},{24,8},{32,16},{40,24},{48,32},{56,40},{64,... | collective-permute-start | bytes 258056 | tf_op jit(solution)/shard_map/ppermute | solution.py:35
  150.8 2.6 %collective-permute-start.5 = (bf16[336,128]{1,0:T(8,128)(2,1)S(1)}, bf16[336,128]{1,0:T(8,128)(2,1)S(1)}, u32[]{:S(2)}, u32[]{:S(2)}) collective-permute-start(bf16[336,128]{1,0:T(8,128)(2,1)S(1)} %get-tuple-element.19), channel_id=1, source_target_pairs={{0,744},{8,752},{16,760},{24,0},{32,8},{40,16},{48,24},{56,32},{64... | collective-permute-start | bytes 258056 | tf_op jit(solution)/shard_map/ppermute | solution.py:35
  153.5 0.0 collective-permute-done.3.refs_1_
  153.5 0.0 collective-permute-done.4.refs_2_
  153.5 4.6 %collective-permute-done.5.refs_3_ = bf16[336,128]{1,0:T(8,128)(2,1)S(1)} collective-permute-done((bf16[336,128]{1,0:T(8,128)(2,1)S(1)}, bf16[336,128]{1,0:T(8,128)(2,1)S(1)}, u32[]{:S(2)}, u32[]{:S(2)}) %collective-permute-start.5) | collective-permute-done | bytes 86048 | tf_op jit(solution)/shard_map/ppermute | solution.py:35
  158.1 0.0 copy-done.3
  158.2 1.1 shard_map.89
  (1 shorter events, 0.0 us)
Async XLA Ops:
  3.5 7.8 %copy-start = (bf16[128,448]{0,1:T(8,128)(2,1)S(1)}, bf16[128,448]{0,1:T(8,128)(2,1)}, u32[]{:S(2)}) copy-start(bf16[128,448]{0,1:T(8,128)(2,1)} %param.7) | copy-start | bytes 344068
  3.5 7.8 %copy-start.1 = (bf16[128,448]{0,1:T(8,128)(2,1)S(1)}, bf16[128,448]{0,1:T(8,128)(2,1)}, u32[]{:S(2)}) copy-start(bf16[128,448]{0,1:T(8,128)(2,1)} %param.8) | copy-start | bytes 344068
  3.5 7.8 %copy-start.2 = (s32[128,2]{0,1:T(2,128)S(1)}, s32[128,2]{0,1:T(2,128)}, u32[]{:S(2)}) copy-start(s32[128,2]{0,1:T(2,128)} %param.12) | copy-start | bytes 3076
  3.5 121.8 %all-to-all-start = ((bf16[8,896,128]{2,1,0:T(8,128)(2,1)}), bf16[8,896,128]{2,1,0:T(8,128)(2,1)S(1)}, u32[]{:S(2)}, u32[]{:S(2)}) async-start(bf16[8,896,128]{2,1,0:T(8,128)(2,1)} %pad_maximum_fusion), calls=%async_computation | async-start | bytes 3670016 | tf_op jit(solution)/shard_map/all_to_all | solution.py:239
  11.8 12.1 %collective-permute-start = (bf16[576,128]{1,0:T(8,128)(2,1)S(1)}, bf16[576,128]{1,0:T(8,128)(2,1)S(1)}, u32[]{:S(2)}, u32[]{:S(2)}) collective-permute-start(bf16[576,128]{1,0:T(8,128)(2,1)S(1)} %get-tuple-element.13), channel_id=1, source_target_pairs={{0,8},{8,16},{16,24},{24,32},{32,40},{40,48},{48,56},{56,64},{64,7... | collective-permute-start | bytes 442376 | tf_op jit(solution)/shard_map/ppermute | solution.py:35
  15.7 17.8 %collective-permute-start.1 = (bf16[576,128]{1,0:T(8,128)(2,1)S(1)}, bf16[576,128]{1,0:T(8,128)(2,1)}, u32[]{:S(2)}, u32[]{:S(2)}) collective-permute-start(bf16[576,128]{1,0:T(8,128)(2,1)S(1)} %get-tuple-element.14), channel_id=1, source_target_pairs={{0,16},{8,24},{16,32},{24,40},{32,48},{40,56},{48,64},{56,72},{64,... | collective-permute-start | bytes 442376 | tf_op jit(solution)/shard_map/ppermute | solution.py:35
  18.9 19.7 %collective-permute-start.2 = (bf16[576,128]{1,0:T(8,128)(2,1)S(1)}, bf16[576,128]{1,0:T(8,128)(2,1)}, u32[]{:S(2)}, u32[]{:S(2)}) collective-permute-start(bf16[576,128]{1,0:T(8,128)(2,1)S(1)} %get-tuple-element.15), channel_id=1, source_target_pairs={{0,24},{8,32},{16,40},{24,48},{32,56},{40,64},{48,72},{56,80},{64,... | collective-permute-start | bytes 442376 | tf_op jit(solution)/shard_map/ppermute | solution.py:35
  125.3 32.9 %copy-start.3 = (s32[128,2]{0,1:T(2,128)S(1)}, s32[128,2]{0,1:T(2,128)}, u32[]{:S(2)}) copy-start(s32[128,2]{0,1:T(2,128)} %param.13) | copy-start | bytes 3076
  126.5 27.0 %collective-permute-start.3 = (bf16[336,128]{1,0:T(8,128)(2,1)S(1)}, bf16[336,128]{1,0:T(8,128)(2,1)S(1)}, u32[]{:S(2)}, u32[]{:S(2)}) collective-permute-start(bf16[336,128]{1,0:T(8,128)(2,1)S(1)} %get-tuple-element.17), channel_id=1, source_target_pairs={{0,760},{8,0},{16,8},{24,16},{32,24},{40,32},{48,40},{56,48},{64,5... | collective-permute-start | bytes 258056 | tf_op jit(solution)/shard_map/ppermute | solution.py:35
  134.3 19.1 %collective-permute-start.4 = (bf16[336,128]{1,0:T(8,128)(2,1)S(1)}, bf16[336,128]{1,0:T(8,128)(2,1)S(1)}, u32[]{:S(2)}, u32[]{:S(2)}) collective-permute-start(bf16[336,128]{1,0:T(8,128)(2,1)S(1)} %get-tuple-element.18), channel_id=1, source_target_pairs={{0,752},{8,760},{16,0},{24,8},{32,16},{40,24},{48,32},{56,40},{64,... | collective-permute-start | bytes 258056 | tf_op jit(solution)/shard_map/ppermute | solution.py:35
  150.8 7.3 %collective-permute-start.5 = (bf16[336,128]{1,0:T(8,128)(2,1)S(1)}, bf16[336,128]{1,0:T(8,128)(2,1)S(1)}, u32[]{:S(2)}, u32[]{:S(2)}) collective-permute-start(bf16[336,128]{1,0:T(8,128)(2,1)S(1)} %get-tuple-element.19), channel_id=1, source_target_pairs={{0,744},{8,752},{16,760},{24,0},{32,8},{40,16},{48,24},{56,32},{64... | collective-permute-start | bytes 258056 | tf_op jit(solution)/shard_map/ppermute | solution.py:35

commit v5 on v3

--- a/solution.py
+++ b/solution.py
@@ -227,7 +227,6 @@
 def body(layer_input, output_grad, gate_weight, up_weight, down_weight, route_offset, gate_fixed):
     route = route_offset.T
     gate_rows = lax.all_to_all(gate_weight[0], "local", 0, 0, tiled=True)
-    up_rows = lax.all_to_all(up_weight[0], "local", 0, 0, tiled=True)
     packed = call(
         pack_kernel,
         [jax.ShapeDtypeStruct((OUT_ROWS, LANE), bf16)] * GROUP,
@@ -237,14 +236,17 @@
     )
     got = [packed[0]] + [from_behind(packed[o], "node", o) for o in range(1, GROUP)]
     shard = jnp.concatenate(got, axis=0).astype(jnp.float16)
-    full = lax.all_gather(shard, "local", axis=0, tiled=True).astype(bf16)
+    shard, down_cols = lax.optimization_barrier((shard, down_weight[0].T))
+    full, late_up = lax.optimization_barrier((lax.all_gather(shard, "local", axis=0, tiled=True), up_weight[0]))
+    full = full.astype(bf16)
+    up_rows = lax.all_to_all(late_up, "local", 0, 0, tiled=True)
     hidden = call(
         hidden_kernel,
         jax.ShapeDtypeStruct((HIDE_ROWS, LANE), bf16),
         full,
         gate_weight[0],
         up_weight[0],
-        down_weight[0].T,
+        down_cols,
     )
     spread = lax.all_gather(hidden.astype(jnp.float16), "local", axis=0, tiled=True).astype(bf16)
     summed = call(

time: 167 us -> 165 us (0.988)
  waiting for transfers between devices: 19.2 us -> 12 us
  other arithmetic: 1.68 us -> 4.69 us
    all_gather x1, blocking collectives: 22.7 us -> 33.8 us  [body(): lax.all_gather(hidden.astype(jnp.float16), 'local', axis=0, tiled=True)]
    all_gather x1, blocking collectives: 67 us -> 56.6 us  [body(): lax.all_gather(shard, 'local', axis=0, tiled=True)]
    ppermute x6, waiting for transfers between devices: 19.2 us -> 12 us  [from_behind(): return lax.ppermute(value, axis, pairs)]
    ppermute x6, starting transfers between devices: 32.8 us -> 35.7 us  [from_behind(): return lax.ppermute(value, axis, pairs)]
    convert_element_type x1, other arithmetic: 0.55 us -> 3.34 us  [body(): full = full.astype(bf16)]
    all_to_all x1, starting transfers between devices: 7.78 us -> 5.16 us  [body(): up_rows = lax.all_to_all(late_up, 'local', 0, 0, tiled=True)]
  transfers between devices with their start and end apart: 8 -> 8, of which waited for: 3 -> 3; matrix products, arithmetic and copies ran while one was open for 2% -> 3% of each run, Pallas kernels for 2% -> 2%
where the time goes in v5:
time: 165 us
  blocking collectives  90.4 us (55%)
  starting transfers between devices  47.7 us (29%)
  waiting for transfers between devices  12 us (7%)
  Pallas kernels  5.93 us (4%)
  other arithmetic  4.69 us (3%)
  local copies, waits for them, and re-layouts  3.1 us (2%)
    all_gather x1, blocking collectives, body(): lax.all_gather(shard, 'local', axis=0, tiled=True)  56.6 us
    ppermute x6, starting transfers between devices, from_behind(): return lax.ppermute(value, axis, pairs)  35.7 us
    all_gather x1, blocking collectives, body(): lax.all_gather(hidden.astype(jnp.float16), 'local', axis=0, tiled=True)  33.8 us
    ppermute x6, waiting for transfers between devices, from_behind(): return lax.ppermute(value, axis, pairs)  12 us
    all_to_all x1, starting transfers between devices, body(): gate_rows = lax.all_to_all(gate_weight[0], 'local', 0, 0, tiled=True)  6.83 us
    pallas_call x4, Pallas kernels, call(): pl.pallas_call(kernel, out_shape=outs, interpret=INTERPRET, compiler_para...  5.93 us
    all_to_all x1, starting transfers between devices, body(): up_rows = lax.all_to_all(late_up, 'local', 0, 0, tiled=True)  5.16 us
    convert_element_type x1, other arithmetic, body(): full = full.astype(bf16)  3.34 us
  transfers between devices with their start and end apart: 8, of which 3 were waited for; matrix products, arithmetic and copies ran while one was open for 3% of the time, Pallas kernels for 2%

profile of v5, /device:TPU:1, one launch (start us, length us, event | category | flops | bytes accessed | tf_op | source)
XLA Modules:
  0.0 164.6 jit_solution(10660062215481075561)
XLA Ops:
  0.6 0.0 copy-start.1
  0.6 0.9 copy-done.1
  1.5 0.0 copy-start.2
  1.5 0.9 copy-done.2
  2.4 0.0 copy-start.3
  2.4 0.7 copy-done.3
  3.1 0.0 copy-start.6
  3.1 0.4 shard_map.86
  3.6 4.5 %collective-permute-start = (bf16[576,128]{1,0:T(8,128)(2,1)S(1)}, bf16[576,128]{1,0:T(8,128)(2,1)}, u32[]{:S(2)}, u32[]{:S(2)}) collective-permute-start(bf16[576,128]{1,0:T(8,128)(2,1)S(1)} %get-tuple-element.17), channel_id=1, source_target_pairs={{0,8},{8,16},{16,24},{24,32},{32,40},{40,48},{48,56},{56,64},{64,7... | collective-permute-start | bytes 442376 | tf_op jit(solution)/shard_map/ppermute | solution.py:34
  8.1 3.1 %collective-permute-start.1 = (bf16[576,128]{1,0:T(8,128)(2,1)S(1)}, bf16[576,128]{1,0:T(8,128)(2,1)}, u32[]{:S(2)}, u32[]{:S(2)}) collective-permute-start(bf16[576,128]{1,0:T(8,128)(2,1)S(1)} %get-tuple-element.18), channel_id=1, source_target_pairs={{0,16},{8,24},{16,32},{24,40},{32,48},{40,56},{48,64},{56,72},{64,... | collective-permute-start | bytes 442376 | tf_op jit(solution)/shard_map/ppermute | solution.py:34
  11.2 3.4 %collective-permute-start.2 = (bf16[576,128]{1,0:T(8,128)(2,1)S(1)}, bf16[576,128]{1,0:T(8,128)(2,1)}, u32[]{:S(2)}, u32[]{:S(2)}) collective-permute-start(bf16[576,128]{1,0:T(8,128)(2,1)S(1)} %get-tuple-element.19), channel_id=1, source_target_pairs={{0,24},{8,32},{16,40},{24,48},{32,56},{40,64},{48,72},{56,80},{64,... | collective-permute-start | bytes 442376 | tf_op jit(solution)/shard_map/ppermute | solution.py:34
  14.7 6.8 %all-to-all-start = ((bf16[8,448,128]{2,1,0:T(8,128)(2,1)}), bf16[8,448,128]{2,1,0:T(8,128)(2,1)S(1)}, u32[]{:S(2)}, u32[]{:S(2)}) async-start(bf16[8,448,128]{2,1,0:T(8,128)(2,1)} %bitcast.15), calls=%async_computation | async-start | bytes 1835008 | tf_op jit(solution)/shard_map/all_to_all | solution.py:229
  21.5 0.0 copy-done.6
  21.5 0.6 copy.9
  22.1 0.0 collective-permute-done
  22.1 4.3 %collective-permute-done.1 = bf16[576,128]{1,0:T(8,128)(2,1)} collective-permute-done((bf16[576,128]{1,0:T(8,128)(2,1)S(1)}, bf16[576,128]{1,0:T(8,128)(2,1)}, u32[]{:S(2)}, u32[]{:S(2)}) %collective-permute-start.1) | collective-permute-done | bytes 147488 | tf_op jit(solution)/shard_map/ppermute | solution.py:34
  26.5 4.4 %collective-permute-done.2 = bf16[576,128]{1,0:T(8,128)(2,1)} collective-permute-done((bf16[576,128]{1,0:T(8,128)(2,1)S(1)}, bf16[576,128]{1,0:T(8,128)(2,1)}, u32[]{:S(2)}, u32[]{:S(2)}) %collective-permute-start.2) | collective-permute-done | bytes 147488 | tf_op jit(solution)/shard_map/ppermute | solution.py:34
  30.9 1.2 maximum_convert_fusion
  32.0 56.6 %all-gather.2 = f16[18432,128]{1,0:T(8,128)(2,1)} all-gather(f16[2304,128]{1,0:T(8,128)(2,1)S(1)} %maximum_convert_fusion), channel_id=1, replica_groups=mesh['node'=96,'local'=8] {'local'}, dimensions={0}, use_global_device_ids=true | all-gather | bytes 5308416 | tf_op jit(solution)/shard_map/all_gather | solution.py:240
  88.6 0.0 all-to-all-done
  88.6 5.2 %all-to-all-start.1 = ((bf16[8,448,128]{2,1,0:T(8,128)(2,1)}), bf16[8,448,128]{2,1,0:T(8,128)(2,1)S(1)}, u32[]{:S(2)}, u32[]{:S(2)}) async-start(bf16[8,448,128]{2,1,0:T(8,128)(2,1)} %bitcast.10), calls=%async_computation.1 | async-start | bytes 1835008 | tf_op jit(solution)/shard_map/all_to_all | solution.py:242
  93.8 0.0 copy-start
  93.8 3.3 %convert_element_type.13.got_ref = bf16[18432,128]{1,0:T(8,128)(2,1)S(1)} convert(f16[18432,128]{1,0:T(8,128)(2,1)} %all-gather.2) | non-fusion elementwise | flops 2359296 | bytes 9437184 | tf_op jit(solution)/shard_map/convert_element_type | solution.py:241
  97.1 0.0 copy-done
  97.1 3.2 %shard_map.87 = bf16[656,128]{1,0:T(8,128)(2,1)S(1)} custom-call(bf16[18432,128]{1,0:T(8,128)(2,1)S(1)} %convert_element_type.13.got_ref, bf16[3584,128]{1,0:T(8,128)(2,1)S(1)} %bitcast.16, bf16[3584,128]{1,0:T(8,128)(2,1)} %bitcast.6.up_ref, bf16[3584,128]{1,0:T(8,128)(2,1)S(1)} %bitcast.17), custom_call_target="tpu_custom_call" | custom-call | tf_op jit(solution)/shard_map/pallas_call | solution.py:224
  100.4 33.8 %all-gather.3 = f16[5248,128]{1,0:T(8,128)(2,1)S(1)} all-gather(f16[656,128]{1,0:T(8,128)(2,1)S(1)} %convert_element_type.14), channel_id=1, replica_groups=mesh['node'=96,'local'=8] {'local'}, dimensions={0}, use_global_device_ids=true | all-gather | bytes 1511424 | tf_op jit(solution)/shard_map/all_gather | solution.py:251
  134.2 0.1 convert_element_type.15.got_ref
  134.3 0.0 all-to-all-done.1
  134.4 0.0 copy-start.4
  134.4 0.0 copy-start.5
  134.4 1.2 shard_map.88
  135.6 8.6 %collective-permute-start.3 = (bf16[336,128]{1,0:T(8,128)(2,1)S(1)}, bf16[336,128]{1,0:T(8,128)(2,1)S(1)}, u32[]{:S(2)}, u32[]{:S(2)}) collective-permute-start(bf16[336,128]{1,0:T(8,128)(2,1)S(1)} %get-tuple-element.25), channel_id=1, source_target_pairs={{0,760},{8,0},{16,8},{24,16},{32,24},{40,32},{48,40},{56,48},{64,5... | collective-permute-start | bytes 258056 | tf_op jit(solution)/shard_map/ppermute | solution.py:34
  144.1 12.1 %collective-permute-start.4 = (bf16[336,128]{1,0:T(8,128)(2,1)S(1)}, bf16[336,128]{1,0:T(8,128)(2,1)S(1)}, u32[]{:S(2)}, u32[]{:S(2)}) collective-permute-start(bf16[336,128]{1,0:T(8,128)(2,1)S(1)} %get-tuple-element.26), channel_id=1, source_target_pairs={{0,752},{8,760},{16,0},{24,8},{32,16},{40,24},{48,32},{56,40},{64,... | collective-permute-start | bytes 258056 | tf_op jit(solution)/shard_map/ppermute | solution.py:34
  156.2 4.0 %collective-permute-start.5 = (bf16[336,128]{1,0:T(8,128)(2,1)S(1)}, bf16[336,128]{1,0:T(8,128)(2,1)S(1)}, u32[]{:S(2)}, u32[]{:S(2)}) collective-permute-start(bf16[336,128]{1,0:T(8,128)(2,1)S(1)} %get-tuple-element.27), channel_id=1, source_target_pairs={{0,744},{8,752},{16,760},{24,0},{32,8},{40,16},{48,24},{56,32},{64... | collective-permute-start | bytes 258056 | tf_op jit(solution)/shard_map/ppermute | solution.py:34
  160.2 0.0 collective-permute-done.3.refs_1_
  160.2 0.0 collective-permute-done.4.refs_2_
  160.2 3.3 %collective-permute-done.5.refs_3_ = bf16[336,128]{1,0:T(8,128)(2,1)S(1)} collective-permute-done((bf16[336,128]{1,0:T(8,128)(2,1)S(1)}, bf16[336,128]{1,0:T(8,128)(2,1)S(1)}, u32[]{:S(2)}, u32[]{:S(2)}) %collective-permute-start.5) | collective-permute-done | bytes 86048 | tf_op jit(solution)/shard_map/ppermute | solution.py:34
  163.5 0.0 copy-done.4
  163.5 0.0 copy-done.5
  163.5 1.1 shard_map.89
  (1 shorter events, 0.0 us)
Async XLA Ops:
  0.6 0.9 copy-start.1
  1.5 0.9 copy-start.2
  2.4 0.7 copy-start.3
  3.1 18.4 %copy-start.6 = (bf16[1,128,3584]{2,1,0:T(8,128)(2,1)S(1)}, bf16[1,128,3584]{2,1,0:T(8,128)(2,1)}, u32[]{:S(2)}) copy-start(bf16[1,128,3584]{2,1,0:T(8,128)(2,1)} %param.11) | copy-start | bytes 2752516
  3.6 18.6 %collective-permute-start = (bf16[576,128]{1,0:T(8,128)(2,1)S(1)}, bf16[576,128]{1,0:T(8,128)(2,1)}, u32[]{:S(2)}, u32[]{:S(2)}) collective-permute-start(bf16[576,128]{1,0:T(8,128)(2,1)S(1)} %get-tuple-element.17), channel_id=1, source_target_pairs={{0,8},{8,16},{16,24},{24,32},{32,40},{40,48},{48,56},{56,64},{64,7... | collective-permute-start | bytes 442376 | tf_op jit(solution)/shard_map/ppermute | solution.py:34
  8.1 18.4 %collective-permute-start.1 = (bf16[576,128]{1,0:T(8,128)(2,1)S(1)}, bf16[576,128]{1,0:T(8,128)(2,1)}, u32[]{:S(2)}, u32[]{:S(2)}) collective-permute-start(bf16[576,128]{1,0:T(8,128)(2,1)S(1)} %get-tuple-element.18), channel_id=1, source_target_pairs={{0,16},{8,24},{16,32},{24,40},{32,48},{40,56},{48,64},{56,72},{64,... | collective-permute-start | bytes 442376 | tf_op jit(solution)/shard_map/ppermute | solution.py:34
  11.2 19.7 %collective-permute-start.2 = (bf16[576,128]{1,0:T(8,128)(2,1)S(1)}, bf16[576,128]{1,0:T(8,128)(2,1)}, u32[]{:S(2)}, u32[]{:S(2)}) collective-permute-start(bf16[576,128]{1,0:T(8,128)(2,1)S(1)} %get-tuple-element.19), channel_id=1, source_target_pairs={{0,24},{8,32},{16,40},{24,48},{32,56},{40,64},{48,72},{56,80},{64,... | collective-permute-start | bytes 442376 | tf_op jit(solution)/shard_map/ppermute | solution.py:34
  14.7 74.0 %all-to-all-start = ((bf16[8,448,128]{2,1,0:T(8,128)(2,1)}), bf16[8,448,128]{2,1,0:T(8,128)(2,1)S(1)}, u32[]{:S(2)}, u32[]{:S(2)}) async-start(bf16[8,448,128]{2,1,0:T(8,128)(2,1)} %bitcast.15), calls=%async_computation | async-start | bytes 1835008 | tf_op jit(solution)/shard_map/all_to_all | solution.py:229
  88.6 45.7 %all-to-all-start.1 = ((bf16[8,448,128]{2,1,0:T(8,128)(2,1)}), bf16[8,448,128]{2,1,0:T(8,128)(2,1)S(1)}, u32[]{:S(2)}, u32[]{:S(2)}) async-start(bf16[8,448,128]{2,1,0:T(8,128)(2,1)} %bitcast.10), calls=%async_computation.1 | async-start | bytes 1835008 | tf_op jit(solution)/shard_map/all_to_all | solution.py:242
  93.8 3.4 %copy-start = (bf16[1,3584,128]{2,1,0:T(8,128)(2,1)S(1)}, bf16[1,3584,128]{2,1,0:T(8,128)(2,1)}, u32[]{:S(2)}) copy-start(bf16[1,3584,128]{2,1,0:T(8,128)(2,1)} %param.9) | copy-start | bytes 2752516
  134.4 29.1 %copy-start.4 = (s32[128,2]{0,1:T(2,128)S(1)}, s32[128,2]{0,1:T(2,128)}, u32[]{:S(2)}) copy-start(s32[128,2]{0,1:T(2,128)} %param.12) | copy-start | bytes 3076
  134.4 29.1 %copy-start.5 = (s32[128,2]{0,1:T(2,128)S(1)}, s32[128,2]{0,1:T(2,128)}, u32[]{:S(2)}) copy-start(s32[128,2]{0,1:T(2,128)} %param.13) | copy-start | bytes 3076
  135.6 24.6 %collective-permute-start.3 = (bf16[336,128]{1,0:T(8,128)(2,1)S(1)}, bf16[336,128]{1,0:T(8,128)(2,1)S(1)}, u32[]{:S(2)}, u32[]{:S(2)}) collective-permute-start(bf16[336,128]{1,0:T(8,128)(2,1)S(1)} %get-tuple-element.25), channel_id=1, source_target_pairs={{0,760},{8,0},{16,8},{24,16},{32,24},{40,32},{48,40},{56,48},{64,5... | collective-permute-start | bytes 258056 | tf_op jit(solution)/shard_map/ppermute | solution.py:34
  144.1 16.1 %collective-permute-start.4 = (bf16[336,128]{1,0:T(8,128)(2,1)S(1)}, bf16[336,128]{1,0:T(8,128)(2,1)S(1)}, u32[]{:S(2)}, u32[]{:S(2)}) collective-permute-start(bf16[336,128]{1,0:T(8,128)(2,1)S(1)} %get-tuple-element.26), channel_id=1, source_target_pairs={{0,752},{8,760},{16,0},{24,8},{32,16},{40,24},{48,32},{56,40},{64,... | collective-permute-start | bytes 258056 | tf_op jit(solution)/shard_map/ppermute | solution.py:34
  156.2 7.3 %collective-permute-start.5 = (bf16[336,128]{1,0:T(8,128)(2,1)S(1)}, bf16[336,128]{1,0:T(8,128)(2,1)S(1)}, u32[]{:S(2)}, u32[]{:S(2)}) collective-permute-start(bf16[336,128]{1,0:T(8,128)(2,1)S(1)} %get-tuple-element.27), channel_id=1, source_target_pairs={{0,744},{8,752},{16,760},{24,0},{32,8},{40,16},{48,24},{56,32},{64... | collective-permute-start | bytes 258056 | tf_op jit(solution)/shard_map/ppermute | solution.py:34

commit v6 on v2

--- a/solution.py
+++ b/solution.py
@@ -16,6 +16,9 @@
 OUT_ROWS = 7 * CAP + 16
 PART_ROWS = 3 * ROUTED + 2 * CAP + 16
 HOME_ROWS = 4 * CAP + 16
+HIDE_ROWS = 2 * ROUTED + 16
+SHARES = LOCAL // 2
+HALF_ROWS = SHARES * FEAT
 LEVELS = 15
 INTERPRET = False
 
@@ -29,6 +32,21 @@
     count = lax.axis_size(axis)
     pairs = [(source, (source + steps) % count) for source in range(count)]
     return lax.ppermute(value, axis, pairs)
+
+
+def swap(value):
+    nodes, count = lax.axis_size("node"), lax.axis_size("local")
+    pairs = []
+    for node in range(nodes):
+        for place in range(count):
+            step = 1 if place % 2 == node % 2 else -1
+            pairs.append((node * count + place, node * count + (place + step) % count))
+    return lax.ppermute(value, ("node", "local"), pairs)
+
+
+def half_of(weight, parity):
+    rows = weight.reshape(SHARES, 2, FEAT, HID)
+    return lax.dynamic_index_in_dim(rows, parity, 1, keepdims=False).reshape(HALF_ROWS, HID)
 
 
 def tables(route):
@@ -84,7 +102,7 @@
         out_refs[o][7 * CAP : OUT_ROWS, :] = levels
 
 
-def expert_kernel(got_ref, gate_ref, up_ref, down_ref, out_ref):
+def hidden_kernel(got_ref, gate_ref, up_ref, down_ref, out_ref):
     zero_cols = jnp.zeros((64, 2 * HID), bf16)
     zero_half = jnp.zeros((64, HID), bf16)
     pre = jnp.zeros((ROUTED, 2 * HID), f32)
@@ -130,8 +148,6 @@
     product = swish * up_pre * grad
     up_grad = (grad * swish).astype(bf16)
     pre_grad = (grad * up_pre * sigmoid * (1.0 + gate_pre * (1.0 - sigmoid))).astype(bf16)
-    hidden = jnp.concatenate([pre_grad, up_grad], axis=1)
-    paired = jnp.concatenate([hidden[0 : 2 * CAP], hidden[2 * CAP : 4 * CAP]], axis=1)
     line = lax.broadcasted_iota(jnp.int32, (16, LANE), 0)
     gate_rows = jnp.zeros((16, LANE), f32)
     for o in range(GROUP):
@@ -139,19 +155,55 @@
         total = lax.dot_general(
             jnp.ones((8, HID), f32), piece, NT, preferred_element_type=f32, precision=lax.Precision.HIGHEST
         )[0:1]
-        high = total.astype(bf16).astype(f32)
-        gate_rows = jnp.where(line == 2 * o, high, gate_rows)
-        gate_rows = jnp.where(line == 2 * o + 1, total - high, gate_rows)
+        gate_rows = with_gate(gate_rows, line, o, total)
+    out_ref[0:ROUTED, :] = pre_grad
+    out_ref[ROUTED : 2 * ROUTED, :] = up_grad
+    out_ref[2 * ROUTED : HIDE_ROWS, :] = gate_rows.astype(bf16)
+
+
+def with_gate(rows, line, o, total):
+    high = total.astype(bf16).astype(f32)
+    return jnp.where(line == 2 * o, high, jnp.where(line == 2 * o + 1, total - high, rows))
+
+
+def back_kernel(own_ref, other_ref, own_gate_ref, own_up_ref, other_ref_rows, out_ref):
+    zero_cols = jnp.zeros((64, 4 * HID), bf16)
+    hidden = jnp.concatenate(
+        [
+            own_ref[0:ROUTED, :],
+            own_ref[ROUTED : 2 * ROUTED, :],
+            other_ref[0:ROUTED, :],
+            other_ref[ROUTED : 2 * ROUTED, :],
+        ],
+        axis=1,
+    )
+    paired = jnp.concatenate([hidden[0 : 2 * CAP], hidden[2 * CAP : 4 * CAP]], axis=1)
+    own_gates = own_ref[2 * ROUTED : HIDE_ROWS, :].astype(f32)
+    other_gates = other_ref[2 * ROUTED : HIDE_ROWS, :].astype(f32)
+    line = lax.broadcasted_iota(jnp.int32, (16, LANE), 0)
+    gate_rows = jnp.zeros((16, LANE), f32)
+    for o in range(GROUP):
+        own = own_gates[2 * o : 2 * o + 1] + own_gates[2 * o + 1 : 2 * o + 2]
+        other = other_gates[2 * o : 2 * o + 1] + other_gates[2 * o + 1 : 2 * o + 2]
+        gate_rows = with_gate(gate_rows, line, o, own + other)
     gate_rows = gate_rows.astype(bf16)
-    for d in range(LOCAL):
+    for d in range(SHARES):
         low = d * FEAT
         base = d * PART_ROWS
-        both = jnp.concatenate([gate_ref[low : low + FEAT, :], up_ref[low : low + FEAT, :]], axis=1)
-        wide = lax.dot_general(hidden, both[0:384], NT, preferred_element_type=f32).astype(bf16)
+        weights = jnp.concatenate(
+            [
+                own_gate_ref[low : low + FEAT, :],
+                own_up_ref[low : low + FEAT, :],
+                other_ref_rows[low : low + FEAT, :],
+                other_ref_rows[HALF_ROWS + low : HALF_ROWS + low + FEAT, :],
+            ],
+            axis=1,
+        )
+        wide = lax.dot_general(hidden, weights[0:384], NT, preferred_element_type=f32).astype(bf16)
         for j in range(3):
             out_ref[base + j * ROUTED : base + (j + 1) * ROUTED, :] = wide[:, j * LANE : (j + 1) * LANE]
-        corner = jnp.concatenate([both[384:448], zero_cols], axis=1)
-        other = jnp.concatenate([zero_cols, both[384:448]], axis=1)
+        corner = jnp.concatenate([weights[384:448], zero_cols], axis=1)
+        other = jnp.concatenate([zero_cols, weights[384:448]], axis=1)
         ends = jnp.concatenate([corner, other], axis=0)
         tail = lax.dot_general(paired, ends, NT, preferred_element_type=f32).astype(bf16)
         out_ref[base + 3 * ROUTED : base + 3 * ROUTED + 2 * CAP, :] = tail
@@ -161,7 +213,7 @@
 def sum_kernel(part_ref, *out_refs):
     def total(start, rows):
         value = part_ref[start : start + rows, :].astype(f32)
-        for d in range(1, LOCAL):
+        for d in range(1, SHARES):
             value = value + part_ref[d * PART_ROWS + start : d * PART_ROWS + start + rows, :].astype(f32)
         return value
 
@@ -211,6 +263,10 @@
 
 def body(layer_input, output_grad, gate_weight, up_weight, down_weight, route_offset, gate_fixed):
     route = route_offset.T
+    parity = lax.axis_index("local") % 2
+    other_rows = swap(
+        jnp.concatenate([half_of(gate_weight[0], 1 - parity), half_of(up_weight[0], 1 - parity)], axis=0)
+    )
     packed = call(
         pack_kernel,
         [jax.ShapeDtypeStruct((OUT_ROWS, LANE), bf16)] * GROUP,
@@ -220,16 +276,30 @@
     )
     got = [packed[0]] + [from_behind(packed[o], "node", o) for o in range(1, GROUP)]
     shard = jnp.concatenate(got, axis=0).astype(jnp.float16)
+    shard, down_cols, kept_gate, kept_up = lax.optimization_barrier(
+        (shard, down_weight[0].T, half_of(gate_weight[0], parity), half_of(up_weight[0], parity))
+    )
     full = lax.all_gather(shard, "local", axis=0, tiled=True).astype(bf16)
-    partial = call(
-        expert_kernel,
-        jax.ShapeDtypeStruct((LOCAL * PART_ROWS, LANE), bf16),
+    hidden = call(
+        hidden_kernel,
+        jax.ShapeDtypeStruct((HIDE_ROWS, LANE), bf16),
         full,
         gate_weight[0],
         up_weight[0],
-        down_weight[0].T,
-    )
-    shares = lax.all_to_all(partial, "local", 0, 0, tiled=True)
+        down_cols,
+    )
+    other_hidden = swap(hidden)
+    partial = call(
+        back_kernel,
+        jax.ShapeDtypeStruct((SHARES * PART_ROWS, LANE), bf16),
+        hidden,
+        other_hidden,
+        kept_gate,
+        kept_up,
+        other_rows,
+    )
+    groups = [[2 * place + odd for place in range(SHARES)] for odd in range(2)]
+    shares = lax.all_to_all(partial, "local", 0, 0, tiled=True, axis_index_groups=groups)
     summed = call(sum_kernel, [jax.ShapeDtypeStruct((HOME_ROWS, LANE), bf16)] * GROUP, shares)
     home = [summed[0]] + [from_behind(summed[o], "node", -o) for o in range(1, GROUP)]
     input_grad, gate_grad = call(

time: 162 us -> 149 us (0.920)
  blocking collectives: 110 us -> 83.4 us
  starting transfers between devices: 20.5 us -> 36.4 us
  waiting for transfers between devices: 19.9 us -> 13.7 us
  other arithmetic: 0.67 us -> 2.64 us
    all_to_all x1, blocking collectives: 59.9 us -> 33.3 us  [body(): lax.all_to_all(partial, 'local', 0, 0, tiled=True, axis_index_groups=groups)]
    ppermute x6, waiting for transfers between devices: 19.9 us -> 9.91 us  [from_behind(): return lax.ppermute(value, axis, pairs)]
    ppermute x0 -> x2, starting transfers between devices: none -> 8.61 us  [swap(): return lax.ppermute(value, ('node', 'local'), pairs)]
    ppermute x6, starting transfers between devices: 20.5 us -> 27.7 us  [from_behind(): return lax.ppermute(value, axis, pairs)]
    ppermute x0 -> x2, waiting for transfers between devices: none -> 3.8 us  [swap(): return lax.ppermute(value, ('node', 'local'), pairs)]
    pallas_call x4 -> x5, Pallas kernels: 4.81 us -> 4.81 us  [call(): pl.pallas_call(kernel, out_shape=outs, interpret=INTERPRET, compiler_para...]
  transfers between devices with their start and end apart: 6 -> 8, of which waited for: 5 -> 4; matrix products, arithmetic and copies ran while one was open for 1% -> 4% of each run, Pallas kernels for 0% -> 1%
where the time goes in v6:
time: 149 us; the launch traced here: 148 us
  blocking collectives  83.4 us (56%)
  starting transfers between devices  36.4 us (24%)
  waiting for transfers between devices  13.7 us (9%)
  local copies, waits for them, and re-layouts  6.52 us (4%)
  Pallas kernels  4.81 us (3%)
  other arithmetic  2.64 us (2%)
    all_gather x1, blocking collectives, body(): full = lax.all_gather(shard, 'local', axis=0, tiled=True).astype(bf16)  50.1 us
    all_to_all x1, blocking collectives, body(): lax.all_to_all(partial, 'local', 0, 0, tiled=True, axis_index_groups=groups)  33.3 us
    ppermute x6, starting transfers between devices, from_behind(): return lax.ppermute(value, axis, pairs)  27.7 us
    ppermute x6, waiting for transfers between devices, from_behind(): return lax.ppermute(value, axis, pairs)  9.91 us
    ppermute x2, starting transfers between devices, swap(): return lax.ppermute(value, ('node', 'local'), pairs)  8.61 us
    unnamed x15, local copies, waits for them, and re-layouts  4.93 us
    pallas_call x5, Pallas kernels, call(): pl.pallas_call(kernel, out_shape=outs, interpret=INTERPRET, compiler_para...  4.81 us
    ppermute x2, waiting for transfers between devices, swap(): return lax.ppermute(value, ('node', 'local'), pairs)  3.8 us
  transfers between devices with their start and end apart: 8, of which 4 were waited for; matrix products, arithmetic and copies ran while one was open for 4% of the time, Pallas kernels for 1%

profile of v6, /device:TPU:1, one launch (start us, length us, event | category | flops | bytes accessed | tf_op | source)
XLA Modules:
  0.0 148.2 jit_solution(9057866933259627137)
XLA Ops:
  0.6 0.0 copy-start.2
  0.6 0.9 copy-done.2
  1.5 0.0 copy-start.3
  1.5 0.9 copy-done.3
  2.4 0.0 copy-start.4
  2.4 0.7 copy-done.4
  3.1 0.4 shard_map.86
  3.6 4.5 %collective-permute-start = (bf16[576,128]{1,0:T(8,128)(2,1)S(1)}, bf16[576,128]{1,0:T(8,128)(2,1)S(1)}, u32[]{:S(2)}, u32[]{:S(2)}) collective-permute-start(bf16[576,128]{1,0:T(8,128)(2,1)S(1)} %get-tuple-element.17), channel_id=1, source_target_pairs={{0,8},{8,16},{16,24},{24,32},{32,40},{40,48},{48,56},{56,64},{64,7... | collective-permute-start | bytes 442376 | tf_op jit(solution)/shard_map/ppermute | solution.py:34
  8.1 3.1 %collective-permute-start.1 = (bf16[576,128]{1,0:T(8,128)(2,1)S(1)}, bf16[576,128]{1,0:T(8,128)(2,1)}, u32[]{:S(2)}, u32[]{:S(2)}) collective-permute-start(bf16[576,128]{1,0:T(8,128)(2,1)S(1)} %get-tuple-element.18), channel_id=1, source_target_pairs={{0,16},{8,24},{16,32},{24,40},{32,48},{40,56},{48,64},{56,72},{64,... | collective-permute-start | bytes 442376 | tf_op jit(solution)/shard_map/ppermute | solution.py:34
  11.2 3.4 %collective-permute-start.2 = (bf16[576,128]{1,0:T(8,128)(2,1)S(1)}, bf16[576,128]{1,0:T(8,128)(2,1)}, u32[]{:S(2)}, u32[]{:S(2)}) collective-permute-start(bf16[576,128]{1,0:T(8,128)(2,1)S(1)} %get-tuple-element.19), channel_id=1, source_target_pairs={{0,24},{8,32},{16,40},{24,48},{32,56},{40,64},{48,72},{56,80},{64,... | collective-permute-start | bytes 442376 | tf_op jit(solution)/shard_map/ppermute | solution.py:34
  14.7 1.6 %constant_dynamic-slice_fusion = (bf16[4,1,448,128]{3,2,1,0:T(8,128)(2,1)S(1)}, bf16[4,1,448,128]{3,2,1,0:T(8,128)(2,1)S(1)}, bf16[4,1,448,128]{3,2,1,0:T(8,128)(2,1)S(1)}, bf16[4,1,448,128]{3,2,1,0:T(8,128)(2,1)S(1)}) fusion(bf16[4,2,448,128]{3,2,1,0:T(8,128)(2,1)} %bitcast.32, s32[]{:T(128)S(6)} %select_n.18, s32[]{:T(128)S(6)} %select_n.17, ...), kind=kLoop, calls=%fused_computation.2 | loop fusion | bytes 3670024 | tf_op jit(solution)/shard_map/jit(dynamic_index_in_dim)/dynamic_slice | solution.py:49
  16.3 1.0 pad_maximum_fusion
  17.3 5.1 %collective-permute-start.4 = (bf16[3584,128]{1,0:T(8,128)(2,1)}, bf16[3584,128]{1,0:T(8,128)(2,1)S(1)}, u32[]{:S(2)}, u32[]{:S(2)}) collective-permute-start(bf16[3584,128]{1,0:T(8,128)(2,1)} %pad_maximum_fusion), channel_id=1, source_target_pairs={{0,1},{1,0},{2,3},{3,2},{4,5},{5,4},{6,7},{7,6},{8,15},{9,10},{10,... | collective-permute-start | bytes 2752520 | tf_op jit(solution)/shard_map/ppermute | solution.py:44
  22.3 1.6 %copy.9 = bf16[1,128,3584]{1,2,0:T(8,128)(2,1)S(1)} copy(bf16[1,128,3584]{2,1,0:T(8,128)(2,1)} %param.11) | data formatting | bytes 1835008 | tf_op args[4]
  23.9 0.0 collective-permute-done
  23.9 2.5 %collective-permute-done.1 = bf16[576,128]{1,0:T(8,128)(2,1)} collective-permute-done((bf16[576,128]{1,0:T(8,128)(2,1)S(1)}, bf16[576,128]{1,0:T(8,128)(2,1)}, u32[]{:S(2)}, u32[]{:S(2)}) %collective-permute-start.1) | collective-permute-done | bytes 147488 | tf_op jit(solution)/shard_map/ppermute | solution.py:34
  26.5 4.4 %collective-permute-done.2 = bf16[576,128]{1,0:T(8,128)(2,1)} collective-permute-done((bf16[576,128]{1,0:T(8,128)(2,1)S(1)}, bf16[576,128]{1,0:T(8,128)(2,1)}, u32[]{:S(2)}, u32[]{:S(2)}) %collective-permute-start.2) | collective-permute-done | bytes 147488 | tf_op jit(solution)/shard_map/ppermute | solution.py:34
  30.9 1.1 maximum_convert_fusion
  32.0 50.1 %all-gather.1 = f16[18432,128]{1,0:T(8,128)(2,1)S(1)} all-gather(f16[2304,128]{1,0:T(8,128)(2,1)S(1)} %maximum_convert_fusion), channel_id=1, replica_groups=mesh['node'=96,'local'=8] {'local'}, dimensions={0}, use_global_device_ids=true | all-gather | bytes 5308416 | tf_op jit(solution)/shard_map/all_gather | solution.py:282
  82.1 0.0 copy-start
  82.1 0.0 copy-start.1
  82.1 0.5 convert_element_type.7.got_ref
  82.7 0.6 copy-done
  83.3 0.3 copy-done.1
  83.6 1.9 %shard_map.87.own_ref = bf16[656,128]{1,0:T(8,128)(2,1)S(1)} custom-call(bf16[18432,128]{1,0:T(8,128)(2,1)S(1)} %convert_element_type.7.got_ref, bf16[3584,128]{1,0:T(8,128)(2,1)S(1)} %bitcast.31, bf16[3584,128]{1,0:T(8,128)(2,1)S(1)} %bitcast.33, bf16[3584,128]{1,0:T(8,128)(2,1)S(1)} %bitcast.29), custom_call_target="tpu_custom_call" | custom-call | tf_op jit(solution)/shard_map/pallas_call | solution.py:261
  85.5 3.5 %collective-permute-start.3 = (bf16[656,128]{1,0:T(8,128)(2,1)S(1)}, bf16[656,128]{1,0:T(8,128)(2,1)S(1)}, u32[]{:S(2)}, u32[]{:S(2)}) collective-permute-start(bf16[656,128]{1,0:T(8,128)(2,1)S(1)} %shard_map.87.own_ref), channel_id=1, source_target_pairs={{0,1},{1,0},{2,3},{3,2},{4,5},{5,4},{6,7},{7,6},{8,15},{9,10},{10,... | collective-permute-start | bytes 503816 | tf_op jit(solution)/shard_map/ppermute | solution.py:44
  89.0 3.8 %collective-permute-done.3.other_ref = bf16[656,128]{1,0:T(8,128)(2,1)S(1)} collective-permute-done((bf16[656,128]{1,0:T(8,128)(2,1)S(1)}, bf16[656,128]{1,0:T(8,128)(2,1)S(1)}, u32[]{:S(2)}, u32[]{:S(2)}) %collective-permute-start.3) | collective-permute-done | bytes 167968 | tf_op jit(solution)/shard_map/ppermute | solution.py:44
  92.8 0.0 collective-permute-done.4.other_ref_rows
  92.8 1.2 shard_map.88
  94.0 0.0 copy-start.5
  94.0 0.0 copy-start.6
  94.0 33.3 %all_to_all.11 = bf16[4,1136,128]{2,1,0:T(8,128)(2,1)S(1)} all-to-all(bf16[4,1136,128]{2,1,0:T(8,128)(2,1)S(1)} %bitcast.27), channel_id=1, replica_groups={{0,2,4,6},{1,3,5,7},{8,10,12,14},{9,11,13,15},{16,18,20,22},{17,19,21,2..., dimensions={0} | all-to-all | bytes 2326528 | tf_op jit(solution)/shard_map/all_to_all | solution.py:302
  127.3 0.2 shard_map.89
  127.5 3.5 %collective-permute-start.5 = (bf16[336,128]{1,0:T(8,128)(2,1)S(1)}, bf16[336,128]{1,0:T(8,128)(2,1)S(1)}, u32[]{:S(2)}, u32[]{:S(2)}) collective-permute-start(bf16[336,128]{1,0:T(8,128)(2,1)S(1)} %get-tuple-element.25), channel_id=1, source_target_pairs={{0,760},{8,0},{16,8},{24,16},{32,24},{40,32},{48,40},{56,48},{64,5... | collective-permute-start | bytes 258056 | tf_op jit(solution)/shard_map/ppermute | solution.py:34
  131.0 8.9 %collective-permute-start.6 = (bf16[336,128]{1,0:T(8,128)(2,1)S(1)}, bf16[336,128]{1,0:T(8,128)(2,1)S(1)}, u32[]{:S(2)}, u32[]{:S(2)}) collective-permute-start(bf16[336,128]{1,0:T(8,128)(2,1)S(1)} %get-tuple-element.26), channel_id=1, source_target_pairs={{0,752},{8,760},{16,0},{24,8},{32,16},{40,24},{48,32},{56,40},{64,... | collective-permute-start | bytes 258056 | tf_op jit(solution)/shard_map/ppermute | solution.py:34
  139.8 4.3 %collective-permute-start.7 = (bf16[336,128]{1,0:T(8,128)(2,1)S(1)}, bf16[336,128]{1,0:T(8,128)(2,1)S(1)}, u32[]{:S(2)}, u32[]{:S(2)}) collective-permute-start(bf16[336,128]{1,0:T(8,128)(2,1)S(1)} %get-tuple-element.27), channel_id=1, source_target_pairs={{0,744},{8,752},{16,760},{24,0},{32,8},{40,16},{48,24},{56,32},{64... | collective-permute-start | bytes 258056 | tf_op jit(solution)/shard_map/ppermute | solution.py:34
  144.2 0.0 collective-permute-done.5.refs_1_
  144.2 0.0 collective-permute-done.6.refs_2_
  144.2 3.0 %collective-permute-done.7.refs_3_ = bf16[336,128]{1,0:T(8,128)(2,1)S(1)} collective-permute-done((bf16[336,128]{1,0:T(8,128)(2,1)S(1)}, bf16[336,128]{1,0:T(8,128)(2,1)S(1)}, u32[]{:S(2)}, u32[]{:S(2)}) %collective-permute-start.7) | collective-permute-done | bytes 86048 | tf_op jit(solution)/shard_map/ppermute | solution.py:34
  147.2 0.0 copy-done.5
  147.2 0.0 copy-done.6
  147.2 1.1 shard_map.90
Async XLA Ops:
  0.6 0.9 copy-start.2
  1.5 0.9 copy-start.3
  2.4 0.7 copy-start.4
  3.6 20.4 %collective-permute-start = (bf16[576,128]{1,0:T(8,128)(2,1)S(1)}, bf16[576,128]{1,0:T(8,128)(2,1)S(1)}, u32[]{:S(2)}, u32[]{:S(2)}) collective-permute-start(bf16[576,128]{1,0:T(8,128)(2,1)S(1)} %get-tuple-element.17), channel_id=1, source_target_pairs={{0,8},{8,16},{16,24},{24,32},{32,40},{40,48},{48,56},{56,64},{64,7... | collective-permute-start | bytes 442376 | tf_op jit(solution)/shard_map/ppermute | solution.py:34
  8.1 18.4 %collective-permute-start.1 = (bf16[576,128]{1,0:T(8,128)(2,1)S(1)}, bf16[576,128]{1,0:T(8,128)(2,1)}, u32[]{:S(2)}, u32[]{:S(2)}) collective-permute-start(bf16[576,128]{1,0:T(8,128)(2,1)S(1)} %get-tuple-element.18), channel_id=1, source_target_pairs={{0,16},{8,24},{16,32},{24,40},{32,48},{40,56},{48,64},{56,72},{64,... | collective-permute-start | bytes 442376 | tf_op jit(solution)/shard_map/ppermute | solution.py:34
  11.2 19.7 %collective-permute-start.2 = (bf16[576,128]{1,0:T(8,128)(2,1)S(1)}, bf16[576,128]{1,0:T(8,128)(2,1)}, u32[]{:S(2)}, u32[]{:S(2)}) collective-permute-start(bf16[576,128]{1,0:T(8,128)(2,1)S(1)} %get-tuple-element.19), channel_id=1, source_target_pairs={{0,24},{8,32},{16,40},{24,48},{32,56},{40,64},{48,72},{56,80},{64,... | collective-permute-start | bytes 442376 | tf_op jit(solution)/shard_map/ppermute | solution.py:34
  17.3 75.5 %collective-permute-start.4 = (bf16[3584,128]{1,0:T(8,128)(2,1)}, bf16[3584,128]{1,0:T(8,128)(2,1)S(1)}, u32[]{:S(2)}, u32[]{:S(2)}) collective-permute-start(bf16[3584,128]{1,0:T(8,128)(2,1)} %pad_maximum_fusion), channel_id=1, source_target_pairs={{0,1},{1,0},{2,3},{3,2},{4,5},{5,4},{6,7},{7,6},{8,15},{9,10},{10,... | collective-permute-start | bytes 2752520 | tf_op jit(solution)/shard_map/ppermute | solution.py:44
  82.1 1.2 copy-start
  82.1 1.5 copy-start.1
  85.5 7.3 %collective-permute-start.3 = (bf16[656,128]{1,0:T(8,128)(2,1)S(1)}, bf16[656,128]{1,0:T(8,128)(2,1)S(1)}, u32[]{:S(2)}, u32[]{:S(2)}) collective-permute-start(bf16[656,128]{1,0:T(8,128)(2,1)S(1)} %shard_map.87.own_ref), channel_id=1, source_target_pairs={{0,1},{1,0},{2,3},{3,2},{4,5},{5,4},{6,7},{7,6},{8,15},{9,10},{10,... | collective-permute-start | bytes 503816 | tf_op jit(solution)/shard_map/ppermute | solution.py:44
  94.0 53.2 %copy-start.5 = (s32[128,2]{0,1:T(2,128)S(1)}, s32[128,2]{0,1:T(2,128)}, u32[]{:S(2)}) copy-start(s32[128,2]{0,1:T(2,128)} %param.12) | copy-start | bytes 3076
  94.0 53.1 %copy-start.6 = (s32[128,2]{0,1:T(2,128)S(1)}, s32[128,2]{0,1:T(2,128)}, u32[]{:S(2)}) copy-start(s32[128,2]{0,1:T(2,128)} %param.13) | copy-start | bytes 3076
  127.5 16.7 %collective-permute-start.5 = (bf16[336,128]{1,0:T(8,128)(2,1)S(1)}, bf16[336,128]{1,0:T(8,128)(2,1)S(1)}, u32[]{:S(2)}, u32[]{:S(2)}) collective-permute-start(bf16[336,128]{1,0:T(8,128)(2,1)S(1)} %get-tuple-element.25), channel_id=1, source_target_pairs={{0,760},{8,0},{16,8},{24,16},{32,24},{40,32},{48,40},{56,48},{64,5... | collective-permute-start | bytes 258056 | tf_op jit(solution)/shard_map/ppermute | solution.py:34
  131.0 13.2 %collective-permute-start.6 = (bf16[336,128]{1,0:T(8,128)(2,1)S(1)}, bf16[336,128]{1,0:T(8,128)(2,1)S(1)}, u32[]{:S(2)}, u32[]{:S(2)}) collective-permute-start(bf16[336,128]{1,0:T(8,128)(2,1)S(1)} %get-tuple-element.26), channel_id=1, source_target_pairs={{0,752},{8,760},{16,0},{24,8},{32,16},{40,24},{48,32},{56,40},{64,... | collective-permute-start | bytes 258056 | tf_op jit(solution)/shard_map/ppermute | solution.py:34
  139.8 7.3 %collective-permute-start.7 = (bf16[336,128]{1,0:T(8,128)(2,1)S(1)}, bf16[336,128]{1,0:T(8,128)(2,1)S(1)}, u32[]{:S(2)}, u32[]{:S(2)}) collective-permute-start(bf16[336,128]{1,0:T(8,128)(2,1)S(1)} %get-tuple-element.27), channel_id=1, source_target_pairs={{0,744},{8,752},{16,760},{24,0},{32,8},{40,16},{48,24},{56,32},{64... | collective-permute-start | bytes 258056 | tf_op jit(solution)/shard_map/ppermute | solution.py:34

commit v7 on v6

--- a/solution.py
+++ b/solution.py
@@ -14,6 +14,7 @@
 LOCAL = 8
 ROUTED = GROUP * CAP
 OUT_ROWS = 7 * CAP + 16
+SHARD_ROWS = GROUP * 7 * CAP + 16
 PART_ROWS = 3 * ROUTED + 2 * CAP + 16
 HOME_ROWS = 4 * CAP + 16
 HIDE_ROWS = 2 * ROUTED + 16
@@ -34,19 +35,36 @@
     return lax.ppermute(value, axis, pairs)
 
 
-def swap(value):
+def beside(core, place):
+    return (place + 1 - 2 * ((place + core) & 1)) & 7
+
+
+def across(core, place):
+    return ((((place - 2 * core) & 7) ^ 2) + 2 * core) & 7
+
+
+def swap(value, partner, turn):
     nodes, count = lax.axis_size("node"), lax.axis_size("local")
-    pairs = []
-    for node in range(nodes):
-        for place in range(count):
-            step = 1 if place % 2 == node % 2 else -1
-            pairs.append((node * count + place, node * count + (place + step) % count))
+    pairs = [
+        (node * count + place, node * count + partner((node + turn) & 1, place))
+        for node in range(nodes)
+        for place in range(count)
+    ]
     return lax.ppermute(value, ("node", "local"), pairs)
 
 
-def half_of(weight, parity):
-    rows = weight.reshape(SHARES, 2, FEAT, HID)
-    return lax.dynamic_index_in_dim(rows, parity, 1, keepdims=False).reshape(HALF_ROWS, HID)
+def targets(core, place):
+    return place, across(1 - core, place), across(core, place), (place + 4) & 7
+
+
+def pick_kernel(where_ref, gate_ref, up_ref, out_ref):
+    core = where_ref[0] & 1
+    theirs = targets(core, beside(core, where_ref[1]))
+    for turn in range(SHARES):
+        start = pl.multiple_of(theirs[turn] * FEAT, 64)
+        low = turn * FEAT
+        out_ref[low : low + FEAT, :] = gate_ref[pl.ds(start, FEAT), :]
+        out_ref[HALF_ROWS + low : HALF_ROWS + low + FEAT, :] = up_ref[pl.ds(start, FEAT), :]
 
 
 def tables(route):
@@ -97,9 +115,9 @@
         for o in range(GROUP):
             out_refs[o][place * CAP : (place + 1) * CAP, :] = packed[o * CAP : (o + 1) * CAP]
     line = lax.broadcasted_iota(jnp.int32, (16, LANE), 0)
-    levels = jnp.where(line == 0, level_in, jnp.where(line == 1, level_grad, 0.0)).astype(bf16)
-    for o in range(GROUP):
-        out_refs[o][7 * CAP : OUT_ROWS, :] = levels
+    for o in range(GROUP):
+        levels = jnp.where(line == 2 * o, level_in, jnp.where(line == 2 * o + 1, level_grad, 0.0))
+        out_refs[o][7 * CAP : OUT_ROWS, :] = levels.astype(bf16)
 
 
 def hidden_kernel(got_ref, gate_ref, up_ref, down_ref, out_ref):
@@ -109,7 +127,7 @@
     grad = jnp.zeros((ROUTED, HID), f32)
 
     def rows_of(d, o, place):
-        start = d * GROUP * OUT_ROWS + o * OUT_ROWS + place * CAP
+        start = d * SHARD_ROWS + (o * 7 + place) * CAP
         return got_ref[start : start + CAP, :]
 
     def column(d, place):
@@ -132,11 +150,10 @@
         part_grad = part_grad + jnp.dot(grad_b, down_b, preferred_element_type=f32)
         back_in = []
         back_grad = []
+        levels = got_ref[(d + 1) * SHARD_ROWS - 16 : (d + 1) * SHARD_ROWS, :].astype(f32)
         for o in range(GROUP):
-            start = d * GROUP * OUT_ROWS + o * OUT_ROWS + 7 * CAP
-            levels = got_ref[start : start + 16, :].astype(f32)
-            inverse_in = power_of(levels[0:1], -1)
-            inverse_grad = power_of(levels[1:2], -1)
+            inverse_in = power_of(levels[2 * o : 2 * o + 1], -1)
+            inverse_grad = power_of(levels[2 * o + 1 : 2 * o + 2], -1)
             back_in.append(part[o * CAP : (o + 1) * CAP] * jnp.concatenate([inverse_in, inverse_in], axis=1))
             back_grad.append(part_grad[o * CAP : (o + 1) * CAP] * inverse_grad)
         pre = pre + jnp.concatenate(back_in, axis=0)
@@ -166,7 +183,8 @@
     return jnp.where(line == 2 * o, high, jnp.where(line == 2 * o + 1, total - high, rows))
 
 
-def back_kernel(own_ref, other_ref, own_gate_ref, own_up_ref, other_ref_rows, out_ref):
+def back_kernel(where_ref, own_ref, other_ref, own_gate_ref, own_up_ref, other_ref_rows, kept_ref, sent_ref):
+    mine = targets(where_ref[0] & 1, where_ref[1])
     zero_cols = jnp.zeros((64, 4 * HID), bf16)
     hidden = jnp.concatenate(
         [
@@ -186,36 +204,49 @@
         own = own_gates[2 * o : 2 * o + 1] + own_gates[2 * o + 1 : 2 * o + 2]
         other = other_gates[2 * o : 2 * o + 1] + other_gates[2 * o + 1 : 2 * o + 2]
         gate_rows = with_gate(gate_rows, line, o, own + other)
-    gate_rows = gate_rows.astype(bf16)
     for d in range(SHARES):
         low = d * FEAT
-        base = d * PART_ROWS
+        base = d % 2 * PART_ROWS
+        out_ref = kept_ref if d < 2 else sent_ref
+        kind = f32 if d < 2 else bf16
+        start = pl.multiple_of(mine[d] * FEAT, 64)
         weights = jnp.concatenate(
             [
-                own_gate_ref[low : low + FEAT, :],
-                own_up_ref[low : low + FEAT, :],
+                own_gate_ref[pl.ds(start, FEAT), :],
+                own_up_ref[pl.ds(start, FEAT), :],
                 other_ref_rows[low : low + FEAT, :],
                 other_ref_rows[HALF_ROWS + low : HALF_ROWS + low + FEAT, :],
             ],
             axis=1,
         )
-        wide = lax.dot_general(hidden, weights[0:384], NT, preferred_element_type=f32).astype(bf16)
+        wide = lax.dot_general(hidden, weights[0:384], NT, preferred_element_type=f32).astype(kind)
         for j in range(3):
             out_ref[base + j * ROUTED : base + (j + 1) * ROUTED, :] = wide[:, j * LANE : (j + 1) * LANE]
         corner = jnp.concatenate([weights[384:448], zero_cols], axis=1)
         other = jnp.concatenate([zero_cols, weights[384:448]], axis=1)
         ends = jnp.concatenate([corner, other], axis=0)
-        tail = lax.dot_general(paired, ends, NT, preferred_element_type=f32).astype(bf16)
+        tail = lax.dot_general(paired, ends, NT, preferred_element_type=f32).astype(kind)
         out_ref[base + 3 * ROUTED : base + 3 * ROUTED + 2 * CAP, :] = tail
-        out_ref[base + 3 * ROUTED + 2 * CAP : base + PART_ROWS, :] = gate_rows
-
-
-def sum_kernel(part_ref, *out_refs):
+        out_ref[base + 3 * ROUTED + 2 * CAP : base + PART_ROWS, :] = gate_rows.astype(kind)
+
+
+def merge_kernel(kept_ref, got_ref, own_ref, sent_ref):
+    last = PART_ROWS - 16
+    own_ref[...] = kept_ref[0:PART_ROWS, :] + got_ref[0:PART_ROWS, :].astype(f32)
+    sent_ref[0:last, :] = (
+        kept_ref[PART_ROWS : PART_ROWS + last, :] + got_ref[PART_ROWS : PART_ROWS + last, :].astype(f32)
+    ).astype(bf16)
+    gates = kept_ref[PART_ROWS + last :, :] + got_ref[PART_ROWS + last :, :].astype(f32)
+    line = lax.broadcasted_iota(jnp.int32, (16, LANE), 0)
+    rows = jnp.zeros((16, LANE), f32)
+    for o in range(GROUP):
+        rows = with_gate(rows, line, o, gates[2 * o : 2 * o + 1] + gates[2 * o + 1 : 2 * o + 2])
+    sent_ref[last:PART_ROWS, :] = rows.astype(bf16)
+
+
+def sum_kernel(own_ref, got_ref, *out_refs):
     def total(start, rows):
-        value = part_ref[start : start + rows, :].astype(f32)
-        for d in range(1, SHARES):
-            value = value + part_ref[d * PART_ROWS + start : d * PART_ROWS + start + rows, :].astype(f32)
-        return value
+        return own_ref[start : start + rows, :] + got_ref[start : start + rows, :].astype(f32)
 
     for j in range(3):
         for o in range(GROUP):
@@ -257,16 +288,29 @@
     gate_ref[...] = gate
 
 
-def call(kernel, outs, *args):
-    return pl.pallas_call(kernel, out_shape=outs, interpret=INTERPRET, compiler_params=pltpu.CompilerParams(vmem_limit_bytes=24 * 1024 * 1024))(*args)
+def call(kernel, outs, *args, scalars=0):
+    spaces = [pltpu.SMEM if number < scalars else pltpu.VMEM for number in range(len(args))]
+    return pl.pallas_call(
+        kernel,
+        out_shape=outs,
+        in_specs=[pl.BlockSpec(memory_space=space) for space in spaces],
+        interpret=INTERPRET,
+        compiler_params=pltpu.CompilerParams(vmem_limit_bytes=24 * 1024 * 1024),
+    )(*args)
 
 
 def body(layer_input, output_grad, gate_weight, up_weight, down_weight, route_offset, gate_fixed):
     route = route_offset.T
-    parity = lax.axis_index("local") % 2
-    other_rows = swap(
-        jnp.concatenate([half_of(gate_weight[0], 1 - parity), half_of(up_weight[0], 1 - parity)], axis=0)
-    )
+    where = jnp.stack([lax.axis_index("node"), lax.axis_index("local")])
+    picked = call(
+        pick_kernel,
+        jax.ShapeDtypeStruct((2 * HALF_ROWS, HID), bf16),
+        where,
+        gate_weight[0],
+        up_weight[0],
+        scalars=1,
+    )
+    other_rows = swap(picked, beside, 0)
     packed = call(
         pack_kernel,
         [jax.ShapeDtypeStruct((OUT_ROWS, LANE), bf16)] * GROUP,
@@ -275,10 +319,9 @@
         output_grad.T,
     )
     got = [packed[0]] + [from_behind(packed[o], "node", o) for o in range(1, GROUP)]
-    shard = jnp.concatenate(got, axis=0).astype(jnp.float16)
-    shard, down_cols, kept_gate, kept_up = lax.optimization_barrier(
-        (shard, down_weight[0].T, half_of(gate_weight[0], parity), half_of(up_weight[0], parity))
-    )
+    levels = got[0][7 * CAP :] + got[1][7 * CAP :] + got[2][7 * CAP :] + got[3][7 * CAP :]
+    shard = jnp.concatenate([value[: 7 * CAP] for value in got] + [levels], axis=0).astype(jnp.float16)
+    shard, down_cols = lax.optimization_barrier((shard, down_weight[0].T))
     full = lax.all_gather(shard, "local", axis=0, tiled=True).astype(bf16)
     hidden = call(
         hidden_kernel,
@@ -288,19 +331,30 @@
         up_weight[0],
         down_cols,
     )
-    other_hidden = swap(hidden)
-    partial = call(
+    other_hidden = swap(hidden, beside, 0)
+    kept, sent = call(
         back_kernel,
-        jax.ShapeDtypeStruct((SHARES * PART_ROWS, LANE), bf16),
+        [jax.ShapeDtypeStruct((2 * PART_ROWS, LANE), f32), jax.ShapeDtypeStruct((2 * PART_ROWS, LANE), bf16)],
+        where,
         hidden,
         other_hidden,
-        kept_gate,
-        kept_up,
+        gate_weight[0],
+        up_weight[0],
         other_rows,
-    )
-    groups = [[2 * place + odd for place in range(SHARES)] for odd in range(2)]
-    shares = lax.all_to_all(partial, "local", 0, 0, tiled=True, axis_index_groups=groups)
-    summed = call(sum_kernel, [jax.ShapeDtypeStruct((HOME_ROWS, LANE), bf16)] * GROUP, shares)
+        scalars=1,
+    )
+    own_share, far_share = call(
+        merge_kernel,
+        [jax.ShapeDtypeStruct((PART_ROWS, LANE), f32), jax.ShapeDtypeStruct((PART_ROWS, LANE), bf16)],
+        kept,
+        swap(sent, across, 0),
+    )
+    summed = call(
+        sum_kernel,
+        [jax.ShapeDtypeStruct((HOME_ROWS, LANE), bf16)] * GROUP,
+        own_share,
+        swap(far_share, across, 1),
+    )
     home = [summed[0]] + [from_behind(summed[o], "node", -o) for o in range(1, GROUP)]
     input_grad, gate_grad = call(
         unpack_kernel,

time: 149 us -> 147 us (0.987)
  blocking collectives: 83.4 us -> 49.2 us
  waiting for transfers between devices: 13.7 us -> 34.9 us
  starting transfers between devices: 36.4 us -> 44.2 us
  local copies, waits for them, and re-layouts: 6.52 us -> 9.24 us
    all_to_all x1 -> x0, blocking collectives: 33.3 us -> none  [body(): lax.all_to_all(partial, 'local', 0, 0, tiled=True, axis_index_groups=groups)]
    ppermute x2 -> x4, waiting for transfers between devices: 3.8 us -> 25.6 us  [swap(): return lax.ppermute(value, ('node', 'local'), pairs)]
    ppermute x2 -> x4, starting transfers between devices: 8.61 us -> 14.7 us  [swap(): return lax.ppermute(value, ('node', 'local'), pairs)]
    unnamed x15 -> x23, local copies, waits for them, and re-layouts: 4.93 us -> 9.24 us
    ppermute x6, starting transfers between devices: 27.7 us -> 29.5 us  [from_behind(): return lax.ppermute(value, axis, pairs)]
    dynamic_slice x1 -> x0, local copies, waits for them, and re-layouts: 1.59 us -> none  [half_of(): lax.dynamic_index_in_dim(rows, parity, 1, keepdims=False)]
    pallas_call x5 -> x7, Pallas kernels: 4.81 us -> 6.08 us  [call(): pl.pallas_call(kernel, out_shape=outs, in_specs=[pl.BlockSpec(memory_spac...]
  transfers between devices with their start and end apart: 8 -> 10, of which waited for: 4 -> 6; matrix products, arithmetic and copies ran while one was open for 4% -> 3% of each run, Pallas kernels for 1% -> 2%
where the time goes in v7:
time: 147 us; the launch traced here: 146 us
  blocking collectives  49.2 us (33%)
  starting transfers between devices  44.2 us (30%)
  waiting for transfers between devices  34.9 us (24%)
  local copies, waits for them, and re-layouts  9.24 us (6%)
  Pallas kernels  6.08 us (4%)
    all_gather x1, blocking collectives, body(): full = lax.all_gather(shard, 'local', axis=0, tiled=True).astype(bf16)  49.2 us
    ppermute x6, starting transfers between devices, from_behind(): return lax.ppermute(value, axis, pairs)  29.5 us
    ppermute x4, waiting for transfers between devices, swap(): return lax.ppermute(value, ('node', 'local'), pairs)  25.6 us
    ppermute x4, starting transfers between devices, swap(): return lax.ppermute(value, ('node', 'local'), pairs)  14.7 us
    ppermute x6, waiting for transfers between devices, from_behind(): return lax.ppermute(value, axis, pairs)  9.29 us
    unnamed x23, local copies, waits for them, and re-layouts  9.24 us
    pallas_call x7, Pallas kernels, call(): pl.pallas_call(kernel, out_shape=outs, in_specs=[pl.BlockSpec(memory_spac...  6.08 us
  transfers between devices with their start and end apart: 10, of which 6 were waited for; matrix products, arithmetic and copies ran while one was open for 3% of the time, Pallas kernels for 2%

profile of v7, /device:TPU:1, one launch (start us, length us, event | category | flops | bytes accessed | tf_op | source)
XLA Modules:
  0.0 145.9 jit_solution(410550535426343254)
XLA Ops:
  0.6 0.0 copy-start.4
  0.6 0.9 copy-done.4
  1.5 0.0 copy-start.5
  1.5 0.9 copy-done.5
  2.4 0.0 copy-start.6
  2.4 0.7 copy-done.6
  3.1 0.5 shard_map.86
  3.6 4.5 %collective-permute-start = (bf16[576,128]{1,0:T(8,128)(2,1)S(1)}, bf16[576,128]{1,0:T(8,128)(2,1)S(1)}, u32[]{:S(2)}, u32[]{:S(2)}) collective-permute-start(bf16[576,128]{1,0:T(8,128)(2,1)S(1)} %get-tuple-element.19), channel_id=1, source_target_pairs={{0,8},{8,16},{16,24},{24,32},{32,40},{40,48},{48,56},{56,64},{64,7... | collective-permute-start | bytes 442376 | tf_op jit(solution)/shard_map/ppermute | solution.py:35
  8.1 3.1 %collective-permute-start.1 = (bf16[576,128]{1,0:T(8,128)(2,1)S(1)}, bf16[576,128]{1,0:T(8,128)(2,1)}, u32[]{:S(2)}, u32[]{:S(2)}) collective-permute-start(bf16[576,128]{1,0:T(8,128)(2,1)S(1)} %get-tuple-element.20), channel_id=1, source_target_pairs={{0,16},{8,24},{16,32},{24,40},{32,48},{40,56},{48,64},{56,72},{64,... | collective-permute-start | bytes 442376 | tf_op jit(solution)/shard_map/ppermute | solution.py:35
  11.2 3.4 %collective-permute-start.2 = (bf16[576,128]{1,0:T(8,128)(2,1)S(1)}, bf16[576,128]{1,0:T(8,128)(2,1)}, u32[]{:S(2)}, u32[]{:S(2)}) collective-permute-start(bf16[576,128]{1,0:T(8,128)(2,1)S(1)} %get-tuple-element.21), channel_id=1, source_target_pairs={{0,24},{8,32},{16,40},{24,48},{32,56},{40,64},{48,72},{56,80},{64,... | collective-permute-start | bytes 442376 | tf_op jit(solution)/shard_map/ppermute | solution.py:35
  14.7 0.1 pad_add_fusion.where_ref
  14.7 1.2 copy-done
  15.9 1.2 copy-done.2
  17.1 0.6 shard_map.88
  17.7 5.1 %collective-permute-start.4 = (bf16[3584,128]{1,0:T(8,128)(2,1)S(1)}, bf16[3584,128]{1,0:T(8,128)(2,1)S(1)}, u32[]{:S(2)}, u32[]{:S(2)}) collective-permute-start(bf16[3584,128]{1,0:T(8,128)(2,1)S(1)} %shard_map.88), channel_id=1, source_target_pairs={{0,1},{1,0},{2,3},{3,2},{4,5},{5,4},{6,7},{7,6},{8,15},{9,10},{10,... | collective-permute-start | bytes 2752520 | tf_op jit(solution)/shard_map/ppermute | solution.py:53
  22.8 1.6 %copy.9 = bf16[1,128,3584]{1,2,0:T(8,128)(2,1)S(1)} copy(bf16[1,128,3584]{2,1,0:T(8,128)(2,1)} %param.11) | data formatting | bytes 1835008 | tf_op args[4]
  24.5 0.0 collective-permute-done
  24.5 2.0 %collective-permute-done.1 = bf16[576,128]{1,0:T(8,128)(2,1)} collective-permute-done((bf16[576,128]{1,0:T(8,128)(2,1)S(1)}, bf16[576,128]{1,0:T(8,128)(2,1)}, u32[]{:S(2)}, u32[]{:S(2)}) %collective-permute-start.1) | collective-permute-done | bytes 147488 | tf_op jit(solution)/shard_map/ppermute | solution.py:35
  26.5 0.9 slice_dynamic-update-slice_fusion.1
  27.4 3.5 %collective-permute-done.2 = bf16[576,128]{1,0:T(8,128)(2,1)} collective-permute-done((bf16[576,128]{1,0:T(8,128)(2,1)S(1)}, bf16[576,128]{1,0:T(8,128)(2,1)}, u32[]{:S(2)}, u32[]{:S(2)}) %collective-permute-start.2) | collective-permute-done | bytes 147488 | tf_op jit(solution)/shard_map/ppermute | solution.py:35
  30.9 0.9 slice_dynamic-update-slice_fusion
  31.8 0.7 constant_dynamic-update-slice_fusion
  32.5 0.1 convert_element_type.6
  32.6 49.2 %all-gather.1 = f16[18048,128]{1,0:T(8,128)(2,1)S(1)} all-gather(f16[2256,128]{1,0:T(8,128)(2,1)S(1)} %convert_element_type.6), channel_id=1, replica_groups=mesh['node'=96,'local'=8] {'local'}, dimensions={0}, use_global_device_ids=true | all-gather | bytes 5197824 | tf_op jit(solution)/shard_map/all_gather | solution.py:325
  81.9 0.5 convert_element_type.7.got_ref
  82.4 0.6 copy-done.1
  83.0 0.3 copy-done.3
  83.3 1.9 %shard_map.87.own_ref = bf16[656,128]{1,0:T(8,128)(2,1)S(1)} custom-call(bf16[18048,128]{1,0:T(8,128)(2,1)S(1)} %convert_element_type.7.got_ref, bf16[3584,128]{1,0:T(8,128)(2,1)S(1)} %bitcast.14, bf16[3584,128]{1,0:T(8,128)(2,1)S(1)} %bitcast.17, bf16[3584,128]{1,0:T(8,128)(2,1)S(1)} %bitcast.19), custom_call_target="tpu_custom_call" | custom-call | tf_op jit(solution)/shard_map/pallas_call | solution.py:293
  85.2 0.0 copy-start.8
  85.3 3.6 %collective-permute-start.3 = (bf16[656,128]{1,0:T(8,128)(2,1)S(1)}, bf16[656,128]{1,0:T(8,128)(2,1)S(1)}, u32[]{:S(2)}, u32[]{:S(2)}) collective-permute-start(bf16[656,128]{1,0:T(8,128)(2,1)S(1)} %shard_map.87.own_ref), channel_id=1, source_target_pairs={{0,1},{1,0},{2,3},{3,2},{4,5},{5,4},{6,7},{7,6},{8,15},{9,10},{10,... | collective-permute-start | bytes 503816 | tf_op jit(solution)/shard_map/ppermute | solution.py:53
  88.9 3.8 %collective-permute-done.3.other_ref = bf16[656,128]{1,0:T(8,128)(2,1)S(1)} collective-permute-done((bf16[656,128]{1,0:T(8,128)(2,1)S(1)}, bf16[656,128]{1,0:T(8,128)(2,1)S(1)}, u32[]{:S(2)}, u32[]{:S(2)}) %collective-permute-start.3) | collective-permute-done | bytes 167968 | tf_op jit(solution)/shard_map/ppermute | solution.py:53
  92.7 0.0 collective-permute-done.4.other_ref_rows
  92.7 1.7 %shard_map.89 = (f32[2272,128]{1,0:T(8,128)S(1)}, bf16[2272,128]{1,0:T(8,128)(2,1)S(1)}) custom-call(s32[2]{0:T(128)S(1)} %pad_add_fusion.where_ref, bf16[656,128]{1,0:T(8,128)(2,1)S(1)} %shard_map.87.own_ref, bf16[656,128]{1,0:T(8,128)(2,1)S(1)} %collective-permute-done.3.other_ref, bf16[3584,128]{1,0:T(8,128)(2,1)S(1)} %bitcast.15, ...), custom_call_target="tpu_custom_call" | custom-call | tf_op jit(solution)/shard_map/pallas_call | solution.py:293
  94.5 2.8 %collective-permute-start.5 = (bf16[2272,128]{1,0:T(8,128)(2,1)S(1)}, bf16[2272,128]{1,0:T(8,128)(2,1)S(1)}, u32[]{:S(2)}, u32[]{:S(2)}) collective-permute-start(bf16[2272,128]{1,0:T(8,128)(2,1)S(1)} %get-tuple-element.25), channel_id=1, source_target_pairs={{0,2},{1,3},{2,0},{3,1},{4,6},{5,7},{6,4},{7,5},{8,14},{9,15},{10,... | collective-permute-start | bytes 1744904 | tf_op jit(solution)/shard_map/ppermute | solution.py:53
  97.3 15.8 %collective-permute-done.5.got_ref = bf16[2272,128]{1,0:T(8,128)(2,1)S(1)} collective-permute-done((bf16[2272,128]{1,0:T(8,128)(2,1)S(1)}, bf16[2272,128]{1,0:T(8,128)(2,1)S(1)}, u32[]{:S(2)}, u32[]{:S(2)}) %collective-permute-start.5) | collective-permute-done | bytes 581664 | tf_op jit(solution)/shard_map/ppermute | solution.py:53
  113.1 0.2 shard_map.90
  113.3 3.1 %collective-permute-start.6 = (bf16[1136,128]{1,0:T(8,128)(2,1)S(1)}, bf16[1136,128]{1,0:T(8,128)(2,1)S(1)}, u32[]{:S(2)}, u32[]{:S(2)}) collective-permute-start(bf16[1136,128]{1,0:T(8,128)(2,1)S(1)} %get-tuple-element.27), channel_id=1, source_target_pairs={{0,6},{1,7},{2,4},{3,5},{4,2},{5,3},{6,0},{7,1},{8,10},{9,11},{10,... | collective-permute-start | bytes 872456 | tf_op jit(solution)/shard_map/ppermute | solution.py:53
  116.4 6.0 %collective-permute-done.6.got_ref = bf16[1136,128]{1,0:T(8,128)(2,1)S(1)} collective-permute-done((bf16[1136,128]{1,0:T(8,128)(2,1)S(1)}, bf16[1136,128]{1,0:T(8,128)(2,1)S(1)}, u32[]{:S(2)}, u32[]{:S(2)}) %collective-permute-start.6) | collective-permute-done | bytes 290848 | tf_op jit(solution)/shard_map/ppermute | solution.py:53
  122.3 0.1 shard_map.91
  122.4 4.5 %collective-permute-start.7 = (bf16[336,128]{1,0:T(8,128)(2,1)S(1)}, bf16[336,128]{1,0:T(8,128)(2,1)S(1)}, u32[]{:S(2)}, u32[]{:S(2)}) collective-permute-start(bf16[336,128]{1,0:T(8,128)(2,1)S(1)} %get-tuple-element.29), channel_id=1, source_target_pairs={{0,760},{8,0},{16,8},{24,16},{32,24},{40,32},{48,40},{56,48},{64,5... | collective-permute-start | bytes 258056 | tf_op jit(solution)/shard_map/ppermute | solution.py:35
  126.9 10.6 %collective-permute-start.8 = (bf16[336,128]{1,0:T(8,128)(2,1)S(1)}, bf16[336,128]{1,0:T(8,128)(2,1)S(1)}, u32[]{:S(2)}, u32[]{:S(2)}) collective-permute-start(bf16[336,128]{1,0:T(8,128)(2,1)S(1)} %get-tuple-element.30), channel_id=1, source_target_pairs={{0,752},{8,760},{16,0},{24,8},{32,16},{40,24},{48,32},{56,40},{64,... | collective-permute-start | bytes 258056 | tf_op jit(solution)/shard_map/ppermute | solution.py:35
  137.5 3.4 %collective-permute-start.9 = (bf16[336,128]{1,0:T(8,128)(2,1)S(1)}, bf16[336,128]{1,0:T(8,128)(2,1)S(1)}, u32[]{:S(2)}, u32[]{:S(2)}) collective-permute-start(bf16[336,128]{1,0:T(8,128)(2,1)S(1)} %get-tuple-element.31), channel_id=1, source_target_pairs={{0,744},{8,752},{16,760},{24,0},{32,8},{40,16},{48,24},{56,32},{64... | collective-permute-start | bytes 258056 | tf_op jit(solution)/shard_map/ppermute | solution.py:35
  140.9 0.0 collective-permute-done.7.refs_1_
  140.9 0.0 collective-permute-done.8.refs_2_
  140.9 3.9 %collective-permute-done.9.refs_3_ = bf16[336,128]{1,0:T(8,128)(2,1)S(1)} collective-permute-done((bf16[336,128]{1,0:T(8,128)(2,1)S(1)}, bf16[336,128]{1,0:T(8,128)(2,1)S(1)}, u32[]{:S(2)}, u32[]{:S(2)}) %collective-permute-start.9) | collective-permute-done | bytes 86048 | tf_op jit(solution)/shard_map/ppermute | solution.py:35
  144.8 0.0 copy-done.7
  144.8 0.0 copy-done.8
  144.8 1.1 shard_map.92
  (7 shorter events, 0.0 us)
Async XLA Ops:
  0.6 0.9 copy-start.4
  1.5 0.9 copy-start.5
  2.4 0.7 copy-start.6
  3.6 20.9 %collective-permute-start = (bf16[576,128]{1,0:T(8,128)(2,1)S(1)}, bf16[576,128]{1,0:T(8,128)(2,1)S(1)}, u32[]{:S(2)}, u32[]{:S(2)}) collective-permute-start(bf16[576,128]{1,0:T(8,128)(2,1)S(1)} %get-tuple-element.19), channel_id=1, source_target_pairs={{0,8},{8,16},{16,24},{24,32},{32,40},{40,48},{48,56},{56,64},{64,7... | collective-permute-start | bytes 442376 | tf_op jit(solution)/shard_map/ppermute | solution.py:35
  8.1 18.4 %collective-permute-start.1 = (bf16[576,128]{1,0:T(8,128)(2,1)S(1)}, bf16[576,128]{1,0:T(8,128)(2,1)}, u32[]{:S(2)}, u32[]{:S(2)}) collective-permute-start(bf16[576,128]{1,0:T(8,128)(2,1)S(1)} %get-tuple-element.20), channel_id=1, source_target_pairs={{0,16},{8,24},{16,32},{24,40},{32,48},{40,56},{48,64},{56,72},{64,... | collective-permute-start | bytes 442376 | tf_op jit(solution)/shard_map/ppermute | solution.py:35
  11.2 19.7 %collective-permute-start.2 = (bf16[576,128]{1,0:T(8,128)(2,1)S(1)}, bf16[576,128]{1,0:T(8,128)(2,1)}, u32[]{:S(2)}, u32[]{:S(2)}) collective-permute-start(bf16[576,128]{1,0:T(8,128)(2,1)S(1)} %get-tuple-element.21), channel_id=1, source_target_pairs={{0,24},{8,32},{16,40},{24,48},{32,56},{40,64},{48,72},{56,80},{64,... | collective-permute-start | bytes 442376 | tf_op jit(solution)/shard_map/ppermute | solution.py:35
  14.7 1.2 copy-start
  15.9 1.2 copy-start.2
  17.7 75.0 %collective-permute-start.4 = (bf16[3584,128]{1,0:T(8,128)(2,1)S(1)}, bf16[3584,128]{1,0:T(8,128)(2,1)S(1)}, u32[]{:S(2)}, u32[]{:S(2)}) collective-permute-start(bf16[3584,128]{1,0:T(8,128)(2,1)S(1)} %shard_map.88), channel_id=1, source_target_pairs={{0,1},{1,0},{2,3},{3,2},{4,5},{5,4},{6,7},{7,6},{8,15},{9,10},{10,... | collective-permute-start | bytes 2752520 | tf_op jit(solution)/shard_map/ppermute | solution.py:53
  81.8 1.2 copy-start.1
  81.8 1.5 copy-start.3
  85.2 59.5 %copy-start.7 = (s32[128,2]{0,1:T(2,128)S(1)}, s32[128,2]{0,1:T(2,128)}, u32[]{:S(2)}) copy-start(s32[128,2]{0,1:T(2,128)} %param.12) | copy-start | bytes 3076
  85.2 59.5 %copy-start.8 = (s32[128,2]{0,1:T(2,128)S(1)}, s32[128,2]{0,1:T(2,128)}, u32[]{:S(2)}) copy-start(s32[128,2]{0,1:T(2,128)} %param.13) | copy-start | bytes 3076
  85.3 7.5 %collective-permute-start.3 = (bf16[656,128]{1,0:T(8,128)(2,1)S(1)}, bf16[656,128]{1,0:T(8,128)(2,1)S(1)}, u32[]{:S(2)}, u32[]{:S(2)}) collective-permute-start(bf16[656,128]{1,0:T(8,128)(2,1)S(1)} %shard_map.87.own_ref), channel_id=1, source_target_pairs={{0,1},{1,0},{2,3},{3,2},{4,5},{5,4},{6,7},{7,6},{8,15},{9,10},{10,... | collective-permute-start | bytes 503816 | tf_op jit(solution)/shard_map/ppermute | solution.py:53
  94.5 18.6 %collective-permute-start.5 = (bf16[2272,128]{1,0:T(8,128)(2,1)S(1)}, bf16[2272,128]{1,0:T(8,128)(2,1)S(1)}, u32[]{:S(2)}, u32[]{:S(2)}) collective-permute-start(bf16[2272,128]{1,0:T(8,128)(2,1)S(1)} %get-tuple-element.25), channel_id=1, source_target_pairs={{0,2},{1,3},{2,0},{3,1},{4,6},{5,7},{6,4},{7,5},{8,14},{9,15},{10,... | collective-permute-start | bytes 1744904 | tf_op jit(solution)/shard_map/ppermute | solution.py:53
  113.3 9.1 %collective-permute-start.6 = (bf16[1136,128]{1,0:T(8,128)(2,1)S(1)}, bf16[1136,128]{1,0:T(8,128)(2,1)S(1)}, u32[]{:S(2)}, u32[]{:S(2)}) collective-permute-start(bf16[1136,128]{1,0:T(8,128)(2,1)S(1)} %get-tuple-element.27), channel_id=1, source_target_pairs={{0,6},{1,7},{2,4},{3,5},{4,2},{5,3},{6,0},{7,1},{8,10},{9,11},{10,... | collective-permute-start | bytes 872456 | tf_op jit(solution)/shard_map/ppermute | solution.py:53
  122.4 18.5 %collective-permute-start.7 = (bf16[336,128]{1,0:T(8,128)(2,1)S(1)}, bf16[336,128]{1,0:T(8,128)(2,1)S(1)}, u32[]{:S(2)}, u32[]{:S(2)}) collective-permute-start(bf16[336,128]{1,0:T(8,128)(2,1)S(1)} %get-tuple-element.29), channel_id=1, source_target_pairs={{0,760},{8,0},{16,8},{24,16},{32,24},{40,32},{48,40},{56,48},{64,5... | collective-permute-start | bytes 258056 | tf_op jit(solution)/shard_map/ppermute | solution.py:35
  126.9 14.0 %collective-permute-start.8 = (bf16[336,128]{1,0:T(8,128)(2,1)S(1)}, bf16[336,128]{1,0:T(8,128)(2,1)S(1)}, u32[]{:S(2)}, u32[]{:S(2)}) collective-permute-start(bf16[336,128]{1,0:T(8,128)(2,1)S(1)} %get-tuple-element.30), channel_id=1, source_target_pairs={{0,752},{8,760},{16,0},{24,8},{32,16},{40,24},{48,32},{56,40},{64,... | collective-permute-start | bytes 258056 | tf_op jit(solution)/shard_map/ppermute | solution.py:35
  137.5 7.3 %collective-permute-start.9 = (bf16[336,128]{1,0:T(8,128)(2,1)S(1)}, bf16[336,128]{1,0:T(8,128)(2,1)S(1)}, u32[]{:S(2)}, u32[]{:S(2)}) collective-permute-start(bf16[336,128]{1,0:T(8,128)(2,1)S(1)} %get-tuple-element.31), channel_id=1, source_target_pairs={{0,744},{8,752},{16,760},{24,0},{32,8},{40,16},{48,24},{56,32},{64... | collective-permute-start | bytes 258056 | tf_op jit(solution)/shard_map/ppermute | solution.py:35

commit v8 on v7

--- a/solution.py
+++ b/solution.py
@@ -22,6 +22,7 @@
 HALF_ROWS = SHARES * FEAT
 LEVELS = 15
 INTERPRET = False
+LIMIT = 10
 
 f32 = jnp.float32
 bf16 = jnp.bfloat16
@@ -57,14 +58,23 @@
     return place, across(1 - core, place), across(core, place), (place + 4) & 7
 
 
-def pick_kernel(where_ref, gate_ref, up_ref, out_ref):
+def pick_kernel(where_ref, gate_ref, up_ref, out_ref, sems):
     core = where_ref[0] & 1
     theirs = targets(core, beside(core, where_ref[1]))
+    copies = []
     for turn in range(SHARES):
         start = pl.multiple_of(theirs[turn] * FEAT, 64)
-        low = turn * FEAT
-        out_ref[low : low + FEAT, :] = gate_ref[pl.ds(start, FEAT), :]
-        out_ref[HALF_ROWS + low : HALF_ROWS + low + FEAT, :] = up_ref[pl.ds(start, FEAT), :]
+        for half, ref in enumerate((gate_ref, up_ref)):
+            low = half * HALF_ROWS + turn * FEAT
+            copies.append(
+                pltpu.make_async_copy(
+                    ref.at[pl.ds(start, FEAT), :], out_ref.at[low : low + FEAT, :], sems.at[2 * turn + half]
+                )
+            )
+    for copy in copies:
+        copy.start()
+    for copy in copies:
+        copy.wait()
 
 
 def tables(route):
@@ -103,7 +113,17 @@
     return (wide * power_of(level, 1)).astype(bf16), level
 
 
-def pack_kernel(route_ref, in_ref, grad_ref, *out_refs):
+def pack_kernel(route_hbm, in_hbm, grad_hbm, *refs):
+    out_refs = refs[0:GROUP]
+    route_ref, in_ref, grad_ref, sems = refs[GROUP:]
+    copies = [
+        pltpu.make_async_copy(source, target, sems.at[number])
+        for number, (source, target) in enumerate(((route_hbm, route_ref), (in_hbm, in_ref), (grad_hbm, grad_ref)))
+    ]
+    for copy in copies:
+        copy.start()
+    for copy in copies:
+        copy.wait()
     table = jnp.concatenate(tables(route_ref[...]), axis=0)
     rows_in, level_in = scaled(in_ref[...])
     rows_grad, level_grad = scaled(grad_ref[...])
@@ -118,6 +138,15 @@
     for o in range(GROUP):
         levels = jnp.where(line == 2 * o, level_in, jnp.where(line == 2 * o + 1, level_grad, 0.0))
         out_refs[o][7 * CAP : OUT_ROWS, :] = levels.astype(bf16)
+
+
+def join_kernel(*refs):
+    out_ref = refs[GROUP]
+    levels = jnp.zeros((16, LANE), bf16)
+    for o in range(GROUP):
+        out_ref[o * 7 * CAP : (o + 1) * 7 * CAP, :] = refs[o][0 : 7 * CAP, :]
+        levels = levels + refs[o][7 * CAP : OUT_ROWS, :]
+    out_ref[GROUP * 7 * CAP : SHARD_ROWS, :] = levels
 
 
 def hidden_kernel(got_ref, gate_ref, up_ref, down_ref, out_ref):
@@ -288,14 +317,20 @@
     gate_ref[...] = gate
 
 
-def call(kernel, outs, *args, scalars=0):
-    spaces = [pltpu.SMEM if number < scalars else pltpu.VMEM for number in range(len(args))]
+def call(kernel, outs, *args, scalars=0, far=0, scratch=()):
+    spaces = [pltpu.SMEM] * scalars + [pltpu.HBM] * far
+    spaces += [pltpu.VMEM] * (len(args) - len(spaces))
+    many = isinstance(outs, list)
+    if not INTERPRET:
+        args = [a if s is pltpu.SMEM else pltpu.with_memory_space_constraint(a, s) for a, s in zip(args, spaces)]
     return pl.pallas_call(
         kernel,
         out_shape=outs,
         in_specs=[pl.BlockSpec(memory_space=space) for space in spaces],
+        out_specs=[pl.BlockSpec(memory_space=pltpu.VMEM)] * len(outs) if many else pl.BlockSpec(memory_space=pltpu.VMEM),
+        scratch_shapes=list(scratch),
         interpret=INTERPRET,
-        compiler_params=pltpu.CompilerParams(vmem_limit_bytes=24 * 1024 * 1024),
+        compiler_params=pltpu.CompilerParams(vmem_limit_bytes=LIMIT * 1024 * 1024),
     )(*args)
 
 
@@ -309,6 +344,8 @@
         gate_weight[0],
         up_weight[0],
         scalars=1,
+        far=2,
+        scratch=[pltpu.SemaphoreType.DMA((2 * SHARES,))],
     )
     other_rows = swap(picked, beside, 0)
     packed = call(
@@ -317,11 +354,17 @@
         route,
         layer_input.T,
         output_grad.T,
+        far=3,
+        scratch=[
+            pltpu.VMEM((2, TOK), jnp.int32),
+            pltpu.VMEM((FEAT, TOK), bf16),
+            pltpu.VMEM((FEAT, TOK), bf16),
+            pltpu.SemaphoreType.DMA((3,)),
+        ],
     )
     got = [packed[0]] + [from_behind(packed[o], "node", o) for o in range(1, GROUP)]
-    levels = got[0][7 * CAP :] + got[1][7 * CAP :] + got[2][7 * CAP :] + got[3][7 * CAP :]
-    shard = jnp.concatenate([value[: 7 * CAP] for value in got] + [levels], axis=0).astype(jnp.float16)
-    shard, down_cols = lax.optimization_barrier((shard, down_weight[0].T))
+    got, down_cols = lax.optimization_barrier((got, down_weight[0].T))
+    shard = call(join_kernel, jax.ShapeDtypeStruct((SHARD_ROWS, LANE), bf16), *got).astype(jnp.float16)
     full = lax.all_gather(shard, "local", axis=0, tiled=True).astype(bf16)
     hidden = call(
         hidden_kernel,

time: 147 us -> 144 us (0.980)
  local copies, waits for them, and re-layouts: 9.24 us -> 2.53 us
  Pallas kernels: 6.08 us -> 9.05 us
  waiting for transfers between devices: 34.9 us -> 37.5 us
    unnamed x23 -> x9, local copies, waits for them, and re-layouts: 9.24 us -> 2.53 us
    pallas_call x7 -> x8, Pallas kernels: 6.08 us -> 9.05 us  [call(): pl.pallas_call(kernel, out_shape=outs, in_specs=[pl.BlockSpec(memory_spac...]
    ppermute x6, waiting for transfers between devices: 9.29 us -> 11.4 us  [from_behind(): return lax.ppermute(value, axis, pairs)]
  transfers between devices with their start and end apart: 10 -> 10, of which waited for: 6 -> 6; matrix products, arithmetic and copies ran while one was open for 3% -> 2% of each run, Pallas kernels for 2% -> 3%
where the time goes in v8:
time: 144 us
  blocking collectives  49.3 us (34%)
  starting transfers between devices  44 us (31%)
  waiting for transfers between devices  37.5 us (26%)
  Pallas kernels  9.05 us (6%)
  local copies, waits for them, and re-layouts  2.53 us (2%)
    all_gather x1, blocking collectives, body(): full = lax.all_gather(shard, 'local', axis=0, tiled=True).astype(bf16)  49.3 us
    ppermute x6, starting transfers between devices, from_behind(): return lax.ppermute(value, axis, pairs)  29.4 us
    ppermute x4, waiting for transfers between devices, swap(): return lax.ppermute(value, ('node', 'local'), pairs)  26.1 us
    ppermute x4, starting transfers between devices, swap(): return lax.ppermute(value, ('node', 'local'), pairs)  14.6 us
    ppermute x6, waiting for transfers between devices, from_behind(): return lax.ppermute(value, axis, pairs)  11.4 us
    pallas_call x8, Pallas kernels, call(): pl.pallas_call(kernel, out_shape=outs, in_specs=[pl.BlockSpec(memory_spac...  9.05 us
  transfers between devices with their start and end apart: 10, of which 6 were waited for; matrix products, arithmetic and copies ran while one was open for 2% of the time, Pallas kernels for 3%

profile of v8, /device:TPU:1, one launch (start us, length us, event | category | flops | bytes accessed | tf_op | source)
XLA Modules:
  0.0 144.0 jit_solution(2734884160716864344)
XLA Ops:
  0.6 2.1 %shard_map.86 = (bf16[576,128]{1,0:T(8,128)(2,1)S(1)}, bf16[576,128]{1,0:T(8,128)(2,1)}, bf16[576,128]{1,0:T(8,128)(2,1)}, bf16[576,128]{1,0:T(8,128)(2,1)S(1)}) custom-call(s32[2,128]{1,0:T(2,128)} %bitcast.20, bf16[448,128]{1,0:T(8,128)(2,1)} %bitcast.23, bf16[448,128]{1,0:T(8,128)(2,1)} %bitcast.24), custom_call_target="tpu_custom_call" | custom-call | tf_op jit(solution)/shard_map/pallas_call | solution.py:326
  2.8 4.5 %collective-permute-start = (bf16[576,128]{1,0:T(8,128)(2,1)}, bf16[576,128]{1,0:T(8,128)(2,1)S(1)}, u32[]{:S(2)}, u32[]{:S(2)}) collective-permute-start(bf16[576,128]{1,0:T(8,128)(2,1)} %get-tuple-element.22), channel_id=1, source_target_pairs={{0,8},{8,16},{16,24},{24,32},{32,40},{40,48},{48,56},{56,64},{64,7... | collective-permute-start | bytes 442376 | tf_op jit(solution)/shard_map/ppermute | solution.py:36
  7.3 3.1 %collective-permute-start.1 = (bf16[576,128]{1,0:T(8,128)(2,1)}, bf16[576,128]{1,0:T(8,128)(2,1)S(1)}, u32[]{:S(2)}, u32[]{:S(2)}) collective-permute-start(bf16[576,128]{1,0:T(8,128)(2,1)} %get-tuple-element.23), channel_id=1, source_target_pairs={{0,16},{8,24},{16,32},{24,40},{32,48},{40,56},{48,64},{56,72},{64,... | collective-permute-start | bytes 442376 | tf_op jit(solution)/shard_map/ppermute | solution.py:36
  10.4 3.4 %collective-permute-start.2 = (bf16[576,128]{1,0:T(8,128)(2,1)S(1)}, bf16[576,128]{1,0:T(8,128)(2,1)S(1)}, u32[]{:S(2)}, u32[]{:S(2)}) collective-permute-start(bf16[576,128]{1,0:T(8,128)(2,1)S(1)} %get-tuple-element.24), channel_id=1, source_target_pairs={{0,24},{8,32},{16,40},{24,48},{32,56},{40,64},{48,72},{56,80},{64,... | collective-permute-start | bytes 442376 | tf_op jit(solution)/shard_map/ppermute | solution.py:36
  13.9 0.1 pad_add_fusion.where_ref
  13.9 1.9 %shard_map.89 = bf16[3584,128]{1,0:T(8,128)(2,1)S(1)} custom-call(s32[2]{0:T(128)S(1)} %pad_add_fusion.where_ref, bf16[3584,128]{1,0:T(8,128)(2,1)} %bitcast.13, bf16[3584,128]{1,0:T(8,128)(2,1)} %bitcast.16), custom_call_target="tpu_custom_call" | custom-call | tf_op jit(solution)/shard_map/pallas_call | solution.py:326
  15.8 5.1 %collective-permute-start.4 = (bf16[3584,128]{1,0:T(8,128)(2,1)S(1)}, bf16[3584,128]{1,0:T(8,128)(2,1)S(1)}, u32[]{:S(2)}, u32[]{:S(2)}) collective-permute-start(bf16[3584,128]{1,0:T(8,128)(2,1)S(1)} %shard_map.89), channel_id=1, source_target_pairs={{0,1},{1,0},{2,3},{3,2},{4,5},{5,4},{6,7},{7,6},{8,15},{9,10},{10,... | collective-permute-start | bytes 2752520 | tf_op jit(solution)/shard_map/ppermute | solution.py:54
  20.9 1.6 %copy.9 = bf16[1,128,3584]{1,2,0:T(8,128)(2,1)S(1)} copy(bf16[1,128,3584]{2,1,0:T(8,128)(2,1)} %param.11) | data formatting | bytes 1835008 | tf_op args[4]
  22.6 0.0 collective-permute-done.refs_1_
  22.6 3.2 %collective-permute-done.1.refs_2_ = bf16[576,128]{1,0:T(8,128)(2,1)S(1)} collective-permute-done((bf16[576,128]{1,0:T(8,128)(2,1)}, bf16[576,128]{1,0:T(8,128)(2,1)S(1)}, u32[]{:S(2)}, u32[]{:S(2)}) %collective-permute-start.1) | collective-permute-done | bytes 147488 | tf_op jit(solution)/shard_map/ppermute | solution.py:36
  25.8 4.3 %collective-permute-done.2.refs_3_ = bf16[576,128]{1,0:T(8,128)(2,1)S(1)} collective-permute-done((bf16[576,128]{1,0:T(8,128)(2,1)S(1)}, bf16[576,128]{1,0:T(8,128)(2,1)S(1)}, u32[]{:S(2)}, u32[]{:S(2)}) %collective-permute-start.2) | collective-permute-done | bytes 147488 | tf_op jit(solution)/shard_map/ppermute | solution.py:36
  30.1 0.1 convert_element_type.6
  30.2 49.3 %all-gather.1 = f16[18048,128]{1,0:T(8,128)(2,1)S(1)} all-gather(f16[2256,128]{1,0:T(8,128)(2,1)S(1)} %convert_element_type.6), channel_id=1, replica_groups=mesh['node'=96,'local'=8] {'local'}, dimensions={0}, use_global_device_ids=true | all-gather | bytes 5197824 | tf_op jit(solution)/shard_map/all_gather | solution.py:368
  79.6 0.0 copy-start
  79.6 0.0 copy-start.1
  79.6 0.5 convert_element_type.7.got_ref
  80.1 0.6 copy-done
  80.8 0.3 copy-done.1
  81.0 1.9 %shard_map.88.own_ref = bf16[656,128]{1,0:T(8,128)(2,1)S(1)} custom-call(bf16[18048,128]{1,0:T(8,128)(2,1)S(1)} %convert_element_type.7.got_ref, bf16[3584,128]{1,0:T(8,128)(2,1)S(1)} %bitcast.14, bf16[3584,128]{1,0:T(8,128)(2,1)S(1)} %bitcast.17, bf16[3584,128]{1,0:T(8,128)(2,1)S(1)} %bitcast.19), custom_call_target="tpu_custom_call" | custom-call | tf_op jit(solution)/shard_map/pallas_call | solution.py:326
  82.9 0.0 copy-start.2
  83.0 0.0 copy-start.3
  83.0 3.6 %collective-permute-start.3 = (bf16[656,128]{1,0:T(8,128)(2,1)S(1)}, bf16[656,128]{1,0:T(8,128)(2,1)S(1)}, u32[]{:S(2)}, u32[]{:S(2)}) collective-permute-start(bf16[656,128]{1,0:T(8,128)(2,1)S(1)} %shard_map.88.own_ref), channel_id=1, source_target_pairs={{0,1},{1,0},{2,3},{3,2},{4,5},{5,4},{6,7},{7,6},{8,15},{9,10},{10,... | collective-permute-start | bytes 503816 | tf_op jit(solution)/shard_map/ppermute | solution.py:54
  86.6 3.8 %collective-permute-done.3.other_ref = bf16[656,128]{1,0:T(8,128)(2,1)S(1)} collective-permute-done((bf16[656,128]{1,0:T(8,128)(2,1)S(1)}, bf16[656,128]{1,0:T(8,128)(2,1)S(1)}, u32[]{:S(2)}, u32[]{:S(2)}) %collective-permute-start.3) | collective-permute-done | bytes 167968 | tf_op jit(solution)/shard_map/ppermute | solution.py:54
  90.4 0.0 collective-permute-done.4.other_ref_rows
  90.4 1.7 %shard_map.90 = (f32[2272,128]{1,0:T(8,128)S(1)}, bf16[2272,128]{1,0:T(8,128)(2,1)S(1)}) custom-call(s32[2]{0:T(128)S(1)} %pad_add_fusion.where_ref, bf16[656,128]{1,0:T(8,128)(2,1)S(1)} %shard_map.88.own_ref, bf16[656,128]{1,0:T(8,128)(2,1)S(1)} %collective-permute-done.3.other_ref, bf16[3584,128]{1,0:T(8,128)(2,1)S(1)} %bitcast.15, ...), custom_call_target="tpu_custom_call" | custom-call | tf_op jit(solution)/shard_map/pallas_call | solution.py:326
  92.2 2.8 %collective-permute-start.5 = (bf16[2272,128]{1,0:T(8,128)(2,1)S(1)}, bf16[2272,128]{1,0:T(8,128)(2,1)S(1)}, u32[]{:S(2)}, u32[]{:S(2)}) collective-permute-start(bf16[2272,128]{1,0:T(8,128)(2,1)S(1)} %get-tuple-element.31), channel_id=1, source_target_pairs={{0,2},{1,3},{2,0},{3,1},{4,6},{5,7},{6,4},{7,5},{8,14},{9,15},{10,... | collective-permute-start | bytes 1744904 | tf_op jit(solution)/shard_map/ppermute | solution.py:54
  95.0 15.9 %collective-permute-done.5.got_ref = bf16[2272,128]{1,0:T(8,128)(2,1)S(1)} collective-permute-done((bf16[2272,128]{1,0:T(8,128)(2,1)S(1)}, bf16[2272,128]{1,0:T(8,128)(2,1)S(1)}, u32[]{:S(2)}, u32[]{:S(2)}) %collective-permute-start.5) | collective-permute-done | bytes 581664 | tf_op jit(solution)/shard_map/ppermute | solution.py:54
  110.9 0.2 shard_map.91
  111.1 3.0 %collective-permute-start.6 = (bf16[1136,128]{1,0:T(8,128)(2,1)S(1)}, bf16[1136,128]{1,0:T(8,128)(2,1)S(1)}, u32[]{:S(2)}, u32[]{:S(2)}) collective-permute-start(bf16[1136,128]{1,0:T(8,128)(2,1)S(1)} %get-tuple-element.33), channel_id=1, source_target_pairs={{0,6},{1,7},{2,4},{3,5},{4,2},{5,3},{6,0},{7,1},{8,10},{9,11},{10,... | collective-permute-start | bytes 872456 | tf_op jit(solution)/shard_map/ppermute | solution.py:54
  114.1 6.4 %collective-permute-done.6.got_ref = bf16[1136,128]{1,0:T(8,128)(2,1)S(1)} collective-permute-done((bf16[1136,128]{1,0:T(8,128)(2,1)S(1)}, bf16[1136,128]{1,0:T(8,128)(2,1)S(1)}, u32[]{:S(2)}, u32[]{:S(2)}) %collective-permute-start.6) | collective-permute-done | bytes 290848 | tf_op jit(solution)/shard_map/ppermute | solution.py:54
  120.5 0.1 shard_map.92
  120.5 4.0 %collective-permute-start.7 = (bf16[336,128]{1,0:T(8,128)(2,1)S(1)}, bf16[336,128]{1,0:T(8,128)(2,1)S(1)}, u32[]{:S(2)}, u32[]{:S(2)}) collective-permute-start(bf16[336,128]{1,0:T(8,128)(2,1)S(1)} %get-tuple-element.35), channel_id=1, source_target_pairs={{0,760},{8,0},{16,8},{24,16},{32,24},{40,32},{48,40},{56,48},{64,5... | collective-permute-start | bytes 258056 | tf_op jit(solution)/shard_map/ppermute | solution.py:36
  124.5 11.1 %collective-permute-start.8 = (bf16[336,128]{1,0:T(8,128)(2,1)S(1)}, bf16[336,128]{1,0:T(8,128)(2,1)S(1)}, u32[]{:S(2)}, u32[]{:S(2)}) collective-permute-start(bf16[336,128]{1,0:T(8,128)(2,1)S(1)} %get-tuple-element.36), channel_id=1, source_target_pairs={{0,752},{8,760},{16,0},{24,8},{32,16},{40,24},{48,32},{56,40},{64,... | collective-permute-start | bytes 258056 | tf_op jit(solution)/shard_map/ppermute | solution.py:36
  135.6 3.4 %collective-permute-start.9 = (bf16[336,128]{1,0:T(8,128)(2,1)S(1)}, bf16[336,128]{1,0:T(8,128)(2,1)S(1)}, u32[]{:S(2)}, u32[]{:S(2)}) collective-permute-start(bf16[336,128]{1,0:T(8,128)(2,1)S(1)} %get-tuple-element.37), channel_id=1, source_target_pairs={{0,744},{8,752},{16,760},{24,0},{32,8},{40,16},{48,24},{56,32},{64... | collective-permute-start | bytes 258056 | tf_op jit(solution)/shard_map/ppermute | solution.py:36
  138.9 0.0 collective-permute-done.7.refs_1_
  138.9 0.0 collective-permute-done.8.refs_2_
  139.0 3.9 %collective-permute-done.9.refs_3_ = bf16[336,128]{1,0:T(8,128)(2,1)S(1)} collective-permute-done((bf16[336,128]{1,0:T(8,128)(2,1)S(1)}, bf16[336,128]{1,0:T(8,128)(2,1)S(1)}, u32[]{:S(2)}, u32[]{:S(2)}) %collective-permute-start.9) | collective-permute-done | bytes 86048 | tf_op jit(solution)/shard_map/ppermute | solution.py:36
  142.9 0.0 copy-done.2
  142.9 0.0 copy-done.3
  142.9 1.1 shard_map.93
  (1 shorter events, 0.0 us)
Async XLA Ops:
  2.8 19.8 %collective-permute-start = (bf16[576,128]{1,0:T(8,128)(2,1)}, bf16[576,128]{1,0:T(8,128)(2,1)S(1)}, u32[]{:S(2)}, u32[]{:S(2)}) collective-permute-start(bf16[576,128]{1,0:T(8,128)(2,1)} %get-tuple-element.22), channel_id=1, source_target_pairs={{0,8},{8,16},{16,24},{24,32},{32,40},{40,48},{48,56},{56,64},{64,7... | collective-permute-start | bytes 442376 | tf_op jit(solution)/shard_map/ppermute | solution.py:36
  7.3 18.5 %collective-permute-start.1 = (bf16[576,128]{1,0:T(8,128)(2,1)}, bf16[576,128]{1,0:T(8,128)(2,1)S(1)}, u32[]{:S(2)}, u32[]{:S(2)}) collective-permute-start(bf16[576,128]{1,0:T(8,128)(2,1)} %get-tuple-element.23), channel_id=1, source_target_pairs={{0,16},{8,24},{16,32},{24,40},{32,48},{40,56},{48,64},{56,72},{64,... | collective-permute-start | bytes 442376 | tf_op jit(solution)/shard_map/ppermute | solution.py:36
  10.4 19.7 %collective-permute-start.2 = (bf16[576,128]{1,0:T(8,128)(2,1)S(1)}, bf16[576,128]{1,0:T(8,128)(2,1)S(1)}, u32[]{:S(2)}, u32[]{:S(2)}) collective-permute-start(bf16[576,128]{1,0:T(8,128)(2,1)S(1)} %get-tuple-element.24), channel_id=1, source_target_pairs={{0,24},{8,32},{16,40},{24,48},{32,56},{40,64},{48,72},{56,80},{64,... | collective-permute-start | bytes 442376 | tf_op jit(solution)/shard_map/ppermute | solution.py:36
  15.8 74.6 %collective-permute-start.4 = (bf16[3584,128]{1,0:T(8,128)(2,1)S(1)}, bf16[3584,128]{1,0:T(8,128)(2,1)S(1)}, u32[]{:S(2)}, u32[]{:S(2)}) collective-permute-start(bf16[3584,128]{1,0:T(8,128)(2,1)S(1)} %shard_map.89), channel_id=1, source_target_pairs={{0,1},{1,0},{2,3},{3,2},{4,5},{5,4},{6,7},{7,6},{8,15},{9,10},{10,... | collective-permute-start | bytes 2752520 | tf_op jit(solution)/shard_map/ppermute | solution.py:54
  79.6 1.2 copy-start
  79.6 1.5 %copy-start.1 = (bf16[1,3584,128]{2,1,0:T(8,128)(2,1)S(1)}, bf16[1,3584,128]{2,1,0:T(8,128)(2,1)}, u32[]{:S(2)}) copy-start(bf16[1,3584,128]{2,1,0:T(8,128)(2,1)} %param.10) | copy-start | bytes 2752516
  82.9 59.9 %copy-start.2 = (s32[128,2]{0,1:T(2,128)S(1)}, s32[128,2]{0,1:T(2,128)}, u32[]{:S(2)}) copy-start(s32[128,2]{0,1:T(2,128)} %param.12) | copy-start | bytes 3076
  83.0 59.9 %copy-start.3 = (s32[128,2]{0,1:T(2,128)S(1)}, s32[128,2]{0,1:T(2,128)}, u32[]{:S(2)}) copy-start(s32[128,2]{0,1:T(2,128)} %param.13) | copy-start | bytes 3076
  83.0 7.5 %collective-permute-start.3 = (bf16[656,128]{1,0:T(8,128)(2,1)S(1)}, bf16[656,128]{1,0:T(8,128)(2,1)S(1)}, u32[]{:S(2)}, u32[]{:S(2)}) collective-permute-start(bf16[656,128]{1,0:T(8,128)(2,1)S(1)} %shard_map.88.own_ref), channel_id=1, source_target_pairs={{0,1},{1,0},{2,3},{3,2},{4,5},{5,4},{6,7},{7,6},{8,15},{9,10},{10,... | collective-permute-start | bytes 503816 | tf_op jit(solution)/shard_map/ppermute | solution.py:54
  92.2 18.8 %collective-permute-start.5 = (bf16[2272,128]{1,0:T(8,128)(2,1)S(1)}, bf16[2272,128]{1,0:T(8,128)(2,1)S(1)}, u32[]{:S(2)}, u32[]{:S(2)}) collective-permute-start(bf16[2272,128]{1,0:T(8,128)(2,1)S(1)} %get-tuple-element.31), channel_id=1, source_target_pairs={{0,2},{1,3},{2,0},{3,1},{4,6},{5,7},{6,4},{7,5},{8,14},{9,15},{10,... | collective-permute-start | bytes 1744904 | tf_op jit(solution)/shard_map/ppermute | solution.py:54
  111.1 9.4 %collective-permute-start.6 = (bf16[1136,128]{1,0:T(8,128)(2,1)S(1)}, bf16[1136,128]{1,0:T(8,128)(2,1)S(1)}, u32[]{:S(2)}, u32[]{:S(2)}) collective-permute-start(bf16[1136,128]{1,0:T(8,128)(2,1)S(1)} %get-tuple-element.33), channel_id=1, source_target_pairs={{0,6},{1,7},{2,4},{3,5},{4,2},{5,3},{6,0},{7,1},{8,10},{9,11},{10,... | collective-permute-start | bytes 872456 | tf_op jit(solution)/shard_map/ppermute | solution.py:54
  120.5 18.4 %collective-permute-start.7 = (bf16[336,128]{1,0:T(8,128)(2,1)S(1)}, bf16[336,128]{1,0:T(8,128)(2,1)S(1)}, u32[]{:S(2)}, u32[]{:S(2)}) collective-permute-start(bf16[336,128]{1,0:T(8,128)(2,1)S(1)} %get-tuple-element.35), channel_id=1, source_target_pairs={{0,760},{8,0},{16,8},{24,16},{32,24},{40,32},{48,40},{56,48},{64,5... | collective-permute-start | bytes 258056 | tf_op jit(solution)/shard_map/ppermute | solution.py:36
  124.5 14.5 %collective-permute-start.8 = (bf16[336,128]{1,0:T(8,128)(2,1)S(1)}, bf16[336,128]{1,0:T(8,128)(2,1)S(1)}, u32[]{:S(2)}, u32[]{:S(2)}) collective-permute-start(bf16[336,128]{1,0:T(8,128)(2,1)S(1)} %get-tuple-element.36), channel_id=1, source_target_pairs={{0,752},{8,760},{16,0},{24,8},{32,16},{40,24},{48,32},{56,40},{64,... | collective-permute-start | bytes 258056 | tf_op jit(solution)/shard_map/ppermute | solution.py:36
  135.6 7.3 %collective-permute-start.9 = (bf16[336,128]{1,0:T(8,128)(2,1)S(1)}, bf16[336,128]{1,0:T(8,128)(2,1)S(1)}, u32[]{:S(2)}, u32[]{:S(2)}) collective-permute-start(bf16[336,128]{1,0:T(8,128)(2,1)S(1)} %get-tuple-element.37), channel_id=1, source_target_pairs={{0,744},{8,752},{16,760},{24,0},{32,8},{40,16},{48,24},{56,32},{64... | collective-permute-start | bytes 258056 | tf_op jit(solution)/shard_map/ppermute | solution.py:36

commit v9 on v8

--- a/solution.py
+++ b/solution.py
@@ -140,8 +140,8 @@
         out_refs[o][7 * CAP : OUT_ROWS, :] = levels.astype(bf16)
 
 
-def join_kernel(*refs):
-    out_ref = refs[GROUP]
+def join_kernel(*all_refs):
+    refs, out_ref = all_refs[0:GROUP][::-1], all_refs[GROUP]
     levels = jnp.zeros((16, LANE), bf16)
     for o in range(GROUP):
         out_ref[o * 7 * CAP : (o + 1) * 7 * CAP, :] = refs[o][0 : 7 * CAP, :]
@@ -294,7 +294,7 @@
 
 
 def unpack_kernel(route_ref, fixed_ref, *refs):
-    got_refs = refs[0:GROUP]
+    got_refs = refs[0:GROUP][::-1]
     out_ref, gate_ref = refs[GROUP], refs[GROUP + 1]
     route = route_ref[...]
     weights = fixed_ref[...].astype(f32) / 65536.0
@@ -362,9 +362,10 @@
             pltpu.SemaphoreType.DMA((3,)),
         ],
     )
-    got = [packed[0]] + [from_behind(packed[o], "node", o) for o in range(1, GROUP)]
-    got, down_cols = lax.optimization_barrier((got, down_weight[0].T))
-    shard = call(join_kernel, jax.ShapeDtypeStruct((SHARD_ROWS, LANE), bf16), *got).astype(jnp.float16)
+    got = [packed[0]] + [from_behind(packed[o], "node", o) for o in range(GROUP - 1, 0, -1)][::-1]
+    *got, down_cols = lax.optimization_barrier((*got[::-1], down_weight[0].T))
+    got = got[::-1]
+    shard = call(join_kernel, jax.ShapeDtypeStruct((SHARD_ROWS, LANE), bf16), *got[::-1]).astype(jnp.float16)
     full = lax.all_gather(shard, "local", axis=0, tiled=True).astype(bf16)
     hidden = call(
         hidden_kernel,
@@ -398,13 +399,13 @@
         own_share,
         swap(far_share, across, 1),
     )
-    home = [summed[0]] + [from_behind(summed[o], "node", -o) for o in range(1, GROUP)]
+    home = [summed[0]] + [from_behind(summed[o], "node", -o) for o in range(GROUP - 1, 0, -1)][::-1]
     input_grad, gate_grad = call(
         unpack_kernel,
         [jax.ShapeDtypeStruct((FEAT, TOK), bf16), jax.ShapeDtypeStruct((2, TOK), f32)],
         route,
         gate_fixed.T,
-        *home,
+        *home[::-1],
     )
     return input_grad.T, gate_grad.T
 

time: 144 us -> 144 us (level)
  starting transfers between devices: 44 us -> 47.6 us
  waiting for transfers between devices: 37.5 us -> 35.1 us
  blocking collectives: 49.3 us -> 47.8 us
    ppermute x6, starting transfers between devices: 29.4 us -> 33.2 us  [from_behind(): return lax.ppermute(value, axis, pairs)]
    ppermute x6, waiting for transfers between devices: 11.4 us -> 8.5 us  [from_behind(): return lax.ppermute(value, axis, pairs)]
    all_gather x1, blocking collectives: 49.3 us -> 47.8 us  [body(): full = lax.all_gather(shard, 'local', axis=0, tiled=True).astype(bf16)]
  transfers between devices with their start and end apart: 10 -> 10, of which waited for: 6 -> 7; matrix products, arithmetic and copies ran while one was open for 2% -> 2% of each run, Pallas kernels for 3% -> 3%
where the time goes in v9:
time: 144 us
  blocking collectives  47.8 us (33%)
  starting transfers between devices  47.6 us (33%)
  waiting for transfers between devices  35.1 us (24%)
  Pallas kernels  9.06 us (6%)
  local copies, waits for them, and re-layouts  2.53 us (2%)
    all_gather x1, blocking collectives, body(): full = lax.all_gather(shard, 'local', axis=0, tiled=True).astype(bf16)  47.8 us
    ppermute x6, starting transfers between devices, from_behind(): return lax.ppermute(value, axis, pairs)  33.2 us
    ppermute x4, waiting for transfers between devices, swap(): return lax.ppermute(value, ('node', 'local'), pairs)  26.7 us
    ppermute x4, starting transfers between devices, swap(): return lax.ppermute(value, ('node', 'local'), pairs)  14.4 us
    pallas_call x8, Pallas kernels, call(): pl.pallas_call(kernel, out_shape=outs, in_specs=[pl.BlockSpec(memory_spac...  9.06 us
    ppermute x6, waiting for transfers between devices, from_behind(): return lax.ppermute(value, axis, pairs)  8.5 us
  transfers between devices with their start and end apart: 10, of which 7 were waited for; matrix products, arithmetic and copies ran while one was open for 2% of the time, Pallas kernels for 3%

profile of v9, /device:TPU:1, one launch (start us, length us, event | category | flops | bytes accessed | tf_op | source)
XLA Modules:
  0.0 143.6 jit_solution(4509215709313360391)
XLA Ops:
  0.6 2.2 %shard_map.86 = (bf16[576,128]{1,0:T(8,128)(2,1)S(1)}, bf16[576,128]{1,0:T(8,128)(2,1)S(1)}, bf16[576,128]{1,0:T(8,128)(2,1)}, bf16[576,128]{1,0:T(8,128)(2,1)}) custom-call(s32[2,128]{1,0:T(2,128)} %bitcast.20, bf16[448,128]{1,0:T(8,128)(2,1)} %bitcast.23, bf16[448,128]{1,0:T(8,128)(2,1)} %bitcast.24), custom_call_target="tpu_custom_call" | custom-call | tf_op jit(solution)/shard_map/pallas_call | solution.py:326
  2.8 6.0 %collective-permute-start = (bf16[576,128]{1,0:T(8,128)(2,1)}, bf16[576,128]{1,0:T(8,128)(2,1)S(1)}, u32[]{:S(2)}, u32[]{:S(2)}) collective-permute-start(bf16[576,128]{1,0:T(8,128)(2,1)} %get-tuple-element.21), channel_id=1, source_target_pairs={{0,24},{8,32},{16,40},{24,48},{32,56},{40,64},{48,72},{56,80},{64,... | collective-permute-start | bytes 442376 | tf_op jit(solution)/shard_map/ppermute | solution.py:36
  8.8 2.2 %collective-permute-start.1 = (bf16[576,128]{1,0:T(8,128)(2,1)}, bf16[576,128]{1,0:T(8,128)(2,1)S(1)}, u32[]{:S(2)}, u32[]{:S(2)}) collective-permute-start(bf16[576,128]{1,0:T(8,128)(2,1)} %get-tuple-element.22), channel_id=1, source_target_pairs={{0,16},{8,24},{16,32},{24,40},{32,48},{40,56},{48,64},{56,72},{64,... | collective-permute-start | bytes 442376 | tf_op jit(solution)/shard_map/ppermute | solution.py:36
  11.1 2.2 %collective-permute-start.2 = (bf16[576,128]{1,0:T(8,128)(2,1)S(1)}, bf16[576,128]{1,0:T(8,128)(2,1)S(1)}, u32[]{:S(2)}, u32[]{:S(2)}) collective-permute-start(bf16[576,128]{1,0:T(8,128)(2,1)S(1)} %get-tuple-element.23), channel_id=1, source_target_pairs={{0,8},{8,16},{16,24},{24,32},{32,40},{40,48},{48,56},{56,64},{64,7... | collective-permute-start | bytes 442376 | tf_op jit(solution)/shard_map/ppermute | solution.py:36
  13.3 0.1 pad_add_fusion.where_ref
  13.3 1.9 %shard_map.89 = bf16[3584,128]{1,0:T(8,128)(2,1)S(1)} custom-call(s32[2]{0:T(128)S(1)} %pad_add_fusion.where_ref, bf16[3584,128]{1,0:T(8,128)(2,1)} %bitcast.13, bf16[3584,128]{1,0:T(8,128)(2,1)} %bitcast.16), custom_call_target="tpu_custom_call" | custom-call | tf_op jit(solution)/shard_map/pallas_call | solution.py:326
  15.2 5.1 %collective-permute-start.4 = (bf16[3584,128]{1,0:T(8,128)(2,1)S(1)}, bf16[3584,128]{1,0:T(8,128)(2,1)S(1)}, u32[]{:S(2)}, u32[]{:S(2)}) collective-permute-start(bf16[3584,128]{1,0:T(8,128)(2,1)S(1)} %shard_map.89), channel_id=1, source_target_pairs={{0,1},{1,0},{2,3},{3,2},{4,5},{5,4},{6,7},{7,6},{8,15},{9,10},{10,... | collective-permute-start | bytes 2752520 | tf_op jit(solution)/shard_map/ppermute | solution.py:54
  20.3 1.6 %copy.9 = bf16[1,128,3584]{1,2,0:T(8,128)(2,1)S(1)} copy(bf16[1,128,3584]{2,1,0:T(8,128)(2,1)} %param.11) | data formatting | bytes 1835008 | tf_op args[4]
  21.9 3.6 %collective-permute-done.all_refs_0_ = bf16[576,128]{1,0:T(8,128)(2,1)S(1)} collective-permute-done((bf16[576,128]{1,0:T(8,128)(2,1)}, bf16[576,128]{1,0:T(8,128)(2,1)S(1)}, u32[]{:S(2)}, u32[]{:S(2)}) %collective-permute-start) | collective-permute-done | bytes 147488 | tf_op jit(solution)/shard_map/ppermute | solution.py:36
  25.5 1.7 %collective-permute-done.1.all_refs_1_ = bf16[576,128]{1,0:T(8,128)(2,1)S(1)} collective-permute-done((bf16[576,128]{1,0:T(8,128)(2,1)}, bf16[576,128]{1,0:T(8,128)(2,1)S(1)}, u32[]{:S(2)}, u32[]{:S(2)}) %collective-permute-start.1) | collective-permute-done | bytes 147488 | tf_op jit(solution)/shard_map/ppermute | solution.py:36
  27.2 0.0 collective-permute-done.2.all_refs_2_
  27.3 0.1 convert_element_type.6
  27.4 47.8 %all-gather.1 = f16[18048,128]{1,0:T(8,128)(2,1)S(1)} all-gather(f16[2256,128]{1,0:T(8,128)(2,1)S(1)} %convert_element_type.6), channel_id=1, replica_groups=mesh['node'=96,'local'=8] {'local'}, dimensions={0}, use_global_device_ids=true | all-gather | bytes 5197824 | tf_op jit(solution)/shard_map/all_gather | solution.py:369
  75.2 0.0 copy-start
  75.2 0.0 copy-start.1
  75.2 0.5 convert_element_type.7.got_ref
  75.7 0.6 copy-done
  76.4 0.3 copy-done.1
  76.7 1.9 %shard_map.88.own_ref = bf16[656,128]{1,0:T(8,128)(2,1)S(1)} custom-call(bf16[18048,128]{1,0:T(8,128)(2,1)S(1)} %convert_element_type.7.got_ref, bf16[3584,128]{1,0:T(8,128)(2,1)S(1)} %bitcast.14, bf16[3584,128]{1,0:T(8,128)(2,1)S(1)} %bitcast.17, bf16[3584,128]{1,0:T(8,128)(2,1)S(1)} %bitcast.19), custom_call_target="tpu_custom_call" | custom-call | tf_op jit(solution)/shard_map/pallas_call | solution.py:326
  78.6 0.0 copy-start.2
  78.6 0.0 copy-start.3
  78.6 2.1 %collective-permute-start.3 = (bf16[656,128]{1,0:T(8,128)(2,1)S(1)}, bf16[656,128]{1,0:T(8,128)(2,1)S(1)}, u32[]{:S(2)}, u32[]{:S(2)}) collective-permute-start(bf16[656,128]{1,0:T(8,128)(2,1)S(1)} %shard_map.88.own_ref), channel_id=1, source_target_pairs={{0,1},{1,0},{2,3},{3,2},{4,5},{5,4},{6,7},{7,6},{8,15},{9,10},{10,... | collective-permute-start | bytes 503816 | tf_op jit(solution)/shard_map/ppermute | solution.py:54
  80.7 5.4 %collective-permute-done.3.other_ref = bf16[656,128]{1,0:T(8,128)(2,1)S(1)} collective-permute-done((bf16[656,128]{1,0:T(8,128)(2,1)S(1)}, bf16[656,128]{1,0:T(8,128)(2,1)S(1)}, u32[]{:S(2)}, u32[]{:S(2)}) %collective-permute-start.3) | collective-permute-done | bytes 167968 | tf_op jit(solution)/shard_map/ppermute | solution.py:54
  86.0 0.0 collective-permute-done.4.other_ref_rows
  86.0 1.7 %shard_map.90 = (f32[2272,128]{1,0:T(8,128)S(1)}, bf16[2272,128]{1,0:T(8,128)(2,1)S(1)}) custom-call(s32[2]{0:T(128)S(1)} %pad_add_fusion.where_ref, bf16[656,128]{1,0:T(8,128)(2,1)S(1)} %shard_map.88.own_ref, bf16[656,128]{1,0:T(8,128)(2,1)S(1)} %collective-permute-done.3.other_ref, bf16[3584,128]{1,0:T(8,128)(2,1)S(1)} %bitcast.15, ...), custom_call_target="tpu_custom_call" | custom-call | tf_op jit(solution)/shard_map/pallas_call | solution.py:326
  87.8 1.9 %collective-permute-start.5 = (bf16[2272,128]{1,0:T(8,128)(2,1)S(1)}, bf16[2272,128]{1,0:T(8,128)(2,1)S(1)}, u32[]{:S(2)}, u32[]{:S(2)}) collective-permute-start(bf16[2272,128]{1,0:T(8,128)(2,1)S(1)} %get-tuple-element.31), channel_id=1, source_target_pairs={{0,2},{1,3},{2,0},{3,1},{4,6},{5,7},{6,4},{7,5},{8,14},{9,15},{10,... | collective-permute-start | bytes 1744904 | tf_op jit(solution)/shard_map/ppermute | solution.py:54
  89.7 13.0 %collective-permute-done.5.got_ref = bf16[2272,128]{1,0:T(8,128)(2,1)S(1)} collective-permute-done((bf16[2272,128]{1,0:T(8,128)(2,1)S(1)}, bf16[2272,128]{1,0:T(8,128)(2,1)S(1)}, u32[]{:S(2)}, u32[]{:S(2)}) %collective-permute-start.5) | collective-permute-done | bytes 581664 | tf_op jit(solution)/shard_map/ppermute | solution.py:54
  102.7 0.2 shard_map.91
  102.8 5.4 %collective-permute-start.6 = (bf16[1136,128]{1,0:T(8,128)(2,1)S(1)}, bf16[1136,128]{1,0:T(8,128)(2,1)S(1)}, u32[]{:S(2)}, u32[]{:S(2)}) collective-permute-start(bf16[1136,128]{1,0:T(8,128)(2,1)S(1)} %get-tuple-element.33), channel_id=1, source_target_pairs={{0,6},{1,7},{2,4},{3,5},{4,2},{5,3},{6,0},{7,1},{8,10},{9,11},{10,... | collective-permute-start | bytes 872456 | tf_op jit(solution)/shard_map/ppermute | solution.py:54
  108.2 8.3 %collective-permute-done.6.got_ref = bf16[1136,128]{1,0:T(8,128)(2,1)S(1)} collective-permute-done((bf16[1136,128]{1,0:T(8,128)(2,1)S(1)}, bf16[1136,128]{1,0:T(8,128)(2,1)S(1)}, u32[]{:S(2)}, u32[]{:S(2)}) %collective-permute-start.6) | collective-permute-done | bytes 290848 | tf_op jit(solution)/shard_map/ppermute | solution.py:54
  116.5 0.1 shard_map.92
  116.6 16.9 %collective-permute-start.7 = (bf16[336,128]{1,0:T(8,128)(2,1)S(1)}, bf16[336,128]{1,0:T(8,128)(2,1)S(1)}, u32[]{:S(2)}, u32[]{:S(2)}) collective-permute-start(bf16[336,128]{1,0:T(8,128)(2,1)S(1)} %get-tuple-element.34), channel_id=1, source_target_pairs={{0,744},{8,752},{16,760},{24,0},{32,8},{40,16},{48,24},{56,32},{64... | collective-permute-start | bytes 258056 | tf_op jit(solution)/shard_map/ppermute | solution.py:36
  133.5 3.2 %collective-permute-start.8 = (bf16[336,128]{1,0:T(8,128)(2,1)S(1)}, bf16[336,128]{1,0:T(8,128)(2,1)S(1)}, u32[]{:S(2)}, u32[]{:S(2)}) collective-permute-start(bf16[336,128]{1,0:T(8,128)(2,1)S(1)} %get-tuple-element.35), channel_id=1, source_target_pairs={{0,752},{8,760},{16,0},{24,8},{32,16},{40,24},{48,32},{56,40},{64,... | collective-permute-start | bytes 258056 | tf_op jit(solution)/shard_map/ppermute | solution.py:36
  136.7 2.6 %collective-permute-start.9 = (bf16[336,128]{1,0:T(8,128)(2,1)S(1)}, bf16[336,128]{1,0:T(8,128)(2,1)S(1)}, u32[]{:S(2)}, u32[]{:S(2)}) collective-permute-start(bf16[336,128]{1,0:T(8,128)(2,1)S(1)} %get-tuple-element.36), channel_id=1, source_target_pairs={{0,760},{8,0},{16,8},{24,16},{32,24},{40,32},{48,40},{56,48},{64,5... | collective-permute-start | bytes 258056 | tf_op jit(solution)/shard_map/ppermute | solution.py:36
  139.3 0.0 collective-permute-done.7.refs_0_
  139.3 0.5 collective-permute-done.8.refs_1_
  139.9 2.7 %collective-permute-done.9.refs_2_ = bf16[336,128]{1,0:T(8,128)(2,1)S(1)} collective-permute-done((bf16[336,128]{1,0:T(8,128)(2,1)S(1)}, bf16[336,128]{1,0:T(8,128)(2,1)S(1)}, u32[]{:S(2)}, u32[]{:S(2)}) %collective-permute-start.9) | collective-permute-done | bytes 86048 | tf_op jit(solution)/shard_map/ppermute | solution.py:36
  142.5 0.0 copy-done.2
  142.5 0.0 copy-done.3
  142.5 1.1 shard_map.93
  (1 shorter events, 0.0 us)
Async XLA Ops:
  2.8 22.7 %collective-permute-start = (bf16[576,128]{1,0:T(8,128)(2,1)}, bf16[576,128]{1,0:T(8,128)(2,1)S(1)}, u32[]{:S(2)}, u32[]{:S(2)}) collective-permute-start(bf16[576,128]{1,0:T(8,128)(2,1)} %get-tuple-element.21), channel_id=1, source_target_pairs={{0,24},{8,32},{16,40},{24,48},{32,56},{40,64},{48,72},{56,80},{64,... | collective-permute-start | bytes 442376 | tf_op jit(solution)/shard_map/ppermute | solution.py:36
  8.8 18.4 %collective-permute-start.1 = (bf16[576,128]{1,0:T(8,128)(2,1)}, bf16[576,128]{1,0:T(8,128)(2,1)S(1)}, u32[]{:S(2)}, u32[]{:S(2)}) collective-permute-start(bf16[576,128]{1,0:T(8,128)(2,1)} %get-tuple-element.22), channel_id=1, source_target_pairs={{0,16},{8,24},{16,32},{24,40},{32,48},{40,56},{48,64},{56,72},{64,... | collective-permute-start | bytes 442376 | tf_op jit(solution)/shard_map/ppermute | solution.py:36
  11.1 16.2 %collective-permute-start.2 = (bf16[576,128]{1,0:T(8,128)(2,1)S(1)}, bf16[576,128]{1,0:T(8,128)(2,1)S(1)}, u32[]{:S(2)}, u32[]{:S(2)}) collective-permute-start(bf16[576,128]{1,0:T(8,128)(2,1)S(1)} %get-tuple-element.23), channel_id=1, source_target_pairs={{0,8},{8,16},{16,24},{24,32},{32,40},{40,48},{48,56},{56,64},{64,7... | collective-permute-start | bytes 442376 | tf_op jit(solution)/shard_map/ppermute | solution.py:36
  15.2 70.8 %collective-permute-start.4 = (bf16[3584,128]{1,0:T(8,128)(2,1)S(1)}, bf16[3584,128]{1,0:T(8,128)(2,1)S(1)}, u32[]{:S(2)}, u32[]{:S(2)}) collective-permute-start(bf16[3584,128]{1,0:T(8,128)(2,1)S(1)} %shard_map.89), channel_id=1, source_target_pairs={{0,1},{1,0},{2,3},{3,2},{4,5},{5,4},{6,7},{7,6},{8,15},{9,10},{10,... | collective-permute-start | bytes 2752520 | tf_op jit(solution)/shard_map/ppermute | solution.py:54
  75.2 1.2 copy-start
  75.2 1.5 %copy-start.1 = (bf16[1,3584,128]{2,1,0:T(8,128)(2,1)S(1)}, bf16[1,3584,128]{2,1,0:T(8,128)(2,1)}, u32[]{:S(2)}) copy-start(bf16[1,3584,128]{2,1,0:T(8,128)(2,1)} %param.10) | copy-start | bytes 2752516
  78.6 64.0 %copy-start.2 = (s32[128,2]{0,1:T(2,128)S(1)}, s32[128,2]{0,1:T(2,128)}, u32[]{:S(2)}) copy-start(s32[128,2]{0,1:T(2,128)} %param.12) | copy-start | bytes 3076
  78.6 64.0 %copy-start.3 = (s32[128,2]{0,1:T(2,128)S(1)}, s32[128,2]{0,1:T(2,128)}, u32[]{:S(2)}) copy-start(s32[128,2]{0,1:T(2,128)} %param.13) | copy-start | bytes 3076
  78.6 7.5 %collective-permute-start.3 = (bf16[656,128]{1,0:T(8,128)(2,1)S(1)}, bf16[656,128]{1,0:T(8,128)(2,1)S(1)}, u32[]{:S(2)}, u32[]{:S(2)}) collective-permute-start(bf16[656,128]{1,0:T(8,128)(2,1)S(1)} %shard_map.88.own_ref), channel_id=1, source_target_pairs={{0,1},{1,0},{2,3},{3,2},{4,5},{5,4},{6,7},{7,6},{8,15},{9,10},{10,... | collective-permute-start | bytes 503816 | tf_op jit(solution)/shard_map/ppermute | solution.py:54
  87.8 14.9 %collective-permute-start.5 = (bf16[2272,128]{1,0:T(8,128)(2,1)S(1)}, bf16[2272,128]{1,0:T(8,128)(2,1)S(1)}, u32[]{:S(2)}, u32[]{:S(2)}) collective-permute-start(bf16[2272,128]{1,0:T(8,128)(2,1)S(1)} %get-tuple-element.31), channel_id=1, source_target_pairs={{0,2},{1,3},{2,0},{3,1},{4,6},{5,7},{6,4},{7,5},{8,14},{9,15},{10,... | collective-permute-start | bytes 1744904 | tf_op jit(solution)/shard_map/ppermute | solution.py:54
  102.8 13.7 %collective-permute-start.6 = (bf16[1136,128]{1,0:T(8,128)(2,1)S(1)}, bf16[1136,128]{1,0:T(8,128)(2,1)S(1)}, u32[]{:S(2)}, u32[]{:S(2)}) collective-permute-start(bf16[1136,128]{1,0:T(8,128)(2,1)S(1)} %get-tuple-element.33), channel_id=1, source_target_pairs={{0,6},{1,7},{2,4},{3,5},{4,2},{5,3},{6,0},{7,1},{8,10},{9,11},{10,... | collective-permute-start | bytes 872456 | tf_op jit(solution)/shard_map/ppermute | solution.py:54
  116.6 22.7 %collective-permute-start.7 = (bf16[336,128]{1,0:T(8,128)(2,1)S(1)}, bf16[336,128]{1,0:T(8,128)(2,1)S(1)}, u32[]{:S(2)}, u32[]{:S(2)}) collective-permute-start(bf16[336,128]{1,0:T(8,128)(2,1)S(1)} %get-tuple-element.34), channel_id=1, source_target_pairs={{0,744},{8,752},{16,760},{24,0},{32,8},{40,16},{48,24},{56,32},{64... | collective-permute-start | bytes 258056 | tf_op jit(solution)/shard_map/ppermute | solution.py:36
  133.5 6.3 %collective-permute-start.8 = (bf16[336,128]{1,0:T(8,128)(2,1)S(1)}, bf16[336,128]{1,0:T(8,128)(2,1)S(1)}, u32[]{:S(2)}, u32[]{:S(2)}) collective-permute-start(bf16[336,128]{1,0:T(8,128)(2,1)S(1)} %get-tuple-element.35), channel_id=1, source_target_pairs={{0,752},{8,760},{16,0},{24,8},{32,16},{40,24},{48,32},{56,40},{64,... | collective-permute-start | bytes 258056 | tf_op jit(solution)/shard_map/ppermute | solution.py:36
  136.7 5.8 %collective-permute-start.9 = (bf16[336,128]{1,0:T(8,128)(2,1)S(1)}, bf16[336,128]{1,0:T(8,128)(2,1)S(1)}, u32[]{:S(2)}, u32[]{:S(2)}) collective-permute-start(bf16[336,128]{1,0:T(8,128)(2,1)S(1)} %get-tuple-element.36), channel_id=1, source_target_pairs={{0,760},{8,0},{16,8},{24,16},{32,24},{40,32},{48,40},{56,48},{64,5... | collective-permute-start | bytes 258056 | tf_op jit(solution)/shard_map/ppermute | solution.py:36
